TPU v7x, 32 devices: a whole 2x2x4 slice. The times are simulated.
32 devices in a mesh: dp: 8 (over z, x), tensor: 4 (over y, core).
Axes of the slice: x: 2, y: 2, z: 4, core: 2. Of those that a mesh axis runs over, the one named last changes fastest.
Arguments:
- hidden_in: bfloat16 [4096, 3072], P(('dp', 'tensor')), may hold values from -6 to 6
- cotangent: float32 [4096, 3072], P(('dp', 'tensor')), may hold values from -6 to 6
- lengths: int32 [8], P('dp'), may hold values from 256 to 512, as said below
- gain_attn: bfloat16 [3072], P('dp'), may hold values from 0.5 to 1.5
- w_qkv: bfloat16 [3, 3072, 3072], P(None, 'dp', 'tensor'), may hold values from -0.109375 to 0.109375
- w_out: bfloat16 [3072, 3072], P('tensor', 'dp'), may hold values from -1 to 1
- gain_mlp: bfloat16 [3072], P('dp'), may hold values from 0.5 to 1.5
- w_gate_up: bfloat16 [3072, 2, 8192], P('dp', None, 'tensor'), may hold values from -0.109375 to 0.109375
- w_down: bfloat16 [8192, 3072], P('tensor', 'dp'), may hold values from -0.0625 to 0.0625
Outputs:
- layer_out: float32 [4096, 3072], P(('dp', 'tensor'))
- grad_in: float32 [4096, 3072], P(('dp', 'tensor'))
- grad_gain_attn: float32 [3072], P('dp')
- grad_qkv: float32 [3, 3072, 3072], P(None, 'dp', 'tensor')
- grad_out: float32 [3072, 3072], P('tensor', 'dp')
- grad_gain_mlp: float32 [3072], P('dp')
- grad_gate_up: float32 [3072, 2, 8192], P('dp', None, 'tensor')
- grad_down: float32 [8192, 3072], P('tensor', 'dp')
Inputs may be any that keep to these rules, and one draw needn't show every extreme that they name: Group g holds one sequence in its first lengths[g] rows; its other rows are padding. Some group is full and some group holds exactly 256 live rows.
All inputs are finite; a program needn't handle non-finite values.
Results may differ from a plain program's by a relative error of at most 0.019.
Values may be sent and summed in bfloat16 or wider, within the bound.
No kernel may reach another device: no remote copies, remote signals or barrier semaphores. Data moves between devices by JAX's collectives and lax.ppermute only.
A program may use at most 256 MiB of HBM per device.

v0:
```python
import math

import jax
import jax.numpy as jnp
from jax import lax
from jax.sharding import PartitionSpec as P

HEAD_DIM = 96


NORM_EPS = 1e-05
ROPE_BASE = 10000.0


def rope_tables(row_count, head_width):
    positions = jnp.arange(row_count).astype(jnp.float32)
    exponent = jnp.arange(head_width // 2).astype(jnp.float32) * (2.0 / head_width)
    frequency = ROPE_BASE ** (-exponent)
    angles = positions[:, None] * frequency[None, :]
    cosine = jnp.concatenate([jnp.cos(angles), jnp.cos(angles)], axis=1)[:, None, :]
    sine_table = jnp.concatenate([jnp.sin(angles), jnp.sin(angles)], axis=1)[:, None, :]
    return (cosine, sine_table)


def rotate(values):
    half_width = values.shape[-1] // 2
    return jnp.concatenate([-values[..., half_width:], values[..., :half_width]], axis=-1)


def rotate_back(values):
    half_width = values.shape[-1] // 2
    return jnp.concatenate([values[..., half_width:], -values[..., :half_width]], axis=-1)


def rms_unit(values):
    scale_inv = lax.rsqrt(jnp.mean(values * values, axis=1, keepdims=True) + NORM_EPS)
    return (values * scale_inv, scale_inv)


def norm_back(grad_normed, gain, unit, scale_inv):
    grad_unit = grad_normed * gain
    return scale_inv * (grad_unit - unit * jnp.mean(grad_unit * unit, axis=1, keepdims=True))


def mix(form, left, right):
    return jnp.einsum(form, left, right, preferred_element_type=jnp.float32)


def score_block(queries, keys_all, offset, length, block_rows):
    row_count = keys_all.shape[0]
    key_ids = jnp.arange(row_count, dtype=jnp.int32)
    row_ids = offset + jnp.arange(block_rows, dtype=jnp.int32)
    allowed = (key_ids[None, :] <= row_ids[:, None]) & (
        (row_ids[:, None] < length) == (key_ids[None, :] < length)
    )
    scores = mix("qhd,khd->hqk", queries, keys_all) * (1.0 / math.sqrt(queries.shape[2]))
    return (jnp.where(allowed[None], scores, -jnp.inf), queries)


def block_offsets(row_count, block_rows):
    return jnp.arange(row_count // block_rows) * block_rows


def attend(queries, keys_all, values, length, block_rows):
    row_count, head_count, head_width = queries.shape

    def one_block(offset):
        scores, query_block = score_block(queries, keys_all, offset, length, block_rows)
        row_max = jnp.max(scores, axis=2, keepdims=True)
        log_total = row_max + jnp.log(jnp.sum(jnp.exp(scores - row_max), axis=2, keepdims=True))
        attn_prob = jnp.exp(scores - log_total).astype(jnp.bfloat16)
        mixed = mix("hqk,khd->qhd", attn_prob, values).astype(jnp.bfloat16)
        return (mixed, log_total[..., 0])

    mixed, log_total = lax.map(one_block, block_offsets(row_count, block_rows))
    mixed = mixed.reshape(row_count, head_count, head_width)
    log_total = jnp.transpose(log_total, (1, 0, 2)).reshape(head_count, row_count)
    return (mixed, log_total)


def attend_back(queries, keys_all, values, mixed, log_total, grad_mixed, length, block_rows):
    row_count, head_count, head_width = queries.shape
    delta_all = jnp.sum(grad_mixed.astype(jnp.float32) * mixed.astype(jnp.float32), axis=2)

    def one_block(totals, offset):
        grad_keys, grad_values = totals
        scores, query_block = score_block(queries, keys_all, offset, length, block_rows)
        prob_full = jnp.exp(scores - log_total[..., None])
        prob_half = prob_full.astype(jnp.bfloat16)
        grad_prob = mix("qhd,khd->hqk", grad_mixed, values)
        grad_score = (
            prob_full
            * (grad_prob - jnp.transpose(delta_all)[..., None])
            * (1.0 / math.sqrt(head_width))
        ).astype(jnp.bfloat16)
        grad_query = mix("hqk,khd->qhd", grad_score, keys_all)
        grad_keys = grad_keys + mix("hqk,qhd->khd", grad_score, query_block)
        grad_values = grad_values + mix("hqk,qhd->khd", prob_half, grad_mixed)
        return ((grad_keys, grad_values), grad_query)

    zeros = jnp.zeros((row_count, head_count, head_width), jnp.float32)
    (grad_keys, grad_values), grad_query = lax.scan(
        one_block, (zeros, zeros), block_offsets(row_count, block_rows)
    )
    return (grad_query.reshape(row_count, head_count, head_width), grad_keys, grad_values)


def fetch_attention(gain_attn, w_qkv, w_out):
    return (
        lax.all_gather(gain_attn, "dp", axis=0, tiled=True),
        lax.all_gather(w_qkv, "dp", axis=1, tiled=True),
        lax.all_gather(w_out, "dp", axis=1, tiled=True),
    )


def fetch_mlp(gain_mlp, w_gate_up, w_down):
    return (
        lax.all_gather(gain_mlp, "dp", axis=0, tiled=True),
        lax.all_gather(w_gate_up, "dp", axis=0, tiled=True),
        lax.all_gather(w_down, "dp", axis=1, tiled=True),
    )


def on_device(hidden_in, cotangent, lengths, gain_attn, w_qkv, w_out, gain_mlp, w_gate_up, w_down):
    length = lengths[0]
    local_rows = hidden_in.shape[0]
    row_count = local_rows * lax.axis_size("tensor")
    block_rows = min(512, row_count)
    head_count = w_qkv.shape[2] // HEAD_DIM
    shape_heads = (row_count, head_count, HEAD_DIM)
    own_rows = lax.axis_index("tensor") * local_rows + jnp.arange(local_rows, dtype=jnp.int32)
    live = (own_rows < length).astype(jnp.float32)[:, None]
    cosine, sine_table = rope_tables(row_count, HEAD_DIM)
    full_gain_attn, full_qkv, full_out = fetch_attention(gain_attn, w_qkv, w_out)
    input_f = hidden_in.astype(jnp.float32)
    unit_first, scale_first = rms_unit(input_f)
    normed_first = lax.all_gather(
        (unit_first * full_gain_attn.astype(jnp.float32)).astype(jnp.bfloat16),
        "tensor",
        axis=0,
        tiled=True,
    )
    projected = mix("td,jde->jte", normed_first, full_qkv)
    query_raw = projected[0].reshape(shape_heads)
    key_raw = projected[1].reshape(shape_heads)
    queries = (query_raw * cosine + rotate(query_raw) * sine_table).astype(jnp.bfloat16)
    keys_rot = (key_raw * cosine + rotate(key_raw) * sine_table).astype(jnp.bfloat16)
    values = projected[2].reshape(shape_heads).astype(jnp.bfloat16)
    mixed, log_total = attend(queries, keys_rot, values, length, block_rows)
    attn_flat = mixed.reshape(row_count, -1)
    middle = input_f + lax.psum_scatter(
        jnp.dot(attn_flat, full_out, preferred_element_type=jnp.float32),
        "tensor",
        scatter_dimension=0,
        tiled=True,
    )
    full_gain_mlp, full_gate_up, full_down = fetch_mlp(gain_mlp, w_gate_up, w_down)
    unit_second, scale_second = rms_unit(middle)
    normed_second = lax.all_gather(
        (unit_second * full_gain_mlp.astype(jnp.float32)).astype(jnp.bfloat16),
        "tensor",
        axis=0,
        tiled=True,
    )
    gate_up = mix("td,djf->jtf", normed_second, full_gate_up)
    gate_part = gate_up[0]
    up_part = gate_up[1]
    sigmoid_gate = jax.nn.sigmoid(gate_part)
    activated = (gate_part * sigmoid_gate * up_part).astype(jnp.bfloat16)
    layer_out = (
        middle
        + lax.psum_scatter(
            jnp.dot(activated, full_down, preferred_element_type=jnp.float32).astype(jnp.bfloat16),
            "tensor",
            scatter_dimension=0,
            tiled=True,
        ).astype(jnp.float32)
    ) * live
    full_gain_mlp, full_gate_up, full_down = fetch_mlp(gain_mlp, w_gate_up, w_down)
    grad_rows = cotangent * live
    grad_half = lax.all_gather(grad_rows.astype(jnp.bfloat16), "tensor", axis=0, tiled=True)
    grad_down = jnp.dot(activated.T, grad_half, preferred_element_type=jnp.float32)
    grad_act = jnp.dot(grad_half, full_down.T, preferred_element_type=jnp.float32)
    grad_gu = jnp.stack(
        [
            grad_act * up_part * sigmoid_gate * (1.0 + gate_part * (1.0 - sigmoid_gate)),
            grad_act * gate_part * sigmoid_gate,
        ]
    ).astype(jnp.bfloat16)
    grad_gate_up = mix("td,jtf->djf", normed_second, grad_gu)
    grad_second = lax.psum_scatter(
        mix("jtf,djf->td", grad_gu, full_gate_up), "tensor", scatter_dimension=0, tiled=True
    )
    part_gain_mlp = jnp.sum(grad_second * unit_second, axis=0)
    grad_middle = grad_rows + norm_back(
        grad_second, full_gain_mlp.astype(jnp.float32), unit_second, scale_second
    )
    sum_gain_mlp, sum_gate_up, sum_down = (
        lax.psum_scatter(
            part_gain_mlp.astype(jnp.bfloat16), "dp", scatter_dimension=0, tiled=True
        ).astype(jnp.float32),
        lax.psum_scatter(
            grad_gate_up.astype(jnp.bfloat16), "dp", scatter_dimension=0, tiled=True
        ).astype(jnp.float32),
        lax.psum_scatter(
            grad_down.astype(jnp.bfloat16), "dp", scatter_dimension=1, tiled=True
        ).astype(jnp.float32),
    )
    full_gain_attn, full_qkv, full_out = fetch_attention(gain_attn, w_qkv, w_out)
    middle_half = lax.all_gather(grad_middle.astype(jnp.bfloat16), "tensor", axis=0, tiled=True)
    grad_out = jnp.dot(attn_flat.T, middle_half, preferred_element_type=jnp.float32)
    grad_mixed = (
        jnp.dot(middle_half, full_out.T, preferred_element_type=jnp.float32)
        .astype(jnp.bfloat16)
        .reshape(shape_heads)
    )
    grad_query, grad_keys, grad_values = attend_back(
        queries, keys_rot, values, mixed, log_total, grad_mixed, length, block_rows
    )
    query_back = grad_query * cosine + rotate_back(grad_query * sine_table)
    key_back = grad_keys * cosine + rotate_back(grad_keys * sine_table)
    grad_proj = (
        jnp.stack([query_back, key_back, grad_values])
        .astype(jnp.bfloat16)
        .reshape(3, row_count, -1)
    )
    grad_qkv = mix("td,jte->jde", normed_first, grad_proj)
    grad_first = lax.psum_scatter(
        mix("jte,jde->td", grad_proj, full_qkv).astype(jnp.bfloat16),
        "tensor",
        scatter_dimension=0,
        tiled=True,
    ).astype(jnp.float32)
    part_gain_attn = jnp.sum(grad_first * unit_first, axis=0)
    grad_in = grad_middle + norm_back(
        grad_first, full_gain_attn.astype(jnp.float32), unit_first, scale_first
    )
    sum_gain_attn, sum_qkv, sum_out = (
        lax.psum_scatter(
            part_gain_attn.astype(jnp.bfloat16), "dp", scatter_dimension=0, tiled=True
        ).astype(jnp.float32),
        lax.psum_scatter(
            grad_qkv.astype(jnp.bfloat16), "dp", scatter_dimension=1, tiled=True
        ).astype(jnp.float32),
        lax.psum_scatter(
            grad_out.astype(jnp.bfloat16), "dp", scatter_dimension=1, tiled=True
        ).astype(jnp.float32),
    )
    total_gain_attn, total_gain_mlp = lax.psum((sum_gain_attn, sum_gain_mlp), "tensor")
    return (
        layer_out,
        grad_in,
        total_gain_attn,
        sum_qkv,
        sum_out,
        total_gain_mlp,
        sum_gate_up,
        sum_down,
    )


def solution(mesh):
    placed = (
        P(("dp", "tensor"), None),
        P(("dp", "tensor"), None),
        P("dp"),
        P("dp"),
        P(None, "dp", "tensor"),
        P("tensor", "dp"),
        P("dp"),
        P("dp", None, "tensor"),
        P("tensor", "dp"),
    )
    return jax.shard_map(
        on_device,
        mesh=mesh,
        in_specs=placed,
        out_specs=(
            P(("dp", "tensor"), None),
            P(("dp", "tensor"), None),
            P("dp"),
            P(None, "dp", "tensor"),
            P("tensor", "dp"),
            P("dp"),
            P("dp", None, "tensor"),
            P("tensor", "dp"),
        ),
        check_vma=False,
    )
```

profile of v0, /device:TPU:0, one launch (start us, length us, event | category | flops | bytes accessed | tf_op | source)
XLA Modules:
  0.0 2341.6 jit_solution(4158780240672994647)
XLA Ops:
  7.9 27.7 %all-gather = bf16[8,1,384]{2,1,0:T(2,128)(2,1)S(1)} all-gather(bf16[1,1,384]{2,1,0:T(2,128)(2,1)S(1)} %reshape.150), channel_id=1, replica_groups=mesh['dp'=8,'tensor'=4] {'dp'}, dimensions={0}, use_global_device_ids=true | all-gather | bytes 6912 | tf_op jit(solution)/shard_map/all_gather | solution.py:110
  43.5 24.5 %all-gather.11.cloned.1.call-done = bf16[512,3072]{1,0:T(8,128)(2,1)} async-done(((bf16[128,3072]{1,0:T(8,128)(2,1)}), bf16[512,3072]{1,0:T(8,128)(2,1)}) %all-gather.11.cloned.1.call-update) | async-done | bytes 3145744 | tf_op jit(solution)/shard_map/all_gather | solution.py:137
  67.9 197.8 %all-gather.13.cloned.1.call-done = bf16[3,3072,768]{2,1,0:T(8,128)(2,1)} async-done(((bf16[3,384,768]{2,1,0:T(8,128)(2,1)}), bf16[3,3072,768]{2,1,0:T(8,128)(2,1)}) %all-gather.13.cloned.1.call-update) | async-done | bytes 14155792 | tf_op jit(solution)/shard_map/all_gather | solution.py:111
  265.8 11.3 fusion.11
  295.4 51.7 %all-gather.15.cloned.1.call-done = bf16[768,3072]{1,0:T(8,128)(2,1)} async-done(((bf16[768,384]{1,0:T(8,128)(2,1)}), bf16[768,3072]{1,0:T(8,128)(2,1)}) %all-gather.15.cloned.1.call-update) | async-done | bytes 4718608 | tf_op jit(solution)/shard_map/all_gather | solution.py:112
  347.2 6.9 fusion.40
  354.7 26.4 %all-gather.1 = bf16[8,1,384]{2,1,0:T(2,128)(2,1)S(1)} all-gather(bf16[1,1,384]{2,1,0:T(2,128)(2,1)S(1)} %reshape.152), channel_id=1, replica_groups=mesh['dp'=8,'tensor'=4] {'dp'}, dimensions={0}, use_global_device_ids=true | all-gather | bytes 6912 | tf_op jit(solution)/shard_map/all_gather | solution.py:118
  381.1 29.7 %reduce-scatter.15.cloned.1.call-done = f32[128,3072]{1,0:T(8,128)} async-done(((f32[512,3072]{1,0:T(8,128)}), f32[128,3072]{1,0:T(8,128)}) %reduce-scatter.15.cloned.1.call-update) | async-done | bytes 1572880 | tf_op jit(solution)/shard_map/reduce_scatter | solution.py:151
  422.0 20.3 all-gather.17.cloned.1.call-done
  442.3 482.5 %all-gather.19.cloned.1.call-done = bf16[3072,2,2048]{2,0,1:T(8,128)(2,1)} async-done(((bf16[384,2,2048]{2,0,1:T(8,128)(2,1)}), bf16[3072,2,2048]{2,0,1:T(8,128)(2,1)}) %all-gather.19.cloned.1.call-update) | async-done | bytes 25165840 | tf_op jit(solution)/shard_map/all_gather | solution.py:119
  924.9 20.9 convolution_bitcast_fusion.1
  945.7 9.9 all-gather.23.cloned.1.call-done
  955.6 178.9 %all-gather.21.cloned.1.call-done = bf16[2048,3072]{1,0:T(8,128)(2,1)} async-done(((bf16[2048,384]{1,0:T(8,128)(2,1)}), bf16[2048,3072]{1,0:T(8,128)(2,1)}) %all-gather.21.cloned.1.call-update) | async-done | bytes 12582928 | tf_op jit(solution)/shard_map/all_gather | solution.py:120
  1134.5 17.0 fusion.15
  1151.5 19.7 convolution_bitcast_fusion
  1171.2 13.9 convolution_convert_fusion.3
  1185.2 42.6 %reduce-scatter.19.cloned.1.call-done = f32[128,3072]{1,0:T(8,128)} async-done(((f32[512,3072]{1,0:T(8,128)}), f32[128,3072]{1,0:T(8,128)}) %reduce-scatter.19.cloned.1.call-update) | async-done | bytes 1572880 | tf_op jit(solution)/shard_map/reduce_scatter | solution.py:191
  1229.7 39.1 %reduce-scatter.17.cloned.1.call-done = bf16[128,3072]{1,0:T(8,128)(2,1)} async-done(((bf16[512,3072]{1,0:T(8,128)(2,1)}), bf16[128,3072]{1,0:T(8,128)(2,1)}) %reduce-scatter.17.cloned.1.call-update) | async-done | bytes 786448 | tf_op jit(solution)/shard_map/reduce_scatter | solution.py:172
  1273.1 28.6 %all-gather.25.cloned.1.call-done = bf16[512,3072]{1,0:T(8,128)(2,1)} async-done(((bf16[128,3072]{1,0:T(8,128)(2,1)}), bf16[512,3072]{1,0:T(8,128)(2,1)}) %all-gather.25.cloned.1.call-update) | async-done | bytes 3145744 | tf_op jit(solution)/shard_map/all_gather | solution.py:210
  1327.5 12.1 bitcast_convert_fusion
  1339.6 11.9 convolution_convert_fusion.1
  1351.5 16.7 copy.85
  1382.7 12.0 convert_bitcast_fusion
  1394.8 28.3 %copy.81 = bf16[3,3072,768]{2,0,1:T(4,128)(2,1)} copy(bf16[3,3072,768]{1,2,0:T(8,128)(2,1)} %convert_bitcast_fusion) | data formatting | bytes 28311552
  1423.1 16.9 copy.87
  1442.0 19.2 convolution_convert_fusion
  1464.9 39.1 %all-reduce.3 = (bf16[3072]{0:T(1024)(128)(2,1)S(1)}, bf16[3072]{0:T(1024)(128)(2,1)S(1)}) all-reduce(bf16[3072]{0:T(1024)(128)(2,1)S(1)} %get-tuple-element.88, bf16[3072]{0:T(1024)(128)(2,1)S(1)} %get-tuple-element.86), channel_id=6, replica_groups=mesh['dp'=8,'tensor'=4] {'dp'}, use_global_device_ids=true, to_apply=%region_12.13.clone | all-reduce | flops 6144 | bytes 24576
  1513.7 75.4 %reduce-scatter.29.cloned.1.call-done = bf16[384,2048]{1,0:T(8,128)(2,1)} async-done(((bf16[3072,2048]{1,0:T(8,128)(2,1)}), bf16[384,2048]{1,0:T(8,128)(2,1)}) %reduce-scatter.29.cloned.1.call-update) | async-done | bytes 1572880
  1592.9 94.3 %reduce-scatter.27.cloned.1.call-done = bf16[384,768]{1,0:T(8,128)(2,1)} async-done(((bf16[3072,768]{1,0:T(8,128)(2,1)}), bf16[384,768]{1,0:T(8,128)(2,1)}) %reduce-scatter.27.cloned.1.call-update) | async-done | bytes 589840
  1689.6 230.0 %reduce-scatter.25.cloned.1.call-done = bf16[384,2304]{1,0:T(8,128)(2,1)} async-done(((bf16[3072,2304]{1,0:T(8,128)(2,1)}), bf16[384,2304]{1,0:T(8,128)(2,1)}) %reduce-scatter.25.cloned.1.call-update) | async-done | bytes 1769488
  1930.7 396.2 %reduce-scatter.23.cloned.1.call-done = bf16[384,2,2048]{2,0,1:T(8,128)(2,1)} async-done(((bf16[3072,2,2048]{2,0,1:T(8,128)(2,1)}), bf16[384,2,2048]{2,0,1:T(8,128)(2,1)}) %reduce-scatter.23.cloned.1.call-update) | async-done | bytes 3145744 | tf_op jit(solution)/shard_map/reduce_scatter | solution.py:202
  2327.0 7.9 copy.72
  (147 shorter events, 116.1 us)
Async XLA Ops:
  7.2 60.8 %all-gather.11.cloned.1.call-start = ((), (), s32[]{:S(2)}) async-start(), calls=%async_computation.8 | async-start | bytes 3932160 | tf_op jit(solution)/shard_map/all_gather | solution.py:137
  39.8 226.0 %all-gather.13.cloned.1.call-start = ((), (), s32[]{:S(2)}) async-start(), calls=%async_computation.9 | async-start | bytes 15925248 | tf_op jit(solution)/shard_map/all_gather | solution.py:111
  40.6 306.6 %all-gather.15.cloned.1.call-start = ((), (), s32[]{:S(2)}) async-start(), calls=%async_computation.10 | async-start | bytes 5308416 | tf_op jit(solution)/shard_map/all_gather | solution.py:112
  41.3 369.5 %reduce-scatter.15.cloned.1.call-start = ((), (), s32[]{:S(2)}) async-start(), calls=%async_computation.11 | async-start | bytes 7864320 | tf_op jit(solution)/shard_map/reduce_scatter | solution.py:151
  277.1 2.2 copy-start.9
  288.0 1.6 copy-start.3
  288.0 1.6 copy-start.5
  289.7 3.3 copy-start
  289.7 3.3 copy-start.16
  295.4 58.6 %copy-start.10 = (bf16[8,96,512]{2,1,0:T(8,128)(2,1)}, bf16[8,96,512]{2,1,0:T(8,128)(2,1)S(1)}, u32[]{:S(2)}) copy-start(bf16[8,96,512]{2,1,0:T(8,128)(2,1)S(1)} %convolution_convert_fusion.6) | copy-start | bytes 2359300
  354.0 56.8 %copy-start.1 = (bf16[128,3072]{1,0:T(8,128)(2,1)S(1)}, bf16[128,3072]{1,0:T(8,128)(2,1)}, u32[]{:S(2)}) copy-start(bf16[128,3072]{1,0:T(8,128)(2,1)} %param.9) | copy-start | bytes 2359300
  354.1 88.3 %all-gather.17.cloned.1.call-start = ((), (), s32[]{:S(2)}) async-start(), calls=%async_computation.12 | async-start | bytes 3932160 | tf_op jit(solution)/shard_map/all_gather | solution.py:159
  413.7 511.2 %all-gather.19.cloned.1.call-start = ((), (), s32[]{:S(2)}) async-start(), calls=%async_computation.13 | async-start | bytes 28311552 | tf_op jit(solution)/shard_map/all_gather | solution.py:119
  418.6 1.5 copy-start.7
  418.7 537.0 %all-gather.23.cloned.1.call-start = ((), (), s32[]{:S(2)}) async-start(), calls=%async_computation.16 | async-start | bytes 3932160 | tf_op jit(solution)/shard_map/all_gather | solution.py:181
  421.2 713.2 %all-gather.21.cloned.1.call-start = ((), (), s32[]{:S(2)}) async-start(), calls=%async_computation.14 | async-start | bytes 14155776 | tf_op jit(solution)/shard_map/all_gather | solution.py:120
  422.0 805.9 %reduce-scatter.19.cloned.1.call-start = ((), (), s32[]{:S(2)}) async-start(), calls=%async_computation.17 | async-start | bytes 7864320 | tf_op jit(solution)/shard_map/reduce_scatter | solution.py:191
  1171.2 97.7 %reduce-scatter.17.cloned.1.call-start = ((), (), s32[]{:S(2)}) async-start(), calls=%async_computation.15 | async-start | bytes 3932160 | tf_op jit(solution)/shard_map/reduce_scatter | solution.py:172
  1185.2 116.5 %all-gather.25.cloned.1.call-start = ((), (), s32[]{:S(2)}) async-start(), calls=%async_computation.18 | async-start | bytes 3932160 | tf_op jit(solution)/shard_map/all_gather | solution.py:210
  1273.0 190.1 %reduce-scatter.21.cloned.1.call-start = ((), (), s32[]{:S(2)}) async-start(), calls=%async_computation.19 | async-start | bytes 3932160 | tf_op jit(solution)/shard_map/reduce_scatter | solution.py:228
  1307.9 6.6 copy-start.11
  1314.5 1.7 copy-start.17
  1316.2 5.7 copy-start.6
  1339.6 249.5 %reduce-scatter.29.cloned.1.call-start = ((), (), s32[]{:S(2)}) async-start(), calls=%async_computation.23 | async-start | bytes 14155776
  1368.3 318.9 %reduce-scatter.27.cloned.1.call-start = ((), (), s32[]{:S(2)}) async-start(), calls=%async_computation.22 | async-start | bytes 5308416
  1381.6 538.0 %reduce-scatter.25.cloned.1.call-start = ((), (), s32[]{:S(2)}) async-start(), calls=%async_computation.21 | async-start | bytes 15925248
  1440.0 2.0 copy-start.24
  1440.0 887.0 %reduce-scatter.23.cloned.1.call-start = ((), (), s32[]{:S(2)}) async-start(), calls=%async_computation.20 | async-start | bytes 28311552 | tf_op jit(solution)/shard_map/reduce_scatter | solution.py:202
  1461.2 1.9 copy-start.2
  1461.2 1.9 copy-start.20
  1461.2 1.9 copy-start.22
  1461.2 49.7 %copy-start.8 = (f32[128,3072]{1,0:T(8,128)S(1)}, f32[128,3072]{1,0:T(8,128)}, u32[]{:S(2)}) copy-start(f32[128,3072]{1,0:T(8,128)} %get-tuple-element.95) | copy-start | bytes 4718596
  (10 other events, 10.1 us)
Sparse Core Ops, SparseCore 0:
  39.9 27.9 all-gather.10
  70.1 195.6 all-gather.12
  267.8 79.2 all-gather.14
  354.2 56.5 reduce-scatter.14
  413.8 28.5 all-gather.16
  444.4 480.4 all-gather.18
  927.1 28.5 all-gather.22
  957.9 176.5 all-gather.20
  1171.3 56.5 reduce-scatter.18
  1230.8 37.9 reduce-scatter.16
  1273.1 28.5 all-gather.24
  1339.7 37.9 reduce-scatter.20
  1381.3 207.7 reduce-scatter.28
  1592.6 94.4 reduce-scatter.26
  1690.7 228.9 reduce-scatter.24
  1923.4 403.5 reduce-scatter.22
where the time goes:
time: 2350 us; the launch traced here: 2340 us
  waiting for transfers between devices  1900 us (81%)
  matrix products  176 us (7%)
  local copies, waits for them, and re-layouts  118 us (5%)
  blocking collectives  100 us (4%)
  other arithmetic  27.1 us (1%)
    all_gather x1, waiting for transfers between devices, fetch_mlp(): lax.all_gather(w_gate_up, 'dp', axis=0, tiled=True)  483 us
    unnamed x19, waiting for transfers between devices  402 us
    reduce_scatter x1, waiting for transfers between devices, on_device(): lax.psum_scatter(grad_gate_up.astype(jnp.bfloat16), 'dp', scatter_dimensi...  396 us
    all_gather x1, waiting for transfers between devices, fetch_attention(): lax.all_gather(w_qkv, 'dp', axis=1, tiled=True)  198 us
    all_gather x1, waiting for transfers between devices, fetch_mlp(): lax.all_gather(w_down, 'dp', axis=1, tiled=True)  179 us
    dot_general x12, matrix products, mix(): return jnp.einsum(form, left, right, preferred_element_type=jnp.float32)  114 us
    unnamed x66, local copies, waits for them, and re-layouts  108 us
    all_gather x1, waiting for transfers between devices, fetch_attention(): lax.all_gather(w_out, 'dp', axis=1, tiled=True)  51.7 us
  transfers between devices with their start and end apart: 16, of which 15 were waited for; matrix products, arithmetic and copies ran while one was open for 9% of the time, Pallas kernels for 0%

commit v1 on v0

v1 whole, which is shorter than its diff:
```python
import math

import jax
import jax.numpy as jnp
from jax import lax
from jax.sharding import PartitionSpec as P

HEAD_DIM = 96
NORM_EPS = 1e-05
ROPE_BASE = 10000.0
AXES = ("dp", "tensor")
PAIR = 2
NEAR = 1

bf16 = jnp.bfloat16
f32 = jnp.float32


def rotate(values):
    half_width = values.shape[-1] // 2
    return jnp.concatenate([-values[..., half_width:], values[..., :half_width]], axis=-1)


def rotate_back(values):
    half_width = values.shape[-1] // 2
    return jnp.concatenate([values[..., half_width:], -values[..., :half_width]], axis=-1)


def rms_unit(values):
    scale_inv = lax.rsqrt(jnp.mean(values * values, axis=1, keepdims=True) + NORM_EPS)
    return (values * scale_inv, scale_inv)


def norm_back(grad_normed, gain, unit, scale_inv):
    grad_unit = grad_normed * gain
    return scale_inv * (grad_unit - unit * jnp.mean(grad_unit * unit, axis=1, keepdims=True))


def mix(form, left, right):
    return jnp.einsum(form, left, right, preferred_element_type=f32)


class Wires:
    def __init__(self, dp, tp):
        self.dp, self.tp = dp, tp
        self.order = list(range(0, dp, 2)) + list(range(1, dp, 2))
        self.place = {m: p for p, m in enumerate(self.order)}
        self.far = [m for m in range(0, dp, 2) if not m & PAIR]

    def over_dp(self, value, mask):
        pairs = []
        for d in range(self.dp):
            for t in range(self.tp):
                pairs.append((d * self.tp + t, (d ^ mask) * self.tp + t))
        return lax.ppermute(value, AXES, pairs)

    def over_tensor(self, value, mask):
        pairs = []
        for d in range(self.dp):
            for t in range(self.tp):
                pairs.append((d * self.tp + t, d * self.tp + (t ^ mask)))
        return lax.ppermute(value, AXES, pairs)

    def to_relative(self, value, d):
        width = value.shape[1] // self.dp
        return jnp.concatenate(
            [lax.dynamic_slice_in_dim(value, (d ^ m) * width, width, 1) for m in self.order], axis=1
        )

    def to_absolute(self, value, d):
        width = value.shape[1] // self.dp
        parts = []
        for j in range(self.dp):
            m = d ^ j
            place = (m >> 1) + (self.dp // 2) * (m & 1)
            parts.append(lax.dynamic_slice_in_dim(value, place * width, width, 1))
        return jnp.concatenate(parts, axis=1)

    def swap_pair(self, value):
        width = value.shape[1] // self.dp
        parts = []
        for m in self.order:
            p = self.place[m ^ PAIR]
            parts.append(value[:, p * width : (p + 1) * width])
        return jnp.concatenate(parts, axis=1)

    def gather_rows(self, value):
        by_z = self.over_dp(self.swap_pair(value), PAIR)
        by_y = self.over_tensor(value, 2)
        by_zy = self.over_tensor(by_z, 2)
        parts = []
        for part in (value, by_y, by_z, by_zy):
            parts += [part, self.over_tensor(part, 1)]
        return jnp.concatenate(parts, axis=0)

    def sum_rows(self, value):
        rows = value.shape[0] // 8
        blocks = value.reshape(4, 2, rows, value.shape[1])
        halves = []
        for q in range(4):
            got = self.over_tensor(blocks[q, 1].astype(bf16), 1)
            halves.append(blocks[q, 0].astype(f32) + got.astype(f32))
        own, by_y, by_z, by_zy = halves
        got = self.over_tensor(by_zy.astype(bf16), 2)
        by_z = self.swap_pair((by_z + got.astype(f32)).astype(bf16))
        total = own + self.over_tensor(by_y.astype(bf16), 2).astype(f32)
        return total + self.over_dp(by_z, PAIR).astype(f32)

    def gather_weight(self, own, other):
        blocks = {0: own}
        for f in self.far:
            if f:
                blocks[f] = self.over_dp(own, f)
            blocks[f ^ PAIR] = self.over_dp(other, f ^ PAIR)
        for m in list(blocks):
            blocks[m ^ NEAR] = self.over_dp(blocks[m], NEAR)
        return blocks

    def sum_weight(self, even, odd):
        totals = {}
        for m in odd:
            e = m ^ NEAR
            totals[e] = (even[e] + self.over_dp(odd[m].astype(bf16), NEAR).astype(f32)).astype(bf16)
        own = totals[0].astype(f32)
        other = None
        for f in self.far:
            if f:
                own = own + self.over_dp(totals[f], f).astype(f32)
            got = self.over_dp(totals[f ^ PAIR], f ^ PAIR).astype(f32)
            other = got if other is None else other + got
        return own, other


def halves(value, side, axis):
    width = value.shape[axis] // 2
    own = lax.dynamic_slice_in_dim(value, side * width, width, axis)
    other = lax.dynamic_slice_in_dim(value, (1 - side) * width, width, axis)
    return own, other


def joined(own, other, side, axis):
    low = jnp.where(side == 0, own, other)
    high = jnp.where(side == 0, other, own)
    return jnp.concatenate([low, high], axis=axis)


def held_until(value, *waited):
    return lax.optimization_barrier((value, waited))[0]


def on_device(dp, tp, hidden_in, cotangent, lengths, gain_attn, w_qkv, w_out, gain_mlp, w_gate_up, w_down):
    wires = Wires(dp, tp)
    order = wires.order
    half = dp // 2
    d = lax.axis_index("dp")
    t = lax.axis_index("tensor")
    side = (d // PAIR) % 2
    local_rows, width = hidden_in.shape
    group_rows = local_rows * tp
    kb = width // dp
    head_count = w_qkv.shape[2] // HEAD_DIM // 2
    heads = (2, group_rows, head_count, HEAD_DIM)

    pair_gain = jnp.stack([gain_attn, gain_mlp])
    gain_parts = [pair_gain if m == 0 else wires.over_dp(pair_gain, m) for m in order]
    gains = jnp.concatenate(gain_parts, axis=1).astype(f32)
    gain_a, gain_m = gains[0:1], gains[1:2]
    own_length = lengths[0]
    pair_length = wires.over_dp(lengths, PAIR)[0]

    qkv_halves = halves(w_qkv, side, 2)
    out_halves = halves(w_out, side, 0)
    down_halves = halves(w_down, side, 0)
    gu = jnp.transpose(w_gate_up, (1, 0, 2))
    gu_own, gu_other = halves(gu, side, 2)

    b_qkv = wires.gather_weight(*qkv_halves)
    b_out = wires.gather_weight(*held_until(out_halves, b_qkv[PAIR]))
    b_down = wires.gather_weight(*held_until(down_halves, b_out[PAIR], b_qkv[PAIR ^ wires.far[-1]]))
    ff = gu_own.shape[2]
    cut = ff // 2
    b_gu = []
    waited = (b_down[PAIR], b_out[PAIR ^ wires.far[-1]])
    for k in range(2):
        piece = (gu_own[:, :, k * cut : (k + 1) * cut], gu_other[:, :, k * cut : (k + 1) * cut])
        b_gu.append(wires.gather_weight(*held_until(piece, *waited)))
        waited = (b_gu[-1][PAIR], b_down[PAIR ^ wires.far[-1]])

    full_qkv = jnp.concatenate([b_qkv[m] for m in order], axis=1)
    full_out = jnp.concatenate([b_out[m] for m in order], axis=1)
    full_down = jnp.concatenate([b_down[m] for m in order], axis=1)
    full_gu = [jnp.concatenate([b[m] for m in order], axis=1) for b in b_gu]

    starts = jnp.stack([(t ^ q) * local_rows for q in range(tp)])
    positions = (starts[:, None] + jnp.arange(local_rows, dtype=jnp.int32)[None, :]).reshape(-1)
    exponent = jnp.arange(HEAD_DIM // 2).astype(f32) * (2.0 / HEAD_DIM)
    frequency = ROPE_BASE ** (-exponent)
    angles = positions.astype(f32)[:, None] * frequency[None, :]
    cosine = jnp.concatenate([jnp.cos(angles), jnp.cos(angles)], axis=1)[None, :, None, :]
    sine = jnp.concatenate([jnp.sin(angles), jnp.sin(angles)], axis=1)[None, :, None, :]
    live_all = jnp.stack([positions < own_length, positions < pair_length])
    own_rows = t * local_rows + jnp.arange(local_rows, dtype=jnp.int32)
    live = (own_rows < own_length).astype(f32)[:, None]
    allowed = (positions[None, None, :] <= positions[None, :, None]) & (
        live_all[:, :, None] == live_all[:, None, :]
    )

    input_f = wires.to_relative(hidden_in, d).astype(f32)
    unit_first, scale_first = rms_unit(input_f)
    normed_first = wires.gather_rows((unit_first * gain_a).astype(bf16))
    projected = mix("td,jde->jte", normed_first, full_qkv)
    query_raw = projected[0].reshape(heads)
    key_raw = projected[1].reshape(heads)
    queries = (query_raw * cosine + rotate(query_raw) * sine).astype(bf16)
    keys = (key_raw * cosine + rotate(key_raw) * sine).astype(bf16)
    values = projected[2].reshape(heads).astype(bf16)
    scale = 1.0 / math.sqrt(HEAD_DIM)
    scores = mix("gqhd,gkhd->ghqk", queries, keys) * scale
    scores = jnp.where(allowed[:, None], scores, -jnp.inf)
    row_max = jnp.max(scores, axis=3, keepdims=True)
    log_total = row_max + jnp.log(jnp.sum(jnp.exp(scores - row_max), axis=3, keepdims=True))
    attn_prob = jnp.exp(scores - log_total).astype(bf16)
    mixed = mix("ghqk,gkhd->gqhd", attn_prob, values).astype(bf16)
    attn_flat = mixed.reshape(2 * group_rows, -1)
    middle = input_f + wires.sum_rows(jnp.dot(attn_flat, full_out, preferred_element_type=f32).astype(bf16))

    grad_rows = wires.to_relative(cotangent, d) * live
    unit_second, scale_second = rms_unit(middle)
    normed_second = wires.gather_rows((unit_second * gain_m).astype(bf16))
    grad_half = wires.gather_rows(grad_rows.astype(bf16))
    grad_act = jnp.dot(grad_half, full_down.T, preferred_element_type=f32)

    acts, grads_gu, gu_sums, second = [], [], [], None
    cols_even = slice(0, half * kb)
    cols_odd = slice(half * kb, None)

    def row_blocks(big, masks, axis):
        out = {}
        for i, m in enumerate(masks):
            out[m] = lax.slice_in_dim(big, i * kb, (i + 1) * kb, axis=axis)
        return out

    evens, odds = order[:half], order[half:]
    for k in range(2):
        gate_up = mix("td,jdf->jtf", normed_second, full_gu[k])
        gate, up = gate_up[0], gate_up[1]
        sig = jax.nn.sigmoid(gate)
        acts.append((gate * sig * up).astype(bf16))
        ga = grad_act[:, k * cut : (k + 1) * cut]
        g = jnp.stack([ga * up * sig * (1.0 + gate * (1.0 - sig)), ga * gate * sig]).astype(bf16)
        grads_gu.append(g)
        part = mix("jtf,jdf->td", g, full_gu[k])
        second = part if second is None else second + part
    activated = jnp.concatenate(acts, axis=1)

    down_odd = jnp.dot(activated.T, grad_half[:, cols_odd], preferred_element_type=f32).astype(bf16)
    down_even = jnp.dot(activated.T, grad_half[:, cols_even], preferred_element_type=f32)
    sum_down = wires.sum_weight(row_blocks(down_even, evens, 1), row_blocks(down_odd, odds, 1))
    for k in range(2):
        g_odd = mix("td,jtf->jdf", normed_second[:, cols_odd], grads_gu[k]).astype(bf16)
        g_even = mix("td,jtf->jdf", normed_second[:, cols_even], grads_gu[k])
        gu_sums.append(wires.sum_weight(row_blocks(g_even, evens, 1), row_blocks(g_odd, odds, 1)))

    grad_second = wires.sum_rows(second.astype(bf16))
    part_gain_mlp = jnp.sum(grad_second * unit_second, axis=0)
    grad_middle = grad_rows + norm_back(grad_second, gain_m, unit_second, scale_second)
    middle_half = wires.gather_rows(grad_middle.astype(bf16))

    mlp = wires.sum_rows(jnp.dot(activated, full_down, preferred_element_type=f32).astype(bf16))
    layer_out = wires.to_absolute((middle + mlp) * live, d)

    out_odd = jnp.dot(attn_flat.T, middle_half[:, cols_odd], preferred_element_type=f32).astype(bf16)
    out_even = jnp.dot(attn_flat.T, middle_half[:, cols_even], preferred_element_type=f32)
    sum_out = wires.sum_weight(row_blocks(out_even, evens, 1), row_blocks(out_odd, odds, 1))
    grad_mixed = (
        jnp.dot(middle_half, full_out.T, preferred_element_type=f32).astype(bf16).reshape(heads)
    )
    delta = jnp.sum(grad_mixed.astype(f32) * mixed.astype(f32), axis=3)
    delta = jnp.transpose(delta, (0, 2, 1))[..., None]
    prob_full = jnp.exp(scores - log_total)
    grad_prob = mix("gqhd,gkhd->ghqk", grad_mixed, values)
    grad_score = (prob_full * (grad_prob - delta) * scale).astype(bf16)
    grad_query = mix("ghqk,gkhd->gqhd", grad_score, keys)
    grad_keys = mix("ghqk,gqhd->gkhd", grad_score, queries)
    grad_values = mix("ghqk,gqhd->gkhd", prob_full.astype(bf16), grad_mixed)
    query_back = grad_query * cosine + rotate_back(grad_query * sine)
    key_back = grad_keys * cosine + rotate_back(grad_keys * sine)
    grad_proj = (
        jnp.stack([query_back, key_back, grad_values]).astype(bf16).reshape(3, 2 * group_rows, -1)
    )
    q_odd = mix("td,jte->jde", normed_first[:, cols_odd], grad_proj).astype(bf16)
    q_even = mix("td,jte->jde", normed_first[:, cols_even], grad_proj)
    sum_qkv = wires.sum_weight(row_blocks(q_even, evens, 1), row_blocks(q_odd, odds, 1))
    grad_first = wires.sum_rows(mix("jte,jde->td", grad_proj, full_qkv).astype(bf16))
    part_gain_attn = jnp.sum(grad_first * unit_first, axis=0)
    grad_in = grad_middle + norm_back(grad_first, gain_a, unit_first, scale_first)
    grad_in = wires.to_absolute(grad_in, d)

    parts = jnp.stack([part_gain_attn, part_gain_mlp]).reshape(2, dp, kb)
    total = parts[:, wires.place[0]]
    for m in order:
        if m:
            total = total + wires.over_dp(parts[:, wires.place[m]], m)
    for mask in (1, 2):
        total = total + wires.over_tensor(total, mask)

    gu_own = jnp.concatenate([s[0] for s in gu_sums], axis=2)
    gu_other = jnp.concatenate([s[1] for s in gu_sums], axis=2)
    return (
        layer_out,
        grad_in,
        total[0],
        joined(*sum_qkv, side, 2),
        joined(*sum_out, side, 0),
        total[1],
        jnp.transpose(joined(gu_own, gu_other, side, 2), (1, 0, 2)),
        joined(*sum_down, side, 0),
    )


def solution(mesh):
    placed = (
        P(("dp", "tensor"), None),
        P(("dp", "tensor"), None),
        P("dp"),
        P("dp"),
        P(None, "dp", "tensor"),
        P("tensor", "dp"),
        P("dp"),
        P("dp", None, "tensor"),
        P("tensor", "dp"),
    )
    dp, tp = mesh.shape["dp"], mesh.shape["tensor"]

    def body(*args):
        return on_device(dp, tp, *args)

    return jax.shard_map(
        body,
        mesh=mesh,
        in_specs=placed,
        out_specs=(
            P(("dp", "tensor"), None),
            P(("dp", "tensor"), None),
            P("dp"),
            P(None, "dp", "tensor"),
            P("tensor", "dp"),
            P("dp"),
            P("dp", None, "tensor"),
            P("tensor", "dp"),
        ),
        check_vma=False,
    )
```

time: 2350 us -> 1400 us (0.60)
  waiting for transfers between devices: 1900 us -> 790 us
  starting transfers between devices: 0.65 us -> 160 us
  blocking collectives: 100 us -> 0 us
  local copies, waits for them, and re-layouts: 118 us -> 199 us
  other arithmetic: 27.1 us -> 67.5 us
    all_gather x8 -> x0, waiting for transfers between devices: 994 us -> none  [the longest x1 483 us: fetch_mlp(): lax.all_gather(w_gate_up, 'dp', axis=0, tiled=True)]
    ppermute x0 -> x143, waiting for transfers between devices: none -> 790 us  [the longest x93 700 us: over_dp(): return lax.ppermute(value, AXES, pairs)]
    reduce_scatter x5 -> x0, waiting for transfers between devices: 508 us -> none  [the longest x1 396 us: on_device(): lax.psum_scatter(grad_gate_up.astype(jnp.bfloat16), 'dp', scatter_dimensi...]
    unnamed x19 -> x0, waiting for transfers between devices: 402 us -> none
    ppermute x0 -> x143, starting transfers between devices: none -> 160 us  [the longest x93 148 us: over_dp(): return lax.ppermute(value, AXES, pairs)]
    all_gather x2 -> x0, blocking collectives: 54 us -> none  [the longest x1 27.7 us: fetch_attention(): lax.all_gather(gain_attn, 'dp', axis=0, tiled=True)]
    unnamed x1 -> x0, blocking collectives: 39.1 us -> none
    another operation x3 -> x17, local copies, waits for them, and re-layouts: 2.83 us -> 27.5 us  [the longest x7 12 us: on_device(): jnp.stack([query_back, key_back, grad_values]).astype(bf16)]
  transfers between devices with their start and end apart: 16 -> 143, of which waited for: 15 -> 60; matrix products, arithmetic and copies ran while one was open for 9% -> 20% of each run, Pallas kernels for 0% -> 0%
where the time goes in v1:
time: 1400 us; the launch traced here: 1390 us
  waiting for transfers between devices  790 us (56%)
  local copies, waits for them, and re-layouts  199 us (14%)
  matrix products  172 us (12%)
  starting transfers between devices  160 us (11%)
  other arithmetic  67.5 us (5%)
    ppermute x93, waiting for transfers between devices, over_dp(): return lax.ppermute(value, AXES, pairs)  700 us
    ppermute x93, starting transfers between devices, over_dp(): return lax.ppermute(value, AXES, pairs)  148 us
    unnamed x376, local copies, waits for them, and re-layouts  130 us
    dot_general x18, matrix products, mix(): return jnp.einsum(form, left, right, preferred_element_type=f32)  123 us
    ppermute x50, waiting for transfers between devices, over_tensor(): return lax.ppermute(value, AXES, pairs)  89.4 us
  transfers between devices with their start and end apart: 143, of which 60 were waited for; matrix products, arithmetic and copies ran while one was open for 20% of the time, Pallas kernels for 0%

profile of v1, /device:TPU:0, one launch (start us, length us, event | category | flops | bytes accessed | tf_op | source)
XLA Modules:
  0.0 1392.3 jit_solution(13536096128090239769)
XLA Ops:
  74.7 14.3 %collective-permute-done.72 = bf16[128,3072]{1,0:T(8,128)(2,1)S(1)} collective-permute-done((bf16[128,3072]{1,0:T(8,128)(2,1)}, bf16[128,3072]{1,0:T(8,128)(2,1)S(1)}, u32[]{:S(2)}, u32[]{:S(2)}) %collective-permute-start.72) | collective-permute-done | bytes 786464 | tf_op jit(solution)/shard_map/ppermute | solution.py:62
  107.4 23.1 %collective-permute-done = bf16[3,384,384]{1,2,0:T(8,128)(2,1)S(1)} collective-permute-done((bf16[3,384,384]{1,2,0:T(8,128)(2,1)}, bf16[3,384,384]{1,2,0:T(8,128)(2,1)S(1)}, u32[]{:S(2)}, u32[]{:S(2)}) %collective-permute-start) | collective-permute-done | bytes 884768 | tf_op jit(solution)/shard_map/ppermute | solution.py:55
  146.2 29.9 %collective-permute-done.22 = bf16[384,384]{1,0:T(8,128)(2,1)S(1)} collective-permute-done((bf16[384,384]{1,0:T(8,128)(2,1)S(1)}, bf16[384,384]{1,0:T(8,128)(2,1)S(1)}, u32[]{:S(2)}, u32[]{:S(2)}) %collective-permute-start.22) | collective-permute-done | bytes 294944 | tf_op jit(solution)/shard_map/ppermute | solution.py:55
  249.5 18.0 %collective-permute-done.6 = bf16[3,384,384]{1,2,0:T(8,128)(2,1)S(1)} collective-permute-done((bf16[3,384,384]{1,2,0:T(8,128)(2,1)S(1)}, bf16[3,384,384]{1,2,0:T(8,128)(2,1)S(1)}, u32[]{:S(2)}, u32[]{:S(2)}) %collective-permute-start.6) | collective-permute-done | bytes 884768 | tf_op jit(solution)/shard_map/ppermute | solution.py:55
  271.8 14.5 %collective-permute-done.59 = bf16[1024,384]{1,0:T(8,128)(2,1)} collective-permute-done((bf16[1024,384]{1,0:T(8,128)(2,1)}, bf16[1024,384]{1,0:T(8,128)(2,1)}, u32[]{:S(2)}, u32[]{:S(2)}) %collective-permute-start.59) | collective-permute-done | bytes 786464 | tf_op jit(solution)/shard_map/ppermute | solution.py:55
  342.1 13.6 collective-permute-start.38
  372.8 36.8 %collective-permute-done.37 = bf16[2,384,512]{1,2,0:T(8,128)(2,1)S(1)} collective-permute-done((bf16[2,384,512]{1,2,0:T(8,128)(2,1)S(1)}, bf16[2,384,512]{1,2,0:T(8,128)(2,1)S(1)}, u32[]{:S(2)}, u32[]{:S(2)}) %collective-permute-start.37) | collective-permute-done | bytes 786464 | tf_op jit(solution)/shard_map/ppermute | solution.py:55
  428.6 18.0 %collective-permute-done.52 = bf16[2,384,512]{1,2,0:T(8,128)(2,1)S(1)} collective-permute-done((bf16[2,384,512]{1,2,0:T(8,128)(2,1)S(1)}, bf16[2,384,512]{1,2,0:T(8,128)(2,1)S(1)}, u32[]{:S(2)}, u32[]{:S(2)}) %collective-permute-start.52) | collective-permute-done | bytes 786464 | tf_op jit(solution)/shard_map/ppermute | solution.py:55
  452.1 23.2 %collective-permute-done.53 = bf16[2,384,512]{1,2,0:T(8,128)(2,1)S(1)} collective-permute-done((bf16[2,384,512]{1,2,0:T(8,128)(2,1)S(1)}, bf16[2,384,512]{1,2,0:T(8,128)(2,1)S(1)}, u32[]{:S(2)}, u32[]{:S(2)}) %collective-permute-start.53) | collective-permute-done | bytes 786464 | tf_op jit(solution)/shard_map/ppermute | solution.py:55
  494.6 18.0 %collective-permute-done.41 = bf16[2,384,512]{1,2,0:T(8,128)(2,1)S(1)} collective-permute-done((bf16[2,384,512]{1,2,0:T(8,128)(2,1)S(1)}, bf16[2,384,512]{1,2,0:T(8,128)(2,1)S(1)}, u32[]{:S(2)}, u32[]{:S(2)}) %collective-permute-start.41) | collective-permute-done | bytes 786464 | tf_op jit(solution)/shard_map/ppermute | solution.py:55
  513.5 16.0 %collective-permute-done.42 = bf16[2,384,512]{1,2,0:T(8,128)(2,1)S(1)} collective-permute-done((bf16[2,384,512]{1,2,0:T(8,128)(2,1)S(1)}, bf16[2,384,512]{1,2,0:T(8,128)(2,1)S(1)}, u32[]{:S(2)}, u32[]{:S(2)}) %collective-permute-start.42) | collective-permute-done | bytes 786464 | tf_op jit(solution)/shard_map/ppermute | solution.py:55
  530.3 16.0 %collective-permute-done.43 = bf16[2,384,512]{1,2,0:T(8,128)(2,1)S(1)} collective-permute-done((bf16[2,384,512]{1,2,0:T(8,128)(2,1)S(1)}, bf16[2,384,512]{1,2,0:T(8,128)(2,1)S(1)}, u32[]{:S(2)}, u32[]{:S(2)}) %collective-permute-start.43) | collective-permute-done | bytes 786464 | tf_op jit(solution)/shard_map/ppermute | solution.py:55
  547.1 16.0 %collective-permute-done.56 = bf16[2,384,512]{1,2,0:T(8,128)(2,1)S(1)} collective-permute-done((bf16[2,384,512]{1,2,0:T(8,128)(2,1)S(1)}, bf16[2,384,512]{1,2,0:T(8,128)(2,1)S(1)}, u32[]{:S(2)}, u32[]{:S(2)}) %collective-permute-start.56) | collective-permute-done | bytes 786464 | tf_op jit(solution)/shard_map/ppermute | solution.py:55
  564.1 16.0 %collective-permute-done.57 = bf16[2,384,512]{1,2,0:T(8,128)(2,1)S(1)} collective-permute-done((bf16[2,384,512]{1,2,0:T(8,128)(2,1)S(1)}, bf16[2,384,512]{1,2,0:T(8,128)(2,1)S(1)}, u32[]{:S(2)}, u32[]{:S(2)}) %collective-permute-start.57) | collective-permute-done | bytes 786464 | tf_op jit(solution)/shard_map/ppermute | solution.py:55
  580.9 14.1 %collective-permute-done.58 = bf16[2,384,512]{1,2,0:T(8,128)(2,1)S(1)} collective-permute-done((bf16[2,384,512]{1,2,0:T(8,128)(2,1)S(1)}, bf16[2,384,512]{1,2,0:T(8,128)(2,1)S(1)}, u32[]{:S(2)}, u32[]{:S(2)}) %collective-permute-start.58) | collective-permute-done | bytes 786464 | tf_op jit(solution)/shard_map/ppermute | solution.py:55
  751.4 13.7 collective-permute-done.126
  787.2 14.8 %collective-permute-done.83 = bf16[128,3072]{1,0:T(8,128)(2,1)S(1)} collective-permute-done((bf16[128,3072]{1,0:T(8,128)(2,1)S(1)}, bf16[128,3072]{1,0:T(8,128)(2,1)S(1)}, u32[]{:S(2)}, u32[]{:S(2)}) %collective-permute-start.83) | collective-permute-done | bytes 786464 | tf_op jit(solution)/shard_map/ppermute | solution.py:62
  818.2 14.2 %collective-permute-done.130 = bf16[2,384,512]{1,2,0:T(8,128)(2,1)S(1)} collective-permute-done((bf16[2,384,512]{1,2,0:T(8,128)(2,1)S(1)}, bf16[2,384,512]{1,2,0:T(8,128)(2,1)S(1)}, u32[]{:S(2)}, u32[]{:S(2)}) %collective-permute-start.130) | collective-permute-done | bytes 786464 | tf_op jit(solution)/shard_map/ppermute | solution.py:55
  832.4 16.8 %collective-permute-done.125 = bf16[2,384,512]{1,2,0:T(8,128)(2,1)S(1)} collective-permute-done((bf16[2,384,512]{1,2,0:T(8,128)(2,1)}, bf16[2,384,512]{1,2,0:T(8,128)(2,1)S(1)}, u32[]{:S(2)}, u32[]{:S(2)}) %collective-permute-start.125) | collective-permute-done | bytes 786464 | tf_op jit(solution)/shard_map/ppermute | solution.py:55
  849.3 16.8 %collective-permute-done.132 = bf16[2,384,512]{1,2,0:T(8,128)(2,1)S(1)} collective-permute-done((bf16[2,384,512]{1,2,0:T(8,128)(2,1)S(1)}, bf16[2,384,512]{1,2,0:T(8,128)(2,1)S(1)}, u32[]{:S(2)}, u32[]{:S(2)}) %collective-permute-start.132) | collective-permute-done | bytes 786464 | tf_op jit(solution)/shard_map/ppermute | solution.py:55
  866.2 16.4 %collective-permute-done.134 = bf16[2,384,512]{1,2,0:T(8,128)(2,1)S(1)} collective-permute-done((bf16[2,384,512]{1,2,0:T(8,128)(2,1)S(1)}, bf16[2,384,512]{1,2,0:T(8,128)(2,1)S(1)}, u32[]{:S(2)}, u32[]{:S(2)}) %collective-permute-start.134) | collective-permute-done | bytes 786464 | tf_op jit(solution)/shard_map/ppermute | solution.py:55
  890.3 28.1 %collective-permute-done.140 = bf16[1024,384]{1,0:T(8,128)(2,1)} collective-permute-done((bf16[1024,384]{1,0:T(8,128)(2,1)}, bf16[1024,384]{1,0:T(8,128)(2,1)}, u32[]{:S(2)}, u32[]{:S(2)}) %collective-permute-start.140) | collective-permute-done | bytes 786464 | tf_op jit(solution)/shard_map/ppermute | solution.py:55
  918.9 18.2 %collective-permute-start.70 = (bf16[128,3072]{1,0:T(8,128)(2,1)}, bf16[128,3072]{1,0:T(8,128)(2,1)S(1)}, u32[]{:S(2)}, u32[]{:S(2)}) collective-permute-start(bf16[128,3072]{1,0:T(8,128)(2,1)} %copy-done.94), channel_id=1, source_target_pairs={{0,8},{1,9},{2,10},{3,11},{4,12},{5,13},{6,14},{7,15},{8,0},{9,1},... | collective-permute-start | bytes 2359304 | tf_op jit(solution)/shard_map/ppermute | solution.py:55
  937.2 16.0 %collective-permute-done.127 = bf16[2,384,512]{1,2,0:T(8,128)(2,1)} collective-permute-done((bf16[2,384,512]{1,2,0:T(8,128)(2,1)}, bf16[2,384,512]{1,2,0:T(8,128)(2,1)}, u32[]{:S(2)}, u32[]{:S(2)}) %collective-permute-start.127) | collective-permute-done | bytes 786464 | tf_op jit(solution)/shard_map/ppermute | solution.py:55
  971.2 15.6 %collective-permute-done.84 = bf16[128,3072]{1,0:T(8,128)(2,1)S(1)} collective-permute-done((bf16[128,3072]{1,0:T(8,128)(2,1)}, bf16[128,3072]{1,0:T(8,128)(2,1)S(1)}, u32[]{:S(2)}, u32[]{:S(2)}) %collective-permute-start.84) | collective-permute-done | bytes 786464 | tf_op jit(solution)/shard_map/ppermute | solution.py:55
  993.2 27.3 %collective-permute-done.129 = bf16[2,384,512]{1,2,0:T(8,128)(2,1)S(1)} collective-permute-done((bf16[2,384,512]{1,2,0:T(8,128)(2,1)}, bf16[2,384,512]{1,2,0:T(8,128)(2,1)S(1)}, u32[]{:S(2)}, u32[]{:S(2)}) %collective-permute-start.129) | collective-permute-done | bytes 786464 | tf_op jit(solution)/shard_map/ppermute | solution.py:55
  1021.2 32.9 %collective-permute-done.133 = bf16[2,384,512]{1,2,0:T(8,128)(2,1)S(1)} collective-permute-done((bf16[2,384,512]{1,2,0:T(8,128)(2,1)}, bf16[2,384,512]{1,2,0:T(8,128)(2,1)S(1)}, u32[]{:S(2)}, u32[]{:S(2)}) %collective-permute-start.133) | collective-permute-done | bytes 786464 | tf_op jit(solution)/shard_map/ppermute | solution.py:55
  1079.1 19.4 %collective-permute-done.88 = bf16[128,3072]{1,0:T(8,128)(2,1)} collective-permute-done((bf16[128,3072]{1,0:T(8,128)(2,1)}, bf16[128,3072]{1,0:T(8,128)(2,1)}, u32[]{:S(2)}, u32[]{:S(2)}) %collective-permute-start.88) | collective-permute-done | bytes 786464 | tf_op jit(solution)/shard_map/ppermute | solution.py:55
  1247.1 14.5 %collective-permute-done.111 = bf16[3,384,384]{1,2,0:T(8,128)(2,1)S(1)} collective-permute-done((bf16[3,384,384]{1,2,0:T(8,128)(2,1)S(1)}, bf16[3,384,384]{1,2,0:T(8,128)(2,1)S(1)}, u32[]{:S(2)}, u32[]{:S(2)}) %collective-permute-start.111) | collective-permute-done | bytes 884768 | tf_op jit(solution)/shard_map/ppermute | solution.py:55
  1261.7 19.0 %collective-permute-done.113 = bf16[3,384,384]{1,2,0:T(8,128)(2,1)S(1)} collective-permute-done((bf16[3,384,384]{1,2,0:T(8,128)(2,1)S(1)}, bf16[3,384,384]{1,2,0:T(8,128)(2,1)S(1)}, u32[]{:S(2)}, u32[]{:S(2)}) %collective-permute-start.113) | collective-permute-done | bytes 884768 | tf_op jit(solution)/shard_map/ppermute | solution.py:55
  1299.7 24.2 %collective-permute-done.110 = bf16[3,384,384]{1,2,0:T(8,128)(2,1)S(1)} collective-permute-done((bf16[3,384,384]{1,2,0:T(8,128)(2,1)S(1)}, bf16[3,384,384]{1,2,0:T(8,128)(2,1)S(1)}, u32[]{:S(2)}, u32[]{:S(2)}) %collective-permute-start.110) | collective-permute-done | bytes 884768 | tf_op jit(solution)/shard_map/ppermute | solution.py:55
  1325.0 17.9 %collective-permute-done.114 = bf16[3,384,384]{1,2,0:T(8,128)(2,1)S(1)} collective-permute-done((bf16[3,384,384]{1,2,0:T(8,128)(2,1)S(1)}, bf16[3,384,384]{1,2,0:T(8,128)(2,1)S(1)}, u32[]{:S(2)}, u32[]{:S(2)}) %collective-permute-start.114) | collective-permute-done | bytes 884768 | tf_op jit(solution)/shard_map/ppermute | solution.py:55
  (782 shorter events, 774.7 us)
Async XLA Ops:
  8.2 59.5 %collective-permute-start.10 = (bf16[2,384]{1,0:T(2,128)(2,1)}, bf16[2,384]{1,0:T(2,128)(2,1)}, u32[]{:S(2)}, u32[]{:S(2)}) collective-permute-start(bf16[2,384]{1,0:T(2,128)(2,1)} %get-tuple-element.58), channel_id=1, source_target_pairs={{0,4},{1,5},{2,6},{3,7},{4,0},{5,1},{6,2},{7,3},{8,12},{9,13},{10,... | collective-permute-start | bytes 4616 | tf_op jit(solution)/shard_map/ppermute | solution.py:55
  65.0 66.6 %collective-permute-start.1 = (bf16[3,384,384]{1,2,0:T(8,128)(2,1)}, bf16[3,384,384]{1,2,0:T(8,128)(2,1)S(1)}, u32[]{:S(2)}, u32[]{:S(2)}) collective-permute-start(bf16[3,384,384]{1,2,0:T(8,128)(2,1)} %copy-done.15), channel_id=1, source_target_pairs={{0,16},{1,17},{2,18},{3,19},{4,20},{5,21},{6,22},{7,23},{8,24},{9,... | collective-permute-start | bytes 2654216 | tf_op jit(solution)/shard_map/ppermute | solution.py:55
  69.9 60.6 %collective-permute-start = (bf16[3,384,384]{1,2,0:T(8,128)(2,1)}, bf16[3,384,384]{1,2,0:T(8,128)(2,1)S(1)}, u32[]{:S(2)}, u32[]{:S(2)}) collective-permute-start(bf16[3,384,384]{1,2,0:T(8,128)(2,1)} %copy.121), channel_id=1, source_target_pairs={{0,8},{1,9},{2,10},{3,11},{4,12},{5,13},{6,14},{7,15},{8,0},{9,1},... | collective-permute-start | bytes 2654216 | tf_op jit(solution)/shard_map/ppermute | solution.py:55
  105.4 72.7 %collective-permute-start.74 = (bf16[128,3072]{1,0:T(8,128)(2,1)S(1)}, bf16[128,3072]{1,0:T(8,128)(2,1)S(1)}, u32[]{:S(2)}, u32[]{:S(2)}) collective-permute-start(bf16[128,3072]{1,0:T(8,128)(2,1)S(1)} %copy-done.93), channel_id=1, source_target_pairs={{0,8},{1,9},{2,10},{3,11},{4,12},{5,13},{6,14},{7,15},{8,0},{9,1},... | collective-permute-start | bytes 2359304 | tf_op jit(solution)/shard_map/ppermute | solution.py:55
  130.5 70.9 %collective-permute-start.17 = (bf16[128,3072]{1,0:T(8,128)(2,1)S(1)}, bf16[128,3072]{1,0:T(8,128)(2,1)S(1)}, u32[]{:S(2)}, u32[]{:S(2)}) collective-permute-start(bf16[128,3072]{1,0:T(8,128)(2,1)S(1)} %constant_dynamic-update-slice_fusion.24), channel_id=1, source_target_pairs={{0,8},{1,9},{2,10},{3,11},{4,12},{5,13},{6,14},{7,15},{8,0},{9,1},... | collective-permute-start | bytes 2359304 | tf_op jit(solution)/shard_map/ppermute | solution.py:55
  131.7 73.6 %collective-permute-start.73 = (bf16[128,3072]{1,0:T(8,128)(2,1)S(1)}, bf16[128,3072]{1,0:T(8,128)(2,1)S(1)}, u32[]{:S(2)}, u32[]{:S(2)}) collective-permute-start(bf16[128,3072]{1,0:T(8,128)(2,1)S(1)} %collective-permute-done.72), channel_id=1, source_target_pairs={{0,1},{1,0},{2,3},{3,2},{4,5},{5,4},{6,7},{7,6},{8,9},{9,8},{10,11... | collective-permute-start | bytes 2359304 | tf_op jit(solution)/shard_map/ppermute | solution.py:62
  267.5 70.6 %collective-permute-start.60 = (bf16[1024,384]{1,0:T(8,128)(2,1)}, bf16[1024,384]{1,0:T(8,128)(2,1)}, u32[]{:S(2)}, u32[]{:S(2)}) collective-permute-start(bf16[1024,384]{1,0:T(8,128)(2,1)} %get-tuple-element.23), channel_id=1, source_target_pairs={{0,4},{1,5},{2,6},{3,7},{4,0},{5,1},{6,2},{7,3},{8,12},{9,13},{10,... | collective-permute-start | bytes 2359304 | tf_op jit(solution)/shard_map/ppermute | solution.py:55
  268.6 69.6 %collective-permute-start.77 = (bf16[128,3072]{1,0:T(8,128)(2,1)}, bf16[128,3072]{1,0:T(8,128)(2,1)}, u32[]{:S(2)}, u32[]{:S(2)}) collective-permute-start(bf16[128,3072]{1,0:T(8,128)(2,1)} %collective-permute-done.76), channel_id=1, source_target_pairs={{0,1},{1,0},{2,3},{3,2},{4,5},{5,4},{6,7},{7,6},{8,9},{9,8},{10,11... | collective-permute-start | bytes 2359304 | tf_op jit(solution)/shard_map/ppermute | solution.py:62
  288.5 68.6 %collective-permute-start.62 = (bf16[1024,384]{1,0:T(8,128)(2,1)}, bf16[1024,384]{1,0:T(8,128)(2,1)}, u32[]{:S(2)}, u32[]{:S(2)}) collective-permute-start(bf16[1024,384]{1,0:T(8,128)(2,1)} %collective-permute-done.59), channel_id=1, source_target_pairs={{0,4},{1,5},{2,6},{3,7},{4,0},{5,1},{6,2},{7,3},{8,12},{9,13},{10,... | collective-permute-start | bytes 2359304 | tf_op jit(solution)/shard_map/ppermute | solution.py:55
  291.1 67.5 %collective-permute-start.63 = (bf16[1024,384]{1,0:T(8,128)(2,1)}, bf16[1024,384]{1,0:T(8,128)(2,1)}, u32[]{:S(2)}, u32[]{:S(2)}) collective-permute-start(bf16[1024,384]{1,0:T(8,128)(2,1)} %collective-permute-done.51), channel_id=1, source_target_pairs={{0,4},{1,5},{2,6},{3,7},{4,0},{5,1},{6,2},{7,3},{8,12},{9,13},{10,... | collective-permute-start | bytes 2359304 | tf_op jit(solution)/shard_map/ppermute | solution.py:55
  342.1 70.2 %collective-permute-start.38 = (bf16[2,384,512]{1,2,0:T(8,128)(2,1)S(1)}, bf16[2,384,512]{1,2,0:T(8,128)(2,1)S(1)}, u32[]{:S(2)}, u32[]{:S(2)}) collective-permute-start(bf16[2,384,512]{1,2,0:T(8,128)(2,1)S(1)} %copy-done.21), channel_id=1, source_target_pairs={{0,16},{1,17},{2,18},{3,19},{4,20},{5,21},{6,22},{7,23},{8,24},{9,... | collective-permute-start | bytes 2359304 | tf_op jit(solution)/shard_map/ppermute | solution.py:55
  411.7 63.6 %collective-permute-start.53 = (bf16[2,384,512]{1,2,0:T(8,128)(2,1)S(1)}, bf16[2,384,512]{1,2,0:T(8,128)(2,1)S(1)}, u32[]{:S(2)}, u32[]{:S(2)}) collective-permute-start(bf16[2,384,512]{1,2,0:T(8,128)(2,1)S(1)} %copy-done.19), channel_id=1, source_target_pairs={{0,16},{1,17},{2,18},{3,19},{4,20},{5,21},{6,22},{7,23},{8,24},{9,... | collective-permute-start | bytes 2359304 | tf_op jit(solution)/shard_map/ppermute | solution.py:55
  412.3 64.0 %collective-permute-start.54 = (bf16[2,384,512]{1,2,0:T(8,128)(2,1)S(1)}, bf16[2,384,512]{1,2,0:T(8,128)(2,1)S(1)}, u32[]{:S(2)}, u32[]{:S(2)}) collective-permute-start(bf16[2,384,512]{1,2,0:T(8,128)(2,1)S(1)} %copy-done.46), channel_id=1, source_target_pairs={{0,24},{1,25},{2,26},{3,27},{4,28},{5,29},{6,30},{7,31},{8,16},{9,... | collective-permute-start | bytes 2359304 | tf_op jit(solution)/shard_map/ppermute | solution.py:55
  416.7 61.1 %collective-permute-start.29 = (bf16[128,3072]{1,0:T(8,128)(2,1)S(1)}, bf16[128,3072]{1,0:T(8,128)(2,1)S(1)}, u32[]{:S(2)}, u32[]{:S(2)}) collective-permute-start(bf16[128,3072]{1,0:T(8,128)(2,1)S(1)} %get-tuple-element.99), channel_id=1, source_target_pairs={{0,1},{1,0},{2,3},{3,2},{4,5},{5,4},{6,7},{7,6},{8,9},{9,8},{10,11... | collective-permute-start | bytes 2359304 | tf_op jit(solution)/shard_map/ppermute | solution.py:62
  475.3 71.5 %collective-permute-start.55 = (bf16[2,384,512]{1,2,0:T(8,128)(2,1)S(1)}, bf16[2,384,512]{1,2,0:T(8,128)(2,1)S(1)}, u32[]{:S(2)}, u32[]{:S(2)}) collective-permute-start(bf16[2,384,512]{1,2,0:T(8,128)(2,1)S(1)} %copy-done.19), channel_id=1, source_target_pairs={{0,4},{1,5},{2,6},{3,7},{4,0},{5,1},{6,2},{7,3},{8,12},{9,13},{10,... | collective-permute-start | bytes 2359304 | tf_op jit(solution)/shard_map/ppermute | solution.py:55
  478.8 67.5 %collective-permute-start.43 = (bf16[2,384,512]{1,2,0:T(8,128)(2,1)S(1)}, bf16[2,384,512]{1,2,0:T(8,128)(2,1)S(1)}, u32[]{:S(2)}, u32[]{:S(2)}) collective-permute-start(bf16[2,384,512]{1,2,0:T(8,128)(2,1)S(1)} %collective-permute-done.39), channel_id=1, source_target_pairs={{0,4},{1,5},{2,6},{3,7},{4,0},{5,1},{6,2},{7,3},{8,12},{9,13},{10,... | collective-permute-start | bytes 2359304 | tf_op jit(solution)/shard_map/ppermute | solution.py:55
  491.6 71.5 %collective-permute-start.56 = (bf16[2,384,512]{1,2,0:T(8,128)(2,1)S(1)}, bf16[2,384,512]{1,2,0:T(8,128)(2,1)S(1)}, u32[]{:S(2)}, u32[]{:S(2)}) collective-permute-start(bf16[2,384,512]{1,2,0:T(8,128)(2,1)S(1)} %collective-permute-done.52), channel_id=1, source_target_pairs={{0,4},{1,5},{2,6},{3,7},{4,0},{5,1},{6,2},{7,3},{8,12},{9,13},{10,... | collective-permute-start | bytes 2359304 | tf_op jit(solution)/shard_map/ppermute | solution.py:55
  512.6 67.4 %collective-permute-start.57 = (bf16[2,384,512]{1,2,0:T(8,128)(2,1)S(1)}, bf16[2,384,512]{1,2,0:T(8,128)(2,1)S(1)}, u32[]{:S(2)}, u32[]{:S(2)}) collective-permute-start(bf16[2,384,512]{1,2,0:T(8,128)(2,1)S(1)} %collective-permute-done.53), channel_id=1, source_target_pairs={{0,4},{1,5},{2,6},{3,7},{4,0},{5,1},{6,2},{7,3},{8,12},{9,13},{10,... | collective-permute-start | bytes 2359304 | tf_op jit(solution)/shard_map/ppermute | solution.py:55
  529.5 65.6 %collective-permute-start.58 = (bf16[2,384,512]{1,2,0:T(8,128)(2,1)S(1)}, bf16[2,384,512]{1,2,0:T(8,128)(2,1)S(1)}, u32[]{:S(2)}, u32[]{:S(2)}) collective-permute-start(bf16[2,384,512]{1,2,0:T(8,128)(2,1)S(1)} %collective-permute-done.54), channel_id=1, source_target_pairs={{0,4},{1,5},{2,6},{3,7},{4,0},{5,1},{6,2},{7,3},{8,12},{9,13},{10,... | collective-permute-start | bytes 2359304 | tf_op jit(solution)/shard_map/ppermute | solution.py:55
  733.7 70.9 %collective-permute-start.136 = (bf16[1024,384]{1,0:T(8,128)(2,1)}, bf16[1024,384]{1,0:T(8,128)(2,1)}, u32[]{:S(2)}, u32[]{:S(2)}) collective-permute-start(bf16[1024,384]{1,0:T(8,128)(2,1)} %get-tuple-element.117), channel_id=1, source_target_pairs={{0,4},{1,5},{2,6},{3,7},{4,0},{5,1},{6,2},{7,3},{8,12},{9,13},{10,... | collective-permute-start | bytes 2359304 | tf_op jit(solution)/shard_map/ppermute | solution.py:55
  804.6 61.5 %collective-permute-start.132 = (bf16[2,384,512]{1,2,0:T(8,128)(2,1)S(1)}, bf16[2,384,512]{1,2,0:T(8,128)(2,1)S(1)}, u32[]{:S(2)}, u32[]{:S(2)}) collective-permute-start(bf16[2,384,512]{1,2,0:T(8,128)(2,1)S(1)} %copy-done.52), channel_id=1, source_target_pairs={{0,4},{1,5},{2,6},{3,7},{4,0},{5,1},{6,2},{7,3},{8,12},{9,13},{10,... | collective-permute-start | bytes 2359304 | tf_op jit(solution)/shard_map/ppermute | solution.py:55
  805.8 76.8 %collective-permute-start.134 = (bf16[2,384,512]{1,2,0:T(8,128)(2,1)S(1)}, bf16[2,384,512]{1,2,0:T(8,128)(2,1)S(1)}, u32[]{:S(2)}, u32[]{:S(2)}) collective-permute-start(bf16[2,384,512]{1,2,0:T(8,128)(2,1)S(1)} %get-tuple-element.126), channel_id=1, source_target_pairs={{0,4},{1,5},{2,6},{3,7},{4,0},{5,1},{6,2},{7,3},{8,12},{9,13},{10,... | collective-permute-start | bytes 2359304 | tf_op jit(solution)/shard_map/ppermute | solution.py:55
  815.6 67.8 %collective-permute-start.124 = (bf16[2,384,512]{1,2,0:T(8,128)(2,1)S(1)}, bf16[2,384,512]{1,2,0:T(8,128)(2,1)S(1)}, u32[]{:S(2)}, u32[]{:S(2)}) collective-permute-start(bf16[2,384,512]{1,2,0:T(8,128)(2,1)S(1)} %copy-done.61), channel_id=1, source_target_pairs={{0,16},{1,17},{2,18},{3,19},{4,20},{5,21},{6,22},{7,23},{8,24},{9,... | collective-permute-start | bytes 2359304 | tf_op jit(solution)/shard_map/ppermute | solution.py:55
  883.4 69.8 %collective-permute-start.127 = (bf16[2,384,512]{1,2,0:T(8,128)(2,1)}, bf16[2,384,512]{1,2,0:T(8,128)(2,1)}, u32[]{:S(2)}, u32[]{:S(2)}) collective-permute-start(bf16[2,384,512]{1,2,0:T(8,128)(2,1)} %fusion.58), channel_id=1, source_target_pairs={{0,16},{1,17},{2,18},{3,19},{4,20},{5,21},{6,22},{7,23},{8,24},{9,... | collective-permute-start | bytes 2359304 | tf_op jit(solution)/shard_map/ppermute | solution.py:55
  889.6 71.8 %collective-permute-start.78 = (bf16[128,3072]{1,0:T(8,128)(2,1)S(1)}, bf16[128,3072]{1,0:T(8,128)(2,1)S(1)}, u32[]{:S(2)}, u32[]{:S(2)}) collective-permute-start(bf16[128,3072]{1,0:T(8,128)(2,1)S(1)} %copy-done.48), channel_id=1, source_target_pairs={{0,1},{1,0},{2,3},{3,2},{4,5},{5,4},{6,7},{7,6},{8,9},{9,8},{10,11... | collective-permute-start | bytes 2359304 | tf_op jit(solution)/shard_map/ppermute | solution.py:62
  889.7 73.7 %collective-permute-start.66 = (bf16[128,3072]{1,0:T(8,128)(2,1)S(1)}, bf16[128,3072]{1,0:T(8,128)(2,1)S(1)}, u32[]{:S(2)}, u32[]{:S(2)}) collective-permute-start(bf16[128,3072]{1,0:T(8,128)(2,1)S(1)} %copy-done.49), channel_id=1, source_target_pairs={{0,2},{1,3},{2,0},{3,1},{4,6},{5,7},{6,4},{7,5},{8,10},{9,11},{10,... | collective-permute-start | bytes 2359304 | tf_op jit(solution)/shard_map/ppermute | solution.py:62
  961.4 59.1 %collective-permute-start.129 = (bf16[2,384,512]{1,2,0:T(8,128)(2,1)}, bf16[2,384,512]{1,2,0:T(8,128)(2,1)S(1)}, u32[]{:S(2)}, u32[]{:S(2)}) collective-permute-start(bf16[2,384,512]{1,2,0:T(8,128)(2,1)} %get-tuple-element.77), channel_id=1, source_target_pairs={{0,8},{1,9},{2,10},{3,11},{4,12},{5,13},{6,14},{7,15},{8,0},{9,1},... | collective-permute-start | bytes 2359304 | tf_op jit(solution)/shard_map/ppermute | solution.py:55
  964.7 89.4 %collective-permute-start.133 = (bf16[2,384,512]{1,2,0:T(8,128)(2,1)}, bf16[2,384,512]{1,2,0:T(8,128)(2,1)S(1)}, u32[]{:S(2)}, u32[]{:S(2)}) collective-permute-start(bf16[2,384,512]{1,2,0:T(8,128)(2,1)} %get-tuple-element.80), channel_id=1, source_target_pairs={{0,8},{1,9},{2,10},{3,11},{4,12},{5,13},{6,14},{7,15},{8,0},{9,1},... | collective-permute-start | bytes 2359304 | tf_op jit(solution)/shard_map/ppermute | solution.py:55
  969.9 84.2 %collective-permute-start.135 = (bf16[2,384,512]{1,2,0:T(8,128)(2,1)}, bf16[2,384,512]{1,2,0:T(8,128)(2,1)S(1)}, u32[]{:S(2)}, u32[]{:S(2)}) collective-permute-start(bf16[2,384,512]{1,2,0:T(8,128)(2,1)} %get-tuple-element.79), channel_id=1, source_target_pairs={{0,24},{1,25},{2,26},{3,27},{4,28},{5,29},{6,30},{7,31},{8,16},{9,... | collective-permute-start | bytes 2359304 | tf_op jit(solution)/shard_map/ppermute | solution.py:55
  991.7 108.6 %collective-permute-start.85 = (bf16[128,3072]{1,0:T(8,128)(2,1)}, bf16[128,3072]{1,0:T(8,128)(2,1)}, u32[]{:S(2)}, u32[]{:S(2)}) collective-permute-start(bf16[128,3072]{1,0:T(8,128)(2,1)} %get-tuple-element.47), channel_id=1, source_target_pairs={{0,1},{1,0},{2,3},{3,2},{4,5},{5,4},{6,7},{7,6},{8,9},{9,8},{10,11... | collective-permute-start | bytes 2359304 | tf_op jit(solution)/shard_map/ppermute | solution.py:62
  1261.7 89.2 %collective-permute-start.92 = (bf16[128,3072]{1,0:T(8,128)(2,1)}, bf16[128,3072]{1,0:T(8,128)(2,1)S(1)}, u32[]{:S(2)}, u32[]{:S(2)}) collective-permute-start(bf16[128,3072]{1,0:T(8,128)(2,1)} %get-tuple-element.81), channel_id=1, source_target_pairs={{0,1},{1,0},{2,3},{3,2},{4,5},{5,4},{6,7},{7,6},{8,9},{9,8},{10,11... | collective-permute-start | bytes 2359304 | tf_op jit(solution)/shard_map/ppermute | solution.py:62
  1283.2 59.7 %collective-permute-start.114 = (bf16[3,384,384]{1,2,0:T(8,128)(2,1)S(1)}, bf16[3,384,384]{1,2,0:T(8,128)(2,1)S(1)}, u32[]{:S(2)}, u32[]{:S(2)}) collective-permute-start(bf16[3,384,384]{1,2,0:T(8,128)(2,1)S(1)} %get-tuple-element.68), channel_id=1, source_target_pairs={{0,24},{1,25},{2,26},{3,27},{4,28},{5,29},{6,30},{7,31},{8,16},{9,... | collective-permute-start | bytes 2654216 | tf_op jit(solution)/shard_map/ppermute | solution.py:55
  (216 other events, 6468.1 us)

commit v2 on v1

v2 whole, which is shorter than its diff:
```python
import math

import jax
import jax.numpy as jnp
from jax import lax
from jax.experimental import pallas as pl
from jax.experimental.pallas import tpu as pltpu
from jax.sharding import PartitionSpec as P

HEAD_DIM = 96
NORM_EPS = 1e-05
ROPE_BASE = 10000.0
AXES = ("dp", "tensor")
PAIR = 2
NEAR = 1
NEGATIVE = -1e30

bf16 = jnp.bfloat16
f32 = jnp.float32


def rms_unit(values):
    scale_inv = lax.rsqrt(jnp.mean(values * values, axis=1, keepdims=True) + NORM_EPS)
    return (values * scale_inv, scale_inv)


def norm_back(grad_normed, gain, unit, scale_inv):
    grad_unit = grad_normed * gain
    return scale_inv * (grad_unit - unit * jnp.mean(grad_unit * unit, axis=1, keepdims=True))


def mix(form, left, right):
    return jnp.einsum(form, left, right, preferred_element_type=f32)


def held_until(value, *waited):
    return lax.optimization_barrier((value, waited))[0]


def dot_last(a, b):
    return lax.dot_general(a, b, (((1,), (1,)), ((), ())), preferred_element_type=f32)


def dot_first(a, b):
    return lax.dot_general(a, b, (((0,), (0,)), ((), ())), preferred_element_type=f32)


def turned(u, low):
    width = u.shape[1]
    half = HEAD_DIM // 2
    return jnp.where(low, pltpu.roll(u, width - half, 1), pltpu.roll(u, half, 1))


def low_lanes(shape):
    lane = lax.broadcasted_iota(jnp.int32, shape, 1)
    low = lane < 0
    for h in range(shape[1] // HEAD_DIM):
        low = low | ((lane >= h * HEAD_DIM) & (lane < h * HEAD_DIM + HEAD_DIM // 2))
    return low


def group_block(ref):
    v = ref[...]
    return v.reshape(v.shape[0] * v.shape[2], v.shape[3])


def put_block(ref, v):
    ref[...] = v.reshape(ref.shape)


def masked_scores(qh, kh, allowed):
    return jnp.where(allowed, dot_last(qh, kh) * (1.0 / math.sqrt(HEAD_DIM)), NEGATIVE)


def allowed_pairs(rows_ref, cols_ref, length):
    rp, cp = rows_ref[...], cols_ref[...]
    return (cp <= rp) & ((rp < length) == (cp < length))


def attend_kernel(len_ref, rows_ref, cols_ref, cos_ref, sin_ref, q_ref, k_ref, v_ref,
                  o_ref, qo_ref, ko_ref, vo_ref, lse_ref):
    allowed = allowed_pairs(rows_ref, cols_ref, len_ref[pl.program_id(0)])
    cosine, sine = cos_ref[...], sin_ref[...]
    low = low_lanes(cosine.shape)
    q, k = group_block(q_ref), group_block(k_ref)
    q = q * cosine + turned(q, low) * sine
    k = k * cosine + turned(k, low) * sine
    v = group_block(v_ref)
    put_block(qo_ref, q.astype(bf16))
    put_block(ko_ref, k.astype(bf16))
    put_block(vo_ref, v.astype(bf16))
    outs, totals = [], []
    for h in range(q.shape[1] // HEAD_DIM):
        c = slice(h * HEAD_DIM, (h + 1) * HEAD_DIM)
        s = masked_scores(q[:, c].astype(bf16), k[:, c].astype(bf16), allowed)
        top = jnp.max(s, axis=1, keepdims=True)
        e = jnp.exp(s - top)
        total = jnp.sum(e, axis=1, keepdims=True)
        prob = (e * (1.0 / total)).astype(bf16)
        outs.append(jnp.dot(prob, v[:, c].astype(bf16), preferred_element_type=f32))
        totals.append(top + jnp.log(total))
    put_block(o_ref, jnp.concatenate(outs, axis=1).astype(bf16))
    put_block(lse_ref, jnp.concatenate(totals, axis=1))


def attend_back_kernel(len_ref, rows_ref, cols_ref, cos_ref, sin_ref, q_ref, k_ref, v_ref, o_ref, g_ref, lse_ref,
                       dq_ref, dk_ref, dv_ref):
    allowed = allowed_pairs(rows_ref, cols_ref, len_ref[pl.program_id(0)])
    q, k, v, g = (group_block(r).astype(f32) for r in (q_ref, k_ref, v_ref, g_ref))
    go = g * group_block(o_ref).astype(f32)
    totals = group_block(lse_ref)
    dqs, dks, dvs = [], [], []
    for h in range(q.shape[1] // HEAD_DIM):
        c = slice(h * HEAD_DIM, (h + 1) * HEAD_DIM)
        qh, kh, vh, gh = (u[:, c].astype(bf16) for u in (q, k, v, g))
        delta = jnp.sum(go[:, c], axis=1, keepdims=True)
        prob = jnp.exp(masked_scores(qh, kh, allowed) - totals[:, h : h + 1])
        ds = (prob * (dot_last(gh, vh) - delta) * (1.0 / math.sqrt(HEAD_DIM))).astype(bf16)
        dqs.append(jnp.dot(ds, kh, preferred_element_type=f32))
        dks.append(dot_first(ds, qh))
        dvs.append(dot_first(prob.astype(bf16), gh))
    cosine, sine = cos_ref[...], sin_ref[...]
    low = low_lanes(cosine.shape)
    for ref, parts in ((dq_ref, dqs), (dk_ref, dks)):
        u = jnp.concatenate(parts, axis=1)
        put_block(ref, (u * cosine - turned(u, low) * sine).astype(bf16))
    put_block(dv_ref, jnp.concatenate(dvs, axis=1).astype(bf16))


def _specs(group_rows, cols, lanes):
    tall = pl.BlockSpec((2, 1, group_rows // 2, cols), lambda g: (0, g, 0, 0))
    table = pl.BlockSpec((group_rows, cols), lambda g: (0, 0))
    head = [
        pl.BlockSpec(memory_space=pltpu.SMEM),
        pl.BlockSpec((group_rows, 1), lambda g: (0, 0)),
        pl.BlockSpec((1, group_rows), lambda g: (0, 0)),
        table,
        table,
    ]
    return head, tall, pl.BlockSpec((2, 1, group_rows // 2, lanes), lambda g: (0, g, 0, 0))


def attend(lengths, positions, cosine, sine, q, k, v):
    rows, cols = q.shape
    half = rows // 4
    lanes = cols // HEAD_DIM
    head, tall, thin = _specs(rows // 2, cols, lanes)
    shape = (2, 2, half, cols)
    outs = pl.pallas_call(
        attend_kernel,
        grid=(2,),
        in_specs=head + [tall] * 3,
        out_specs=[tall] * 4 + [thin],
        out_shape=[jax.ShapeDtypeStruct(shape, bf16)] * 4 + [jax.ShapeDtypeStruct((2, 2, half, lanes), f32)],
        compiler_params=pltpu.CompilerParams(vmem_limit_bytes=48 << 20),
        cost_estimate=pl.CostEstimate(flops=4 * rows * rows * cols // 2, bytes_accessed=rows * cols * 20, transcendentals=rows * rows * lanes // 2),
        name="attend",
    )(lengths, positions[:, None], positions[None, :], cosine, sine, *(u.reshape(shape) for u in (q, k, v)))
    return outs


def attend_back(lengths, positions, cosine, sine, saved, g):
    o, q, k, v, lse = saved
    shape = q.shape
    _, _, half, cols = shape
    rows = 4 * half
    lanes = cols // HEAD_DIM
    head, tall, thin = _specs(rows // 2, cols, lanes)
    outs = pl.pallas_call(
        attend_back_kernel,
        grid=(2,),
        in_specs=head + [tall] * 5 + [thin],
        out_specs=[tall] * 3,
        out_shape=[jax.ShapeDtypeStruct(shape, bf16)] * 3,
        compiler_params=pltpu.CompilerParams(vmem_limit_bytes=48 << 20),
        cost_estimate=pl.CostEstimate(flops=10 * rows * rows * cols // 2, bytes_accessed=rows * cols * 16, transcendentals=rows * rows * lanes // 2),
        name="attend_back",
    )(lengths, positions[:, None], positions[None, :], cosine, sine, q, k, v, o, g.reshape(shape), lse)
    return [u.reshape(rows, cols) for u in outs]


class Wires:
    def __init__(self, dp, tp):
        self.dp, self.tp = dp, tp
        self.order = list(range(0, dp, 2)) + list(range(1, dp, 2))
        self.far = []
        bit = 2 * PAIR
        while bit < dp:
            self.far.append(bit)
            bit *= 2

    def over_dp(self, value, mask):
        pairs = []
        for d in range(self.dp):
            for t in range(self.tp):
                pairs.append((d * self.tp + t, (d ^ mask) * self.tp + t))
        return lax.ppermute(value, AXES, pairs)

    def over_tensor(self, value, mask):
        pairs = []
        for d in range(self.dp):
            for t in range(self.tp):
                pairs.append((d * self.tp + t, d * self.tp + (t ^ mask)))
        return lax.ppermute(value, AXES, pairs)

    def to_relative(self, value, d):
        width = value.shape[1] // self.dp
        return jnp.concatenate(
            [lax.dynamic_slice_in_dim(value, (d ^ m) * width, width, 1) for m in self.order], axis=1
        )

    def to_absolute(self, value, d):
        width = value.shape[1] // self.dp
        parts = []
        for j in range(self.dp):
            m = d ^ j
            place = (m >> 1) + (self.dp // 2) * (m & 1)
            parts.append(lax.dynamic_slice_in_dim(value, place * width, width, 1))
        return jnp.concatenate(parts, axis=1)

    def swap_pair(self, value):
        width = value.shape[1] // self.dp
        parts = []
        for p in range(self.dp):
            q = p ^ 1
            parts.append(value[:, q * width : (q + 1) * width])
        return jnp.concatenate(parts, axis=1)


def halves(value, side, axis):
    width = value.shape[axis] // 2
    own = lax.dynamic_slice_in_dim(value, side * width, width, axis)
    other = lax.dynamic_slice_in_dim(value, (1 - side) * width, width, axis)
    return own, other


def joined(own, other, side, axis):
    low = jnp.where(side == 0, own, other)
    high = jnp.where(side == 0, other, own)
    return jnp.concatenate([low, high], axis=axis)


class Chain:
    def __init__(self):
        self.last = ()

    def pin(self, *values):
        return lax.optimization_barrier((values, self.last))[0]

    def wait(self, *values):
        self.last = self.pin(*values)
        return self.last if len(values) > 1 else self.last[0]

    def step(self, function, *values):
        out = function(*self.pin(*values))
        self.last = out
        return out


class Piece:
    def __init__(self, wires, chain, own, other):
        self.wires, self.chain, self.blocks, self.other = wires, chain, own, other

    def start1(self):
        self.got = self.wires.over_dp(*self.chain.pin(self.other), PAIR)

    def wait1(self):
        self.blocks = jnp.concatenate([self.blocks, self.chain.wait(self.got)], axis=0)

    def start2(self):
        self.got = self.wires.over_dp(*self.chain.pin(self.blocks), self.wires.far[0])

    def wait2(self):
        self.blocks = jnp.concatenate([self.blocks, self.chain.wait(self.got)], axis=0)
        for bit in self.wires.far[1:]:
            got = self.chain.wait(self.wires.over_dp(self.blocks, bit))
            self.blocks = jnp.concatenate([self.blocks, got], axis=0)

    def start3(self):
        self.got = self.wires.over_dp(*self.chain.pin(self.blocks), NEAR)

    def wait3(self):
        self.pair = (self.blocks, self.chain.wait(self.got))

    def full(self):
        return jnp.concatenate(self.pair, axis=0)


class Grad:
    def __init__(self, wires, chain, x, y):
        self.wires, self.chain, self.x, self.y = wires, chain, x, y

    def part(self, x, y, low, high):
        return mix("tk,tn->kn", x[:, low:high], y)

    def odd(self):
        k = self.x.shape[1] // 2
        self.send = self.chain.step(lambda x, y: self.part(x, y, k, 2 * k).astype(bf16), self.x, self.y)

    def start1(self):
        self.got = self.wires.over_dp(*self.chain.pin(self.send), NEAR)

    def wait1(self):
        got = self.chain.wait(self.got)
        k = self.x.shape[1] // 2
        h = k // 2

        def far_half(x, y, g):
            return (self.part(x, y, h, k) + g[h:].astype(f32)).astype(bf16)

        def near_half(x, y, g):
            return self.part(x, y, 0, h) + g[:h].astype(f32)

        self.send = self.chain.step(far_half, self.x, self.y, got)
        self.got = self.wires.over_dp(self.send, self.wires.far[-1])
        self.keep = self.chain.step(near_half, self.x, self.y, got)

    def wait2(self):
        got = self.chain.wait(self.got)
        for bit in reversed(self.wires.far[:-1]):
            total = self.keep + got.astype(f32)
            rows = total.shape[0] // 2
            self.keep = total[:rows]
            got = self.chain.wait(self.wires.over_dp(total[rows:].astype(bf16), bit))
        rows = got.shape[0] // 2

        def add(keep, g):
            total = keep + g.astype(f32)
            return total[:rows], total[rows:].astype(bf16)

        self.own, send = self.chain.step(add, self.keep, got)
        self.got = self.wires.over_dp(send, PAIR)

    def wait3(self):
        self.other = self.chain.wait(self.got)


class RowGather:
    def __init__(self, wires, chain, value, swapped):
        self.wires, self.chain, self.value = wires, chain, value
        value, swapped = chain.pin(value, swapped)
        self.z = wires.over_dp(swapped, PAIR)
        self.y = wires.over_tensor(value, 2)

    def wait1(self):
        self.z = self.chain.wait(self.z)
        self.zy = self.wires.over_tensor(self.z, 2)

    def wait2(self):
        self.y = self.chain.wait(self.y)
        self.first = self.chain.step(
            lambda v, y, z: jnp.concatenate([v, y, z], axis=0), self.value, self.y, self.z
        )
        self.c = self.wires.over_tensor(self.first, 1)

    def wait3(self):
        self.zy = self.chain.wait(self.zy)
        self.czy = self.wires.over_tensor(self.zy, 1)

    def wait4(self):
        c, czy = self.chain.wait(self.c, self.czy)
        return self.chain.step(lambda *v: jnp.concatenate(v, axis=0), self.first, self.zy, c, czy)


class RowSum:
    def __init__(self, wires, chain, value):
        self.wires, self.chain = wires, chain
        self.rows = value.shape[0] // 8
        self.near, far = chain.step(lambda v: (v[: 4 * self.rows], v[4 * self.rows :]), value)
        self.c = wires.over_tensor(far, 1)

    def wait1(self):
        got = self.chain.wait(self.c)
        rows = self.rows

        def last(near, g):
            return (near[3 * rows :].astype(f32) + g[3 * rows :].astype(f32)).astype(bf16)

        def rest(near, g):
            total = near[: 3 * rows].astype(f32) + g[: 3 * rows].astype(f32)
            return total[:rows], total[rows : 2 * rows].astype(bf16), total[2 * rows :]

        self.zy = self.wires.over_tensor(self.chain.step(last, self.near, got), 2)
        self.own, y, self.z = self.chain.step(rest, self.near, got)
        self.y = self.wires.over_tensor(y, 2)

    def wait2(self):
        got = self.chain.wait(self.zy)
        z = self.chain.step(lambda z, g: self.wires.swap_pair((z + g.astype(f32)).astype(bf16)), self.z, got)
        self.z = self.wires.over_dp(z, PAIR)

    def wait3(self):
        self.y, self.z = self.chain.wait(self.y, self.z)


def on_device(dp, tp, hidden_in, cotangent, lengths, gain_attn, w_qkv, w_out, gain_mlp, w_gate_up, w_down):
    wires = Wires(dp, tp)
    chain = Chain()
    d = lax.axis_index("dp")
    t = lax.axis_index("tensor")
    side = (d // PAIR) % 2
    local_rows, width = hidden_in.shape
    group_rows = local_rows * tp
    kb = width // dp
    cols = w_qkv.shape[2] // 2
    head_count = cols // HEAD_DIM

    pieces = [Piece(wires, chain, *halves(w_qkv[j], side, 1)) for j in range(3)]
    pieces.append(Piece(wires, chain, *[h.T for h in halves(w_out, side, 0)]))
    down_own, down_other = (h.T for h in halves(w_down, side, 0))
    ff = down_own.shape[1]
    n_down, n_gu = 2, 4
    cut = ff // n_down
    for k in range(n_down):
        pieces.append(Piece(wires, chain, *[h[:, k * cut : (k + 1) * cut] for h in (down_own, down_other)]))
    gu_own, gu_other = halves(w_gate_up, side, 2)
    cg = ff // n_gu
    for k in range(n_gu):
        pieces.append(
            Piece(wires, chain, *[h[:, :, k * cg : (k + 1) * cg].reshape(kb, 2 * cg) for h in (gu_own, gu_other)])
        )
    w_q, w_k, w_v, w_o, d0, d1, g0, g1, g2, g3 = pieces
    gus = [g0, g1, g2, g3]

    w_q.start1()
    gains = jnp.stack([gain_attn, gain_mlp])[:, None]
    w_k.start1()
    pair_length = wires.over_dp(lengths, PAIR)
    got = wires.over_dp(gains, PAIR)
    w_q.wait1()
    w_q.start2()
    for bit in wires.far + [NEAR]:
        gains = jnp.concatenate([gains, chain.wait(got)], axis=1)
        got = wires.over_dp(gains, bit)
    gains = jnp.concatenate([gains, chain.wait(got)], axis=1)
    gains = gains.reshape(2, width).astype(f32)
    gain_a, gain_m = gains[0:1], gains[1:2]

    def open_rows(x, gain):
        x = wires.to_relative(x, d).astype(f32)
        unit, scale = rms_unit(x)
        v = (unit * gain).astype(bf16)
        return x, unit, scale, v, wires.swap_pair(v)

    input_f, unit_first, scale_first, v, swapped = chain.step(open_rows, hidden_in, gain_a)
    rows_a = RowGather(wires, chain, v, swapped)
    w_k.wait1()
    w_k.start2()
    w_v.start1()

    def tables(lengths, pair_length):
        starts = jnp.stack([t, t ^ 2, t ^ 1, t ^ 3]) * local_rows
        positions = (starts[:, None] + jnp.arange(local_rows, dtype=jnp.int32)[None, :]).reshape(-1)
        exponent = jnp.arange(HEAD_DIM // 2).astype(f32) * (2.0 / HEAD_DIM)
        frequency = ROPE_BASE ** (-exponent)
        angles = positions.astype(f32)[:, None] * frequency[None, :]
        cosine = jnp.tile(jnp.concatenate([jnp.cos(angles), jnp.cos(angles)], axis=1), (1, head_count))
        sine = jnp.tile(jnp.concatenate([-jnp.sin(angles), jnp.sin(angles)], axis=1), (1, head_count))
        return jnp.concatenate([lengths, pair_length]), positions, cosine, sine

    own_rows = t * local_rows + jnp.arange(local_rows, dtype=jnp.int32)
    live = (own_rows < lengths[0]).astype(f32)[:, None]

    def open_cotangent(c, live):
        g = wires.to_relative(c, d) * live
        h = g.astype(bf16)
        return g, h, wires.swap_pair(h)

    grad_rows, gv, gswapped = chain.step(open_cotangent, cotangent, live)
    rows_a.wait1()
    rows_a.wait2()
    w_q.wait2()
    w_q.start3()
    table = chain.step(tables, lengths, pair_length)
    w_v.wait1()
    w_v.start2()
    rows_a.wait3()
    normed_first = rows_a.wait4()
    w_k.wait2()
    w_k.start3()
    w_o.start1()
    rows_g = RowGather(wires, chain, gv, gswapped)

    def product(x, piece):
        k = width // 2
        return chain.step(
            lambda x, e, o: jnp.dot(x[:, :k], e, preferred_element_type=f32)
            + jnp.dot(x[:, k:], o, preferred_element_type=f32),
            x, *piece.pair,
        )

    w_q.wait3()
    query_raw = product(normed_first, w_q)
    w_o.wait1()
    rows_g.wait1()
    w_v.wait2()
    w_v.start3()
    w_o.start2()
    d0.start1()
    rows_g.wait2()
    w_k.wait3()
    key_raw = product(normed_first, w_k)
    d0.wait1()
    w_o.wait2()
    w_o.start3()
    d0.start2()
    d1.start1()
    rows_g.wait3()
    w_v.wait3()
    value_raw = product(normed_first, w_v)
    saved = chain.step(lambda *a: attend(*a), *table, query_raw, key_raw, value_raw)
    attn_flat = saved[0].reshape(2 * group_rows, cols)
    grad_half = rows_g.wait4()
    w_o.wait3()
    back = lambda y, e, o: mix("tn,kn->tk", y, jnp.concatenate([e, o], axis=0)).astype(bf16)
    mixed_out = RowSum(wires, chain, chain.step(back, attn_flat, *w_o.pair))
    d1.wait1()
    d0.wait2()
    d0.start3()
    d1.start2()
    g0.start1()
    mixed_out.wait1()
    g0.wait1()
    mixed_out.wait2()
    d1.wait2()
    d1.start3()
    g0.start2()
    g1.start1()
    d0.wait3()
    act_0 = product(grad_half, d0)
    mixed_out.wait3()

    def open_second(own, y, z, x, gain):
        middle = x + own + y.astype(f32) + z.astype(f32)
        unit, scale = rms_unit(middle)
        v = (unit * gain).astype(bf16)
        return middle, unit, scale, v, wires.swap_pair(v)

    middle, unit_second, scale_second, v, swapped = chain.step(
        open_second, mixed_out.own, mixed_out.y, mixed_out.z, input_f, gain_m
    )
    rows_n = RowGather(wires, chain, v, swapped)
    g1.wait1()
    d1.wait3()
    act_1 = product(grad_half, d1)
    grad_acts = [act_0, act_1]
    rows_n.wait1()
    g0.wait2()
    g0.start3()
    g1.start2()
    g2.start1()
    rows_n.wait2()
    rows_n.wait3()
    g2.wait1()
    normed_second = rows_n.wait4()
    g1.wait2()
    g1.start3()
    g2.start2()
    g3.start1()

    per = n_gu // n_down
    acts, grads_gu, second, grads = [], [], None, []

    def gated(x, e, o, ga):
        k = width // 2
        gate_up = jnp.dot(x[:, :k], e, preferred_element_type=f32) + jnp.dot(
            x[:, k:], o, preferred_element_type=f32
        )
        gate, up = gate_up[:, :cg], gate_up[:, cg:]
        sig = jax.nn.sigmoid(gate)
        g = jnp.concatenate([ga * up * sig * (1.0 + gate * (1.0 - sig)), ga * gate * sig], axis=1)
        return (gate * sig * up).astype(bf16), g.astype(bf16)

    def forward_gu(k):
        ga = grad_acts[k // per][:, (k % per) * cg : (k % per + 1) * cg]
        return chain.step(gated, normed_second, *gus[k].pair, ga)

    def add_second(parts, g, piece, last):
        def one(g, w, part=None):
            out = mix("tn,kn->tk", g, w)
            if part is not None:
                out = out + part
            return out.astype(bf16) if last else out

        if parts is None:
            return [chain.step(one, g, w) for w in piece.pair]
        return [chain.step(one, g, w, p) for w, p in zip(piece.pair, parts)]

    for k in range(n_gu):
        gus[k].wait3()
        act, g = forward_gu(k)
        acts.append(act)
        if k == n_gu - 1:
            grads[0].start1()
        second = add_second(second, g, gus[k], k == n_gu - 1)
        grads.append(Grad(wires, chain, normed_second, g))
        if k < n_gu - 1:
            grads[k].odd()
        if k == 0:
            g3.wait1()
            g2.wait2()
            g2.start3()
            g3.start2()
        if k == 1:
            g3.wait2()
            g3.start3()

    second = chain.step(lambda e, o: jnp.concatenate([e, o], axis=1), *second)
    sum_second = RowSum(wires, chain, second)
    grads[1].start1()
    grads[3].odd()
    sum_second.wait1()
    acts = [jnp.concatenate(acts[k * per : (k + 1) * per], axis=1) for k in range(n_down)]
    grads += [Grad(wires, chain, grad_half, a) for a in acts]
    grads[4].odd()
    grads[5].odd()
    grads[0].wait1()
    grads[2].start1()
    sum_second.wait2()

    def down_product(a0, a1, *w):
        full = [jnp.concatenate(w[:2], axis=0), jnp.concatenate(w[2:], axis=0)]
        return (mix("tn,kn->tk", a0, full[0]) + mix("tn,kn->tk", a1, full[1])).astype(bf16)

    mlp_part = chain.step(down_product, *acts, *d0.pair, *d1.pair)
    grads[1].wait1()
    grads[3].start1()
    sum_second.wait3()
    grads[0].wait2()

    def close_second(own, y, z, gain, unit, scale, rows):
        grad = own + y.astype(f32) + z.astype(f32)
        middle = rows + norm_back(grad, gain, unit, scale)
        h = middle.astype(bf16)
        return jnp.sum(grad * unit, axis=0), middle, h, wires.swap_pair(h)

    part_gain_mlp, grad_middle, v, swapped = chain.step(
        close_second, sum_second.own, sum_second.y, sum_second.z, gain_m, unit_second, scale_second, grad_rows
    )
    rows_m = RowGather(wires, chain, v, swapped)
    grads[2].wait1()
    grads[4].start1()
    rows_m.wait1()
    grads[1].wait2()
    rows_m.wait2()
    grads[0].wait3()
    rows_m.wait3()
    middle_half = rows_m.wait4()
    mlp = RowSum(wires, chain, mlp_part)
    grad_mixed = product(middle_half, w_o).astype(bf16)
    grads[3].wait1()
    grads[5].start1()
    mlp.wait1()
    grad_proj = chain.step(lambda *a: attend_back(*a), *table, saved, grad_mixed)
    grads[2].wait2()
    grads.append(Grad(wires, chain, middle_half, attn_flat))
    grads[6].odd()
    mlp.wait2()
    grads += [Grad(wires, chain, normed_first, g) for g in grad_proj]
    first = None
    for g, w in zip(grad_proj, (w_q, w_k, w_v)):
        first = add_second(first, g, w, w is w_v)
    first = chain.step(lambda e, o: jnp.concatenate([e, o], axis=1), *first)
    mlp.wait3()
    layer_out = chain.step(
        lambda own, y, z, m, live: wires.to_absolute((m + own + y.astype(f32) + z.astype(f32)) * live, d),
        mlp.own, mlp.y, mlp.z, middle, live,
    )
    sum_first = RowSum(wires, chain, first)
    grads[4].wait1()
    grads[6].start1()
    grads[1].wait3()
    grads[7].odd()
    sum_first.wait1()
    grads[3].wait2()
    grads[8].odd()
    sum_first.wait2()
    grads[2].wait3()
    grads[5].wait1()
    grads[7].start1()
    sum_first.wait3()

    def close_first(own, y, z, gain, unit, scale, rows):
        grad = own + y.astype(f32) + z.astype(f32)
        out = rows + norm_back(grad, gain, unit, scale)
        return jnp.sum(grad * unit, axis=0), wires.to_absolute(out, d)

    part_gain_attn, grad_in = chain.step(
        close_first, sum_first.own, sum_first.y, sum_first.z, gain_a, unit_first, scale_first, grad_middle
    )
    grads[9].odd()
    grads[4].wait2()
    grads[3].wait3()

    total = jnp.stack([part_gain_attn, part_gain_mlp]).reshape(2, dp, kb)
    grads[6].wait1()
    grads[8].start1()

    def gain_step(bit):
        nonlocal total
        rows = total.shape[1] // 2
        total = total[:, :rows] + chain.wait(wires.over_dp(total[:, rows:], bit))

    gain_step(NEAR)
    grads[5].wait2()
    grads[4].wait3()
    for bit in wires.far[::-1]:
        gain_step(bit)
    grads[7].wait1()
    grads[9].start1()
    gain_step(PAIR)
    grads[6].wait2()
    grads[5].wait3()
    total = total[:, 0]
    total = total + chain.wait(wires.over_tensor(total, 1))
    grads[8].wait1()
    total = total + chain.wait(wires.over_tensor(total, 2))
    grads[7].wait2()
    grads[6].wait3()
    grads[9].wait1()
    grads[8].wait2()
    grads[7].wait3()
    grads[9].wait2()
    grads[8].wait3()
    grads[9].wait3()

    sides = ([g.own for g in grads], [g.other.astype(f32) for g in grads])

    def down_of(s):
        return jnp.concatenate(s[4:6], axis=1).T

    def gu_of(s):
        return jnp.concatenate([p.reshape(kb, 2, cg) for p in s[:4]], axis=2)

    return (
        layer_out,
        grad_in,
        total[0],
        jnp.stack([joined(sides[0][i], sides[1][i], side, 1) for i in (7, 8, 9)]),
        joined(sides[0][6].T, sides[1][6].T, side, 0),
        total[1],
        joined(gu_of(sides[0]), gu_of(sides[1]), side, 2),
        joined(down_of(sides[0]), down_of(sides[1]), side, 0),
    )


def solution(mesh):
    placed = (
        P(("dp", "tensor"), None),
        P(("dp", "tensor"), None),
        P("dp"),
        P("dp"),
        P(None, "dp", "tensor"),
        P("tensor", "dp"),
        P("dp"),
        P("dp", None, "tensor"),
        P("tensor", "dp"),
    )
    dp, tp = mesh.shape["dp"], mesh.shape["tensor"]

    def body(*args):
        return on_device(dp, tp, *args)

    return jax.shard_map(
        body,
        mesh=mesh,
        in_specs=placed,
        out_specs=(
            P(("dp", "tensor"), None),
            P(("dp", "tensor"), None),
            P("dp"),
            P(None, "dp", "tensor"),
            P("tensor", "dp"),
            P("dp"),
            P("dp", None, "tensor"),
            P("tensor", "dp"),
        ),
        check_vma=False,
    )
```

time: 1400 us -> 1140 us (0.81)
  waiting for transfers between devices: 790 us -> 563 us
  local copies, waits for them, and re-layouts: 199 us -> 132 us
  starting transfers between devices: 160 us -> 109 us
  matrix products: 172 us -> 205 us
  Pallas kernels: 0 us -> 30.3 us
  other arithmetic: 67.5 us -> 87.8 us
    ppermute x93 -> x75, waiting for transfers between devices: 700 us -> 521 us  [over_dp(): return lax.ppermute(value, AXES, pairs)]
    unnamed x376 -> x382, local copies, waits for them, and re-layouts: 130 us -> 67.9 us
    ppermute x93 -> x75, starting transfers between devices: 148 us -> 89.4 us  [over_dp(): return lax.ppermute(value, AXES, pairs)]
    ppermute x50 -> x30, waiting for transfers between devices: 89.4 us -> 41.4 us  [over_tensor(): return lax.ppermute(value, AXES, pairs)]
    pallas_call x0 -> x2, Pallas kernels: none -> 30.3 us  [the longest x1 16.3 us: attend_back(): pl.pallas_call(attend_back_kernel, grid=(2,), in_specs=head + [tall] * 5...]
    dot_general x18 -> x47, matrix products: 123 us -> 152 us  [mix(): return jnp.einsum(form, left, right, preferred_element_type=f32)]
    another operation x17 -> x7, local copies, waits for them, and re-layouts: 27.5 us -> 1.38 us  [the longest x3 1.21 us: on_device(): total = jnp.stack([part_gain_attn, part_gain_mlp]).reshape(2, dp, kb)]
    slice x9 -> x38, local copies, waits for them, and re-layouts: 10.4 us -> 31.6 us  [the longest x17 8.9 us: add(): return (total[:rows], total[rows:].astype(bf16))]
  transfers between devices with their start and end apart: 143 -> 105, of which waited for: 60 -> 43; matrix products, arithmetic and copies ran while one was open for 20% -> 32% of each run, Pallas kernels for 0% -> 3%
where the time goes in v2:
time: 1140 us; the launch traced here: 1130 us
  waiting for transfers between devices  563 us (49%)
  matrix products  205 us (18%)
  local copies, waits for them, and re-layouts  132 us (12%)
  starting transfers between devices  109 us (10%)
  other arithmetic  87.8 us (8%)
  Pallas kernels  30.3 us (3%)
    ppermute x75, waiting for transfers between devices, over_dp(): return lax.ppermute(value, AXES, pairs)  521 us
    dot_general x47, matrix products, mix(): return jnp.einsum(form, left, right, preferred_element_type=f32)  152 us
    ppermute x75, starting transfers between devices, over_dp(): return lax.ppermute(value, AXES, pairs)  89.4 us
    unnamed x382, local copies, waits for them, and re-layouts  67.9 us
    ppermute x30, waiting for transfers between devices, over_tensor(): return lax.ppermute(value, AXES, pairs)  41.4 us
  transfers between devices with their start and end apart: 105, of which 43 were waited for; matrix products, arithmetic and copies ran while one was open for 32% of the time, Pallas kernels for 3%

profile of v2, /device:TPU:0, one launch (start us, length us, event | category | flops | bytes accessed | tf_op | source)
XLA Modules:
  0.0 1132.3 jit_solution(2705496878277949782)
XLA Ops:
  37.5 13.2 %collective-permute-done.7 = bf16[128,3072]{1,0:T(8,128)(2,1)S(1)} collective-permute-done((bf16[128,3072]{1,0:T(8,128)(2,1)S(1)}, bf16[128,3072]{1,0:T(8,128)(2,1)S(1)}, u32[]{:S(2)}, u32[]{:S(2)}) %collective-permute-start.7) | collective-permute-done | bytes 786464 | tf_op jit(solution)/shard_map/ppermute | solution.py:197
  63.1 23.9 %collective-permute-done.2 = bf16[768,384]{1,0:T(8,128)(2,1)} collective-permute-done((bf16[768,384]{1,0:T(8,128)(2,1)}, bf16[768,384]{1,0:T(8,128)(2,1)}, u32[]{:S(2)}, u32[]{:S(2)}) %collective-permute-start.2) | collective-permute-done | bytes 589856 | tf_op jit(solution)/shard_map/ppermute | solution.py:197
  101.1 29.8 %collective-permute-done.14 = bf16[768,384]{1,0:T(8,128)(2,1)S(1)} collective-permute-done((bf16[768,384]{1,0:T(8,128)(2,1)S(1)}, bf16[768,384]{1,0:T(8,128)(2,1)S(1)}, u32[]{:S(2)}, u32[]{:S(2)}) %collective-permute-start.14) | collective-permute-done | bytes 589856 | tf_op jit(solution)/shard_map/ppermute | solution.py:197
  140.8 9.1 collective-permute-done.19
  149.9 16.7 %collective-permute-done.18 = bf16[128,3072]{1,0:T(8,128)(2,1)S(1)} collective-permute-done((bf16[128,3072]{1,0:T(8,128)(2,1)S(1)}, bf16[128,3072]{1,0:T(8,128)(2,1)S(1)}, u32[]{:S(2)}, u32[]{:S(2)}) %collective-permute-start.18) | collective-permute-done | bytes 786464 | tf_op jit(solution)/shard_map/ppermute | solution.py:197
  181.2 20.0 %collective-permute-done.22 = bf16[768,384]{0,1:T(8,128)(2,1)S(1)} collective-permute-done((bf16[768,384]{0,1:T(8,128)(2,1)S(1)}, bf16[768,384]{0,1:T(8,128)(2,1)S(1)}, u32[]{:S(2)}, u32[]{:S(2)}) %collective-permute-start.22) | collective-permute-done | bytes 589856 | tf_op jit(solution)/shard_map/ppermute | solution.py:197
  209.5 14.0 %attend.1 = (bf16[2,2,256,384]{3,2,1,0:T(8,128)(2,1)S(1)}, bf16[2,2,256,384]{3,2,1,0:T(8,128)(2,1)S(1)}, bf16[2,2,256,384]{3,2,1,0:T(8,128)(2,1)S(1)}, bf16[2,2,...) custom-call(s32[2]{0:T(128)S(1)} %pad_add_fusion.len_ref, s32[512,1]{1,0:T(8,128)S(1)} %copy.27.rows_ref, ...), custom_call_target="tpu_custom_call" | custom-call | flops 805306368 | bytes 7864320 | tf_op jit(solution)/shard_map/attend/pallas_call | solution.py:149
  250.0 19.5 %collective-permute-done.29 = bf16[384,512]{0,1:T(8,128)(2,1)} collective-permute-done((bf16[384,512]{0,1:T(8,128)(2,1)}, bf16[384,512]{0,1:T(8,128)(2,1)}, u32[]{:S(2)}, u32[]{:S(2)}) %collective-permute-start.29) | collective-permute-done | bytes 393248 | tf_op jit(solution)/shard_map/ppermute | solution.py:197
  269.5 10.6 collective-permute-done.28
  296.4 11.5 %collective-permute-done.31 = bf16[128,3072]{1,0:T(8,128)(2,1)S(1)} collective-permute-done((bf16[128,3072]{1,0:T(8,128)(2,1)S(1)}, bf16[128,3072]{1,0:T(8,128)(2,1)S(1)}, u32[]{:S(2)}, u32[]{:S(2)}) %collective-permute-start.31) | collective-permute-done | bytes 786464 | tf_op jit(solution)/shard_map/ppermute | solution.py:204
  308.3 11.8 %collective-permute-done.35 = bf16[768,512]{0,1:T(8,128)(2,1)S(1)} collective-permute-done((bf16[768,512]{0,1:T(8,128)(2,1)S(1)}, bf16[768,512]{0,1:T(8,128)(2,1)S(1)}, u32[]{:S(2)}, u32[]{:S(2)}) %collective-permute-start.35) | collective-permute-done | bytes 786464 | tf_op jit(solution)/shard_map/ppermute | solution.py:197
  328.2 18.4 %collective-permute-done.33 = bf16[128,3072]{1,0:T(8,128)(2,1)S(1)} collective-permute-done((bf16[128,3072]{1,0:T(8,128)(2,1)S(1)}, bf16[128,3072]{1,0:T(8,128)(2,1)S(1)}, u32[]{:S(2)}, u32[]{:S(2)}) %collective-permute-start.33) | collective-permute-done | bytes 786464 | tf_op jit(solution)/shard_map/ppermute | solution.py:197
  349.4 11.7 %collective-permute-done.40 = bf16[384,512]{1,0:T(8,128)(2,1)S(1)} collective-permute-done((bf16[384,512]{1,0:T(8,128)(2,1)S(1)}, bf16[384,512]{1,0:T(8,128)(2,1)S(1)}, u32[]{:S(2)}, u32[]{:S(2)}) %collective-permute-start.40) | collective-permute-done | bytes 393248 | tf_op jit(solution)/shard_map/ppermute | solution.py:197
  365.5 14.4 %collective-permute-done.38 = bf16[128,3072]{1,0:T(8,128)(2,1)S(1)} collective-permute-done((bf16[128,3072]{1,0:T(8,128)(2,1)S(1)}, bf16[128,3072]{1,0:T(8,128)(2,1)S(1)}, u32[]{:S(2)}, u32[]{:S(2)}) %collective-permute-start.38) | collective-permute-done | bytes 786464 | tf_op jit(solution)/shard_map/ppermute | solution.py:197
  382.2 18.2 %collective-permute-done.41 = bf16[128,3072]{1,0:T(8,128)(2,1)S(1)} collective-permute-done((bf16[128,3072]{1,0:T(8,128)(2,1)S(1)}, bf16[128,3072]{1,0:T(8,128)(2,1)S(1)}, u32[]{:S(2)}, u32[]{:S(2)}) %collective-permute-start.41) | collective-permute-done | bytes 786464 | tf_op jit(solution)/shard_map/ppermute | solution.py:204
  406.0 13.7 %collective-permute-done.44 = bf16[384,512]{1,0:T(8,128)(2,1)S(1)} collective-permute-done((bf16[384,512]{1,0:T(8,128)(2,1)S(1)}, bf16[384,512]{1,0:T(8,128)(2,1)S(1)}, u32[]{:S(2)}, u32[]{:S(2)}) %collective-permute-start.44) | collective-permute-done | bytes 393248 | tf_op jit(solution)/shard_map/ppermute | solution.py:197
  420.3 18.3 %collective-permute-done.46 = bf16[768,512]{1,0:T(8,128)(2,1)S(1)} collective-permute-done((bf16[768,512]{1,0:T(8,128)(2,1)S(1)}, bf16[768,512]{1,0:T(8,128)(2,1)S(1)}, u32[]{:S(2)}, u32[]{:S(2)}) %collective-permute-start.46) | collective-permute-done | bytes 786464 | tf_op jit(solution)/shard_map/ppermute | solution.py:197
  458.7 18.6 %collective-permute-done.48 = bf16[768,512]{1,0:T(8,128)(2,1)S(1)} collective-permute-done((bf16[768,512]{1,0:T(8,128)(2,1)S(1)}, bf16[768,512]{1,0:T(8,128)(2,1)S(1)}, u32[]{:S(2)}, u32[]{:S(2)}) %collective-permute-start.48) | collective-permute-done | bytes 786464 | tf_op jit(solution)/shard_map/ppermute | solution.py:197
  494.9 17.1 %collective-permute-done.51 = bf16[768,512]{1,0:T(8,128)(2,1)S(1)} collective-permute-done((bf16[768,512]{1,0:T(8,128)(2,1)S(1)}, bf16[768,512]{1,0:T(8,128)(2,1)S(1)}, u32[]{:S(2)}, u32[]{:S(2)}) %collective-permute-start.51) | collective-permute-done | bytes 786464 | tf_op jit(solution)/shard_map/ppermute | solution.py:197
  528.9 19.5 %collective-permute-done.52 = bf16[1536,512]{1,0:T(8,128)(2,1)S(1)} collective-permute-done((bf16[1536,512]{1,0:T(8,128)(2,1)S(1)}, bf16[1536,512]{1,0:T(8,128)(2,1)S(1)}, u32[]{:S(2)}, u32[]{:S(2)}) %collective-permute-start.52) | collective-permute-done | bytes 1572896 | tf_op jit(solution)/shard_map/ppermute | solution.py:197
  584.6 52.2 %collective-permute-done.55 = bf16[1536,512]{1,0:T(8,128)(2,1)S(1)} collective-permute-done((bf16[1536,512]{1,0:T(8,128)(2,1)}, bf16[1536,512]{1,0:T(8,128)(2,1)S(1)}, u32[]{:S(2)}, u32[]{:S(2)}) %collective-permute-start.55) | collective-permute-done | bytes 1572896 | tf_op jit(solution)/shard_map/ppermute | solution.py:197
  668.4 13.7 %collective-permute-done.57 = bf16[128,3072]{1,0:T(8,128)(2,1)S(1)} collective-permute-done((bf16[128,3072]{1,0:T(8,128)(2,1)}, bf16[128,3072]{1,0:T(8,128)(2,1)S(1)}, u32[]{:S(2)}, u32[]{:S(2)}) %collective-permute-start.57) | collective-permute-done | bytes 786464 | tf_op jit(solution)/shard_map/ppermute | solution.py:197
  698.8 23.2 %collective-permute-done.62 = bf16[128,3072]{1,0:T(8,128)(2,1)S(1)} collective-permute-done((bf16[128,3072]{1,0:T(8,128)(2,1)S(1)}, bf16[128,3072]{1,0:T(8,128)(2,1)S(1)}, u32[]{:S(2)}, u32[]{:S(2)}) %collective-permute-start.62) | collective-permute-done | bytes 786464 | tf_op jit(solution)/shard_map/ppermute | solution.py:197
  727.6 11.2 collective-permute-done.65
  738.8 7.3 collective-permute-done.64
  766.2 26.5 %collective-permute-done.69 = bf16[1536,512]{1,0:T(8,128)(2,1)} collective-permute-done((bf16[1536,512]{1,0:T(8,128)(2,1)}, bf16[1536,512]{1,0:T(8,128)(2,1)}, u32[]{:S(2)}, u32[]{:S(2)}) %collective-permute-start.69) | collective-permute-done | bytes 1572896 | tf_op jit(solution)/shard_map/ppermute | solution.py:197
  814.3 16.3 %attend_back.1 = (bf16[2,2,256,384]{3,2,1,0:T(8,128)(2,1)S(1)}, bf16[2,2,256,384]{3,2,1,0:T(8,128)(2,1)S(1)}, bf16[2,2,256,384]{3,2,1,0:T(8,128)(2,1)S(1)}) custom-call(s32[2]{0:T(128)S(1)} %copy-done.4, s32[512,1]{1,0:T(8,128)S(1)} %copy.38.rows_ref, s32[1,512]{1,0:T(1,128)S(1)} %bitcast.194, f32[512,384]{1,0:T(8,128)S(1)} %copy.39.cos_ref, ...), custom_call_target="tpu_custom_call" | custom-call | flops 2013265920 | bytes 6291456 | tf_op jit(solution)/shard_map/attend_back/pallas_call | solution.py:169
  889.6 16.4 %collective-permute-done.76 = bf16[1536,512]{1,0:T(8,128)(2,1)} collective-permute-done((bf16[1536,512]{1,0:T(8,128)(2,1)}, bf16[1536,512]{1,0:T(8,128)(2,1)}, u32[]{:S(2)}, u32[]{:S(2)}) %collective-permute-start.76) | collective-permute-done | bytes 1572896 | tf_op jit(solution)/shard_map/ppermute | solution.py:197
  969.4 15.3 %collective-permute-done.80 = bf16[128,3072]{1,0:T(8,128)(2,1)} collective-permute-done((bf16[128,3072]{1,0:T(8,128)(2,1)}, bf16[128,3072]{1,0:T(8,128)(2,1)}, u32[]{:S(2)}, u32[]{:S(2)}) %collective-permute-start.80) | collective-permute-done | bytes 786464 | tf_op jit(solution)/shard_map/ppermute | solution.py:197
  1016.8 8.9 pad_maximum_fusion.1
  1078.8 26.0 %collective-permute-done.99 = bf16[768,384]{1,0:T(8,128)(2,1)} collective-permute-done((bf16[768,384]{1,0:T(8,128)(2,1)}, bf16[768,384]{1,0:T(8,128)(2,1)}, u32[]{:S(2)}, u32[]{:S(2)}) %collective-permute-start.99) | collective-permute-done | bytes 589856 | tf_op jit(solution)/shard_map/ppermute | solution.py:197
  1106.3 11.0 collective-permute-done.103
  (821 shorter events, 569.6 us)
Async XLA Ops:
  53.5 42.6 %collective-permute-start.11 = (bf16[384,3072]{1,0:T(8,128)(2,1)}, bf16[384,3072]{1,0:T(8,128)(2,1)}, u32[]{:S(2)}, u32[]{:S(2)}) collective-permute-start(bf16[384,3072]{1,0:T(8,128)(2,1)} %constant_dynamic-update-slice_fusion.32), channel_id=1, source_target_pairs={{0,1},{1,0},{2,3},{3,2},{4,5},{5,4},{6,7},{7,6},{8,9},{9,8},{10,11... | collective-permute-start | bytes 7077896 | tf_op jit(solution)/shard_map/ppermute | solution.py:204
  89.2 41.7 %collective-permute-start.14 = (bf16[768,384]{1,0:T(8,128)(2,1)S(1)}, bf16[768,384]{1,0:T(8,128)(2,1)S(1)}, u32[]{:S(2)}, u32[]{:S(2)}) collective-permute-start(bf16[768,384]{1,0:T(8,128)(2,1)S(1)} %pad_maximum_fusion.27), channel_id=1, source_target_pairs={{0,16},{1,17},{2,18},{3,19},{4,20},{5,21},{6,22},{7,23},{8,24},{9,... | collective-permute-start | bytes 1769480 | tf_op jit(solution)/shard_map/ppermute | solution.py:197
  91.9 76.1 %collective-permute-start.17 = (bf16[768,384]{1,0:T(8,128)(2,1)S(1)}, bf16[768,384]{1,0:T(8,128)(2,1)S(1)}, u32[]{:S(2)}, u32[]{:S(2)}) collective-permute-start(bf16[768,384]{1,0:T(8,128)(2,1)S(1)} %pad_maximum_fusion.28), channel_id=1, source_target_pairs={{0,16},{1,17},{2,18},{3,19},{4,20},{5,21},{6,22},{7,23},{8,24},{9,... | collective-permute-start | bytes 1769480 | tf_op jit(solution)/shard_map/ppermute | solution.py:197
  134.5 39.4 %collective-permute-start.15 = (bf16[1536,384]{1,0:T(8,128)(2,1)S(1)}, bf16[1536,384]{1,0:T(8,128)(2,1)S(1)}, u32[]{:S(2)}, u32[]{:S(2)}) collective-permute-start(bf16[1536,384]{1,0:T(8,128)(2,1)S(1)} %pad_maximum_fusion.9), channel_id=1, source_target_pairs={{0,4},{1,5},{2,6},{3,7},{4,0},{5,1},{6,2},{7,3},{8,12},{9,13},{10,... | collective-permute-start | bytes 3538952 | tf_op jit(solution)/shard_map/ppermute | solution.py:197
  170.8 52.7 %collective-permute-start.25 = (bf16[384,3072]{1,0:T(8,128)(2,1)}, bf16[384,3072]{1,0:T(8,128)(2,1)}, u32[]{:S(2)}, u32[]{:S(2)}) collective-permute-start(bf16[384,3072]{1,0:T(8,128)(2,1)} %constant_dynamic-update-slice_fusion.39), channel_id=1, source_target_pairs={{0,1},{1,0},{2,3},{3,2},{4,5},{5,4},{6,7},{7,6},{8,9},{9,8},{10,11... | collective-permute-start | bytes 7077896 | tf_op jit(solution)/shard_map/ppermute | solution.py:204
  241.0 44.9 %collective-permute-start.27 = (bf16[512,3072]{1,0:T(8,128)(2,1)}, bf16[512,3072]{1,0:T(8,128)(2,1)}, u32[]{:S(2)}, u32[]{:S(2)}) collective-permute-start(bf16[512,3072]{1,0:T(8,128)(2,1)} %get-tuple-element.930), channel_id=1, source_target_pairs={{0,1},{1,0},{2,3},{3,2},{4,5},{5,4},{6,7},{7,6},{8,9},{9,8},{10,11... | collective-permute-start | bytes 9437192 | tf_op jit(solution)/shard_map/ppermute | solution.py:204
  308.3 38.4 %collective-permute-start.33 = (bf16[128,3072]{1,0:T(8,128)(2,1)S(1)}, bf16[128,3072]{1,0:T(8,128)(2,1)S(1)}, u32[]{:S(2)}, u32[]{:S(2)}) collective-permute-start(bf16[128,3072]{1,0:T(8,128)(2,1)S(1)} %constant_dynamic-update-slice_fusion.46), channel_id=1, source_target_pairs={{0,8},{1,9},{2,10},{3,11},{4,12},{5,13},{6,14},{7,15},{8,0},{9,1},... | collective-permute-start | bytes 2359304 | tf_op jit(solution)/shard_map/ppermute | solution.py:197
  321.3 39.8 %collective-permute-start.40 = (bf16[384,512]{1,0:T(8,128)(2,1)S(1)}, bf16[384,512]{1,0:T(8,128)(2,1)S(1)}, u32[]{:S(2)}, u32[]{:S(2)}) collective-permute-start(bf16[384,512]{1,0:T(8,128)(2,1)S(1)} %bitcast.238), channel_id=1, source_target_pairs={{0,8},{1,9},{2,10},{3,11},{4,12},{5,13},{6,14},{7,15},{8,0},{9,1},... | collective-permute-start | bytes 1179656 | tf_op jit(solution)/shard_map/ppermute | solution.py:197
  321.4 58.4 %collective-permute-start.37 = (bf16[768,512]{1,0:T(8,128)(2,1)S(1)}, bf16[768,512]{1,0:T(8,128)(2,1)S(1)}, u32[]{:S(2)}, u32[]{:S(2)}) collective-permute-start(bf16[768,512]{1,0:T(8,128)(2,1)S(1)} %pad_maximum_fusion.21), channel_id=1, source_target_pairs={{0,16},{1,17},{2,18},{3,19},{4,20},{5,21},{6,22},{7,23},{8,24},{9,... | collective-permute-start | bytes 2359304 | tf_op jit(solution)/shard_map/ppermute | solution.py:197
  380.0 39.8 %collective-permute-start.42 = (bf16[384,3072]{1,0:T(8,128)(2,1)S(1)}, bf16[384,3072]{1,0:T(8,128)(2,1)S(1)}, u32[]{:S(2)}, u32[]{:S(2)}) collective-permute-start(bf16[384,3072]{1,0:T(8,128)(2,1)S(1)} %constant_dynamic-update-slice_fusion.62), channel_id=1, source_target_pairs={{0,1},{1,0},{2,3},{3,2},{4,5},{5,4},{6,7},{7,6},{8,9},{9,8},{10,11... | collective-permute-start | bytes 7077896 | tf_op jit(solution)/shard_map/ppermute | solution.py:204
  566.7 96.1 %collective-permute-start.58 = (bf16[1536,512]{1,0:T(8,128)(2,1)}, bf16[1536,512]{1,0:T(8,128)(2,1)}, u32[]{:S(2)}, u32[]{:S(2)}) collective-permute-start(bf16[1536,512]{1,0:T(8,128)(2,1)} %fusion.70), channel_id=1, source_target_pairs={{0,4},{1,5},{2,6},{3,7},{4,0},{5,1},{6,2},{7,3},{8,12},{9,13},{10,... | collective-permute-start | bytes 4718600 | tf_op jit(solution)/shard_map/ppermute | solution.py:197
  567.8 69.0 %collective-permute-start.55 = (bf16[1536,512]{1,0:T(8,128)(2,1)}, bf16[1536,512]{1,0:T(8,128)(2,1)S(1)}, u32[]{:S(2)}, u32[]{:S(2)}) collective-permute-start(bf16[1536,512]{1,0:T(8,128)(2,1)} %fusion.67), channel_id=1, source_target_pairs={{0,4},{1,5},{2,6},{3,7},{4,0},{5,1},{6,2},{7,3},{8,12},{9,13},{10,... | collective-permute-start | bytes 4718600 | tf_op jit(solution)/shard_map/ppermute | solution.py:197
  574.4 66.6 %collective-permute-start.54 = (bf16[128,3072]{1,0:T(8,128)(2,1)S(1)}, bf16[128,3072]{1,0:T(8,128)(2,1)S(1)}, u32[]{:S(2)}, u32[]{:S(2)}) collective-permute-start(bf16[128,3072]{1,0:T(8,128)(2,1)S(1)} %add_convert_fusion.16), channel_id=1, source_target_pairs={{0,2},{1,3},{2,0},{3,1},{4,6},{5,7},{6,4},{7,5},{8,10},{9,11},{10,... | collective-permute-start | bytes 2359304 | tf_op jit(solution)/shard_map/ppermute | solution.py:204
  577.6 90.7 %collective-permute-start.56 = (bf16[128,3072]{1,0:T(8,128)(2,1)}, bf16[128,3072]{1,0:T(8,128)(2,1)S(1)}, u32[]{:S(2)}, u32[]{:S(2)}) collective-permute-start(bf16[128,3072]{1,0:T(8,128)(2,1)} %slice.1393), channel_id=1, source_target_pairs={{0,2},{1,3},{2,0},{3,1},{4,6},{5,7},{6,4},{7,5},{8,10},{9,11},{10,... | collective-permute-start | bytes 2359304 | tf_op jit(solution)/shard_map/ppermute | solution.py:204
  638.8 43.3 %collective-permute-start.59 = (bf16[768,512]{1,0:T(8,128)(2,1)}, bf16[768,512]{1,0:T(8,128)(2,1)}, u32[]{:S(2)}, u32[]{:S(2)}) collective-permute-start(bf16[768,512]{1,0:T(8,128)(2,1)} %add_convert_fusion.15), channel_id=1, source_target_pairs={{0,16},{1,17},{2,18},{3,19},{4,20},{5,21},{6,22},{7,23},{8,24},{9,... | collective-permute-start | bytes 2359304 | tf_op jit(solution)/shard_map/ppermute | solution.py:197
  639.8 51.3 %collective-permute-start.63 = (bf16[1536,512]{1,0:T(8,128)(2,1)}, bf16[1536,512]{1,0:T(8,128)(2,1)}, u32[]{:S(2)}, u32[]{:S(2)}) collective-permute-start(bf16[1536,512]{1,0:T(8,128)(2,1)} %fusion.73), channel_id=1, source_target_pairs={{0,4},{1,5},{2,6},{3,7},{4,0},{5,1},{6,2},{7,3},{8,12},{9,13},{10,... | collective-permute-start | bytes 4718600 | tf_op jit(solution)/shard_map/ppermute | solution.py:197
  755.6 43.5 %collective-permute-start.68 = (bf16[512,3072]{1,0:T(8,128)(2,1)}, bf16[512,3072]{1,0:T(8,128)(2,1)}, u32[]{:S(2)}, u32[]{:S(2)}) collective-permute-start(bf16[512,3072]{1,0:T(8,128)(2,1)} %get-tuple-element.926), channel_id=1, source_target_pairs={{0,1},{1,0},{2,3},{3,2},{4,5},{5,4},{6,7},{7,6},{8,9},{9,8},{10,11... | collective-permute-start | bytes 9437192 | tf_op jit(solution)/shard_map/ppermute | solution.py:204
  756.7 74.0 %collective-permute-start.72 = (bf16[768,512]{1,0:T(8,128)(2,1)}, bf16[768,512]{1,0:T(8,128)(2,1)}, u32[]{:S(2)}, u32[]{:S(2)}) collective-permute-start(bf16[768,512]{1,0:T(8,128)(2,1)} %add_convert_fusion.12), channel_id=1, source_target_pairs={{0,16},{1,17},{2,18},{3,19},{4,20},{5,21},{6,22},{7,23},{8,24},{9,... | collective-permute-start | bytes 2359304 | tf_op jit(solution)/shard_map/ppermute | solution.py:197
  868.5 53.8 %collective-permute-start.74 = (bf16[512,3072]{1,0:T(8,128)(2,1)}, bf16[512,3072]{1,0:T(8,128)(2,1)}, u32[]{:S(2)}, u32[]{:S(2)}) collective-permute-start(bf16[512,3072]{1,0:T(8,128)(2,1)} %get-tuple-element.924), channel_id=1, source_target_pairs={{0,1},{1,0},{2,3},{3,2},{4,5},{5,4},{6,7},{7,6},{8,9},{9,8},{10,11... | collective-permute-start | bytes 9437192 | tf_op jit(solution)/shard_map/ppermute | solution.py:204
  875.2 38.4 %collective-permute-start.75 = (bf16[384,512]{1,0:T(8,128)(2,1)}, bf16[384,512]{1,0:T(8,128)(2,1)}, u32[]{:S(2)}, u32[]{:S(2)}) collective-permute-start(bf16[384,512]{1,0:T(8,128)(2,1)} %slice.1399), channel_id=1, source_target_pairs={{0,8},{1,9},{2,10},{3,11},{4,12},{5,13},{6,14},{7,15},{8,0},{9,1},... | collective-permute-start | bytes 1179656 | tf_op jit(solution)/shard_map/ppermute | solution.py:197
  881.5 49.9 %collective-permute-start.79 = (bf16[768,512]{1,0:T(8,128)(2,1)}, bf16[768,512]{1,0:T(8,128)(2,1)}, u32[]{:S(2)}, u32[]{:S(2)}) collective-permute-start(bf16[768,512]{1,0:T(8,128)(2,1)} %add_convert_fusion.11), channel_id=1, source_target_pairs={{0,16},{1,17},{2,18},{3,19},{4,20},{5,21},{6,22},{7,23},{8,24},{9,... | collective-permute-start | bytes 2359304 | tf_op jit(solution)/shard_map/ppermute | solution.py:197
  883.6 75.7 %collective-permute-start.81 = (bf16[1536,512]{1,0:T(8,128)(2,1)}, bf16[1536,512]{1,0:T(8,128)(2,1)}, u32[]{:S(2)}, u32[]{:S(2)}) collective-permute-start(bf16[1536,512]{1,0:T(8,128)(2,1)} %fusion.82), channel_id=1, source_target_pairs={{0,4},{1,5},{2,6},{3,7},{4,0},{5,1},{6,2},{7,3},{8,12},{9,13},{10,... | collective-permute-start | bytes 4718600 | tf_op jit(solution)/shard_map/ppermute | solution.py:197
  906.0 47.7 %collective-permute-start.82 = (bf16[384,512]{1,0:T(8,128)(2,1)}, bf16[384,512]{1,0:T(8,128)(2,1)}, u32[]{:S(2)}, u32[]{:S(2)}) collective-permute-start(bf16[384,512]{1,0:T(8,128)(2,1)} %slice.1398), channel_id=1, source_target_pairs={{0,8},{1,9},{2,10},{3,11},{4,12},{5,13},{6,14},{7,15},{8,0},{9,1},... | collective-permute-start | bytes 1179656 | tf_op jit(solution)/shard_map/ppermute | solution.py:197
  915.5 80.6 %collective-permute-start.86 = (bf16[768,512]{1,0:T(8,128)(2,1)}, bf16[768,512]{1,0:T(8,128)(2,1)}, u32[]{:S(2)}, u32[]{:S(2)}) collective-permute-start(bf16[768,512]{1,0:T(8,128)(2,1)} %add_convert_fusion.8), channel_id=1, source_target_pairs={{0,16},{1,17},{2,18},{3,19},{4,20},{5,21},{6,22},{7,23},{8,24},{9,... | collective-permute-start | bytes 2359304 | tf_op jit(solution)/shard_map/ppermute | solution.py:197
  953.7 47.9 %collective-permute-start.84 = (bf16[1536,384]{1,0:T(8,128)(2,1)}, bf16[1536,384]{1,0:T(8,128)(2,1)}, u32[]{:S(2)}, u32[]{:S(2)}) collective-permute-start(bf16[1536,384]{1,0:T(8,128)(2,1)} %fusion.85), channel_id=1, source_target_pairs={{0,4},{1,5},{2,6},{3,7},{4,0},{5,1},{6,2},{7,3},{8,12},{9,13},{10,... | collective-permute-start | bytes 3538952 | tf_op jit(solution)/shard_map/ppermute | solution.py:197
  959.3 40.5 %collective-permute-start.85 = (bf16[384,512]{1,0:T(8,128)(2,1)}, bf16[384,512]{1,0:T(8,128)(2,1)}, u32[]{:S(2)}, u32[]{:S(2)}) collective-permute-start(bf16[384,512]{1,0:T(8,128)(2,1)} %slice.1397), channel_id=1, source_target_pairs={{0,8},{1,9},{2,10},{3,11},{4,12},{5,13},{6,14},{7,15},{8,0},{9,1},... | collective-permute-start | bytes 1179656 | tf_op jit(solution)/shard_map/ppermute | solution.py:197
  969.1 61.1 %collective-permute-start.89 = (bf16[768,512]{1,0:T(8,128)(2,1)}, bf16[768,512]{1,0:T(8,128)(2,1)}, u32[]{:S(2)}, u32[]{:S(2)}) collective-permute-start(bf16[768,512]{1,0:T(8,128)(2,1)} %add_convert_fusion.5), channel_id=1, source_target_pairs={{0,16},{1,17},{2,18},{3,19},{4,20},{5,21},{6,22},{7,23},{8,24},{9,... | collective-permute-start | bytes 2359304 | tf_op jit(solution)/shard_map/ppermute | solution.py:197
  984.7 50.2 %collective-permute-start.91 = (bf16[1536,384]{1,0:T(8,128)(2,1)}, bf16[1536,384]{1,0:T(8,128)(2,1)}, u32[]{:S(2)}, u32[]{:S(2)}) collective-permute-start(bf16[1536,384]{1,0:T(8,128)(2,1)} %fusion.88), channel_id=1, source_target_pairs={{0,4},{1,5},{2,6},{3,7},{4,0},{5,1},{6,2},{7,3},{8,12},{9,13},{10,... | collective-permute-start | bytes 3538952 | tf_op jit(solution)/shard_map/ppermute | solution.py:197
  1005.1 42.2 %collective-permute-start.94 = (bf16[768,384]{1,0:T(8,128)(2,1)}, bf16[768,384]{1,0:T(8,128)(2,1)}, u32[]{:S(2)}, u32[]{:S(2)}) collective-permute-start(bf16[768,384]{1,0:T(8,128)(2,1)} %fusion.229), channel_id=1, source_target_pairs={{0,16},{1,17},{2,18},{3,19},{4,20},{5,21},{6,22},{7,23},{8,24},{9,... | collective-permute-start | bytes 1769480 | tf_op jit(solution)/shard_map/ppermute | solution.py:197
  1063.4 41.4 %collective-permute-start.99 = (bf16[768,384]{1,0:T(8,128)(2,1)}, bf16[768,384]{1,0:T(8,128)(2,1)}, u32[]{:S(2)}, u32[]{:S(2)}) collective-permute-start(bf16[768,384]{1,0:T(8,128)(2,1)} %fusion.223), channel_id=1, source_target_pairs={{0,16},{1,17},{2,18},{3,19},{4,20},{5,21},{6,22},{7,23},{8,24},{9,... | collective-permute-start | bytes 1769480 | tf_op jit(solution)/shard_map/ppermute | solution.py:197
  1067.9 38.2 %collective-permute-start.98 = (bf16[384,384]{1,0:T(8,128)(2,1)S(1)}, bf16[384,384]{1,0:T(8,128)(2,1)S(1)}, u32[]{:S(2)}, u32[]{:S(2)}) collective-permute-start(bf16[384,384]{1,0:T(8,128)(2,1)S(1)} %slice.1403), channel_id=1, source_target_pairs={{0,8},{1,9},{2,10},{3,11},{4,12},{5,13},{6,14},{7,15},{8,0},{9,1},... | collective-permute-start | bytes 884744 | tf_op jit(solution)/shard_map/ppermute | solution.py:197
  1075.6 41.7 %collective-permute-start.103 = (bf16[768,384]{1,0:T(8,128)(2,1)S(1)}, bf16[768,384]{1,0:T(8,128)(2,1)S(1)}, u32[]{:S(2)}, u32[]{:S(2)}) collective-permute-start(bf16[768,384]{1,0:T(8,128)(2,1)S(1)} %fusion.220), channel_id=1, source_target_pairs={{0,16},{1,17},{2,18},{3,19},{4,20},{5,21},{6,22},{7,23},{8,24},{9,... | collective-permute-start | bytes 1769480 | tf_op jit(solution)/shard_map/ppermute | solution.py:197
  (201 other events, 4839.9 us)

commit v3 on v1

v3 whole, which is shorter than its diff:
```python
import math

import jax
import jax.numpy as jnp
from jax import lax
from jax.experimental import pallas as pl
from jax.experimental.pallas import tpu as pltpu
from jax.sharding import PartitionSpec as P

HEAD_DIM = 96
NORM_EPS = 1e-05
ROPE_BASE = 10000.0
AXES = ("dp", "tensor")
PAIR = 2
NEAR = 1
NEGATIVE = -1e30

bf16 = jnp.bfloat16
f32 = jnp.float32


def dot_last(a, b):
    return lax.dot_general(a, b, (((1,), (1,)), ((), ())), preferred_element_type=f32)


def dot_first(a, b):
    return lax.dot_general(a, b, (((0,), (0,)), ((), ())), preferred_element_type=f32)


def turned(u, low):
    width = u.shape[1]
    half = HEAD_DIM // 2
    return jnp.where(low, pltpu.roll(u, width - half, 1), pltpu.roll(u, half, 1))


def low_lanes(shape):
    lane = lax.broadcasted_iota(jnp.int32, shape, 1)
    low = lane < 0
    for h in range(shape[1] // HEAD_DIM):
        low = low | ((lane >= h * HEAD_DIM) & (lane < h * HEAD_DIM + HEAD_DIM // 2))
    return low


def group_block(ref):
    return ref[...]


def put_block(ref, v):
    ref[...] = v


def masked_scores(qh, kh, allowed):
    return jnp.where(allowed, dot_last(qh, kh) * (1.0 / math.sqrt(HEAD_DIM)), NEGATIVE)


def allowed_pairs(rows_ref, cols_ref, length):
    rp, cp = rows_ref[...], cols_ref[...]
    return (cp <= rp) & ((rp < length) == (cp < length))


def attend_kernel(len_ref, rows_ref, cols_ref, cos_ref, sin_ref, q_ref, k_ref, v_ref,
                  o_ref, qo_ref, ko_ref, vo_ref, lse_ref):
    allowed = allowed_pairs(rows_ref, cols_ref, len_ref[pl.program_id(0)])
    cosine, sine = cos_ref[...], sin_ref[...]
    low = low_lanes(cosine.shape)
    q, k = group_block(q_ref), group_block(k_ref)
    q = q * cosine + turned(q, low) * sine
    k = k * cosine + turned(k, low) * sine
    v = group_block(v_ref)
    put_block(qo_ref, q.astype(bf16))
    put_block(ko_ref, k.astype(bf16))
    put_block(vo_ref, v.astype(bf16))
    outs, totals = [], []
    for h in range(q.shape[1] // HEAD_DIM):
        c = slice(h * HEAD_DIM, (h + 1) * HEAD_DIM)
        s = masked_scores(q[:, c].astype(bf16), k[:, c].astype(bf16), allowed)
        top = jnp.max(s, axis=1, keepdims=True)
        e = jnp.exp(s - top)
        total = jnp.sum(e, axis=1, keepdims=True)
        prob = (e * (1.0 / total)).astype(bf16)
        outs.append(jnp.dot(prob, v[:, c].astype(bf16), preferred_element_type=f32))
        totals.append(top + jnp.log(total))
    put_block(o_ref, jnp.concatenate(outs, axis=1).astype(bf16))
    put_block(lse_ref, jnp.concatenate(totals, axis=1))


def attend_back_kernel(len_ref, rows_ref, cols_ref, cos_ref, sin_ref, q_ref, k_ref, v_ref, o_ref, g_ref, lse_ref,
                       dq_ref, dk_ref, dv_ref):
    allowed = allowed_pairs(rows_ref, cols_ref, len_ref[pl.program_id(0)])
    q, k, v, g = (group_block(r).astype(f32) for r in (q_ref, k_ref, v_ref, g_ref))
    go = g * group_block(o_ref).astype(f32)
    totals = group_block(lse_ref)
    dqs, dks, dvs = [], [], []
    for h in range(q.shape[1] // HEAD_DIM):
        c = slice(h * HEAD_DIM, (h + 1) * HEAD_DIM)
        qh, kh, vh, gh = (u[:, c].astype(bf16) for u in (q, k, v, g))
        delta = jnp.sum(go[:, c], axis=1, keepdims=True)
        prob = jnp.exp(masked_scores(qh, kh, allowed) - totals[:, h : h + 1])
        ds = (prob * (dot_last(gh, vh) - delta) * (1.0 / math.sqrt(HEAD_DIM))).astype(bf16)
        dqs.append(jnp.dot(ds, kh, preferred_element_type=f32))
        dks.append(dot_first(ds, qh))
        dvs.append(dot_first(prob.astype(bf16), gh))
    cosine, sine = cos_ref[...], sin_ref[...]
    low = low_lanes(cosine.shape)
    for ref, parts in ((dq_ref, dqs), (dk_ref, dks)):
        u = jnp.concatenate(parts, axis=1)
        put_block(ref, (u * cosine - turned(u, low) * sine).astype(bf16))
    put_block(dv_ref, jnp.concatenate(dvs, axis=1).astype(bf16))


def attend_specs(group_rows, cols, lanes):
    tall = pl.BlockSpec((group_rows, cols), lambda g: (g, 0))
    table = pl.BlockSpec((group_rows, cols), lambda g: (0, 0))
    head = [
        pl.BlockSpec(memory_space=pltpu.SMEM),
        pl.BlockSpec((group_rows, 1), lambda g: (0, 0)),
        pl.BlockSpec((1, group_rows), lambda g: (0, 0)),
        table,
        table,
    ]
    return head, tall, pl.BlockSpec((group_rows, lanes), lambda g: (g, 0))


def attend(lengths, positions, cosine, sine, q, k, v):
    rows, cols = q.shape
    lanes = cols // HEAD_DIM
    head, tall, thin = attend_specs(rows // 2, cols, lanes)
    return run(
        attend_kernel, "attend", [((rows, cols), bf16)] * 4 + [((rows, lanes), f32)],
        [lengths, positions[:, None], positions[None, :], cosine, sine, q, k, v], (2,),
        head + [tall] * 3, [tall] * 4 + [thin],
    )


def attend_back(lengths, positions, cosine, sine, saved, g):
    o, q, k, v, lse = saved
    rows, cols = q.shape
    head, tall, thin = attend_specs(rows // 2, cols, cols // HEAD_DIM)
    return run(
        attend_back_kernel, "attend_back", [((rows, cols), bf16)] * 3,
        [lengths, positions[:, None], positions[None, :], cosine, sine, q, k, v, o, g, lse], (2,),
        head + [tall] * 5 + [thin], [tall] * 3,
    )


def run(kernel, name, outs, args, grid=(), in_specs=None, out_specs=None, scratch=(), scalars=0):
    whole = pl.BlockSpec(memory_space=pltpu.VMEM)
    if in_specs is None:
        in_specs = [whole] * (len(args) - scalars)
    if out_specs is None:
        out_specs = [whole] * len(outs)
    got = pl.pallas_call(
        kernel,
        out_shape=[jax.ShapeDtypeStruct(s, t) for s, t in outs],
        grid_spec=pltpu.PrefetchScalarGridSpec(
            num_scalar_prefetch=scalars, grid=grid, in_specs=in_specs, out_specs=out_specs, scratch_shapes=scratch
        ),
        compiler_params=pltpu.CompilerParams(vmem_limit_bytes=52 << 20),
        cost_estimate=pl.CostEstimate(flops=1, bytes_accessed=1, transcendentals=0),
        name=name,
    )(*args)
    return list(got)


SMALL = pl.BlockSpec(memory_space=pltpu.SMEM)
VMEM = pl.BlockSpec(memory_space=pltpu.VMEM)


def tiles(rows, width):
    return pl.BlockSpec((rows, width), lambda i: (i, 0))


def still(shape):
    return pl.BlockSpec(shape, lambda i: (0,) * len(shape), pipeline_mode=pl.Buffered(1))


def product(x, pair, dtype=f32):
    rows, width = x.shape
    k, n = pair[0].shape
    tile = rows // 4

    def kernel(x_ref, even, odd, out):
        total = jnp.dot(x_ref[:, :k], even[...], preferred_element_type=f32)
        total += jnp.dot(x_ref[:, k:], odd[...], preferred_element_type=f32)
        out[...] = total.astype(dtype)

    return run(
        kernel, "product", [((rows, n), dtype)], [x, *pair], (4,),
        [tiles(tile, width)] + [still((k, n))] * 2, [tiles(tile, n)],
    )[0]


def gated(x, pair, grad_act, column):
    rows, width = x.shape
    k, n = pair[0].shape
    c = n // 2
    tile = rows // 4

    def kernel(x_ref, even, odd, ga_ref, act, grad):
        total = jnp.dot(x_ref[:, :k], even[...], preferred_element_type=f32)
        total += jnp.dot(x_ref[:, k:], odd[...], preferred_element_type=f32)
        gate, up, ga = total[:, :c], total[:, c:], ga_ref[...]
        sig = jax.nn.sigmoid(gate)
        act[...] = (gate * sig * up).astype(bf16)
        grad[:, :c] = (ga * up * sig * (1.0 + gate * (1.0 - sig))).astype(bf16)
        grad[:, c:] = (ga * gate * sig).astype(bf16)

    return run(
        kernel, "gated", [((rows, c), bf16), ((rows, n), bf16)], [x, *pair, grad_act], (4,),
        [tiles(tile, width)] + [still((k, n))] * 2 + [pl.BlockSpec((tile, c), lambda i: (i, column))],
        [tiles(tile, c), tiles(tile, n)],
    )


def back(ys, pairs, dtype, part=None):
    rows = ys[0].shape[0]
    k = pairs[0][0].shape[0]
    count = len(ys)
    tile = rows // 4

    def kernel(*refs):
        y_refs, w_refs, out = refs[:count], refs[count : 3 * count], refs[-1]
        for s in range(2):
            c = slice(s * k, (s + 1) * k)
            total = refs[3 * count][:, c] if part is not None else None
            for y, w in zip(y_refs, w_refs[s::2]):
                term = dot_last(y[...], w[...])
                total = term if total is None else total + term
            out[:, c] = total.astype(dtype)

    flat = [w for p in pairs for w in p]
    return run(
        kernel, "back", [((rows, 2 * k), dtype)], [*ys, *flat] + ([] if part is None else [part]), (4,),
        [tiles(tile, y.shape[1]) for y in ys]
        + [still(w.shape) for w in flat]
        + ([] if part is None else [tiles(tile, 2 * k)]),
        [tiles(tile, 2 * k)],
    )[0]


def weight_part(x, y, first, count, dtype, got=None, got_first=0):
    rows = x.shape[0]
    n = y.shape[1]
    tile = count if count <= 768 else count // 2
    base, got_base = first // tile, got_first // tile

    def kernel(x_ref, y_ref, *rest):
        total = dot_first(x_ref[...], y_ref[...])
        if got is not None:
            total += rest[0][...].astype(f32)
        rest[-1][...] = total.astype(dtype)

    extra = [] if got is None else [pl.BlockSpec((tile, n), lambda i: (i + got_base, 0))]
    return run(
        kernel, "weight_part", [((count, n), dtype)], [x, y] + ([] if got is None else [got]), (count // tile,),
        [pl.BlockSpec((rows, tile), lambda i: (0, i + base)), still(y.shape)] + extra, [tiles(tile, n)],
    )[0]


class Rows:
    def __init__(self, wires, info, rows, width):
        self.wires, self.info, self.rows, self.width = wires, info, rows, width
        self.kb = width // wires.dp
        self.inside = self.kb % 128 == 0

    def load_relative(self, ref, info):
        if not self.inside:
            return ref[...].astype(f32)
        kb = self.kb
        parts = []
        for m in self.wires.order:
            parts.append(ref[:, pl.ds(pl.multiple_of((info[0] ^ m) * kb, 128), kb)].astype(f32))
        return jnp.concatenate(parts, axis=1)

    def store_absolute(self, ref, value, scratch, info):
        if not self.inside:
            ref[...] = value
            return
        kb, half = self.kb, self.wires.dp // 2
        scratch[...] = value
        for j in range(self.wires.dp):
            m = info[0] ^ j
            place = (m >> 1) + half * (m & 1)
            ref[:, j * kb : (j + 1) * kb] = scratch[:, pl.ds(pl.multiple_of(place * kb, 128), kb)]

    def relative(self, x):
        return x if self.inside else self.wires.to_relative(x, self.info[0])

    def absolute(self, x):
        return x if self.inside else self.wires.to_absolute(x, self.info[0])

    def live(self, info, shape):
        row = info[1] * shape[0] + lax.broadcasted_iota(jnp.int32, (shape[0], 1), 0)
        return (row < info[2]).astype(f32)

    def outs(self, *dtypes):
        return [((self.rows, self.width), t) for t in dtypes]

    def open_first(self, x, gains):
        def kernel(info, x_ref, gain_ref, rel, scale_ref, v):
            x = self.load_relative(x_ref, info)
            scale = lax.rsqrt(jnp.mean(x * x, axis=1, keepdims=True) + NORM_EPS)
            rel[...] = x
            scale_ref[...] = scale
            v[...] = (x * scale * gain_ref[0:1].astype(f32)).astype(bf16)

        return run(
            kernel, "open_first", self.outs(f32) + [((self.rows, 1), f32)] + self.outs(bf16),
            [self.info, self.relative(x), gains], in_specs=[SMALL, VMEM, VMEM],
        )

    def open_cotangent(self, c):
        def kernel(info, c_ref, g, v):
            x = self.load_relative(c_ref, info)
            x = x * self.live(info, x.shape)
            g[...] = x
            v[...] = x.astype(bf16)

        return run(
            kernel, "open_cotangent", self.outs(f32, bf16), [self.info, self.relative(c)], in_specs=[SMALL, VMEM]
        )

    def open_second(self, x, got, gains):
        def kernel(x_ref, got_ref, gain_ref, mid, scale_ref, v):
            middle = x_ref[...] + got_ref[...].astype(f32)
            scale = lax.rsqrt(jnp.mean(middle * middle, axis=1, keepdims=True) + NORM_EPS)
            mid[...] = middle
            scale_ref[...] = scale
            v[...] = (middle * scale * gain_ref[1:2].astype(f32)).astype(bf16)

        return run(
            kernel, "open_second", self.outs(f32) + [((self.rows, 1), f32)] + self.outs(bf16), [x, got, gains]
        )

    def norm_back(self, got_ref, gain, x_ref, scale_ref, rows_ref, part):
        grad = got_ref[...].astype(f32)
        scale = scale_ref[...]
        unit = x_ref[...] * scale
        part[...] = jnp.sum(grad * unit, axis=0, keepdims=True)
        e = grad * gain
        return rows_ref[...] + scale * (e - unit * jnp.mean(e * unit, axis=1, keepdims=True))

    def close_second(self, got, gains, middle, scale, rows):
        def kernel(got_ref, gain_ref, x_ref, scale_ref, rows_ref, part, mid, v):
            grad = self.norm_back(got_ref, gain_ref[1:2].astype(f32), x_ref, scale_ref, rows_ref, part)
            mid[...] = grad
            v[...] = grad.astype(bf16)

        return run(
            kernel, "close_second", [((1, self.width), f32)] + self.outs(f32, bf16),
            [got, gains, middle, scale, rows],
        )

    def close_first(self, got, gains, x, scale, rows):
        def kernel(info, got_ref, gain_ref, x_ref, scale_ref, rows_ref, part, out, scratch):
            grad = self.norm_back(got_ref, gain_ref[0:1].astype(f32), x_ref, scale_ref, rows_ref, part)
            self.store_absolute(out, grad, scratch, info)

        part, out = run(
            kernel, "close_first", [((1, self.width), f32)] + self.outs(f32),
            [self.info, got, gains, x, scale, rows], in_specs=[SMALL] + [VMEM] * 5,
            scratch=[pltpu.VMEM((self.rows, self.width), f32)],
        )
        return part, self.absolute(out)

    def close_layer(self, got, middle):
        def kernel(info, got_ref, mid_ref, out, scratch):
            total = mid_ref[...] + got_ref[...].astype(f32)
            self.store_absolute(out, total * self.live(info, total.shape), scratch, info)

        out, = run(
            kernel, "close_layer", self.outs(f32), [self.info, got, middle], in_specs=[SMALL] + [VMEM] * 2,
            scratch=[pltpu.VMEM((self.rows, self.width), f32)],
        )
        return self.absolute(out)


def in_order(side, own, far, far_pair, pair):
    kb, n = own.shape

    def kernel(side_ref, *refs):
        i, s = pl.program_id(0), side_ref[0]
        for at, ref in enumerate((refs[0], refs[3], refs[1], refs[2])):

            @pl.when((i ^ s) == at)
            def _(ref=ref):
                refs[-1][...] = ref[...]

    whole = pl.BlockSpec((kb, n), lambda i, s: (0, 0))
    return run(
        kernel, "in_order", [((4 * kb, n), bf16)], [side, own, far, far_pair, pair], (4,), [whole] * 4,
        [pl.BlockSpec((kb, n), lambda i, s: (i, 0))], scalars=1,
    )[0]


def weight_blocks(side, x, y, got, at, kb, dtypes):
    rows = x.shape[0]
    n = y.shape[1]

    def kernel(side_ref, x_ref, y_ref, g_ref, *outs):
        total = dot_first(x_ref[...], y_ref[...]) + g_ref[...].astype(f32)
        for q, out in enumerate(outs):

            @pl.when(pl.program_id(0) == q)
            def _(out=out):
                out[...] = total.astype(out.dtype)

    return run(
        kernel, "weight_blocks", [((kb, n), t) for t in dtypes], [side, x, y, got], (2,),
        [
            pl.BlockSpec((rows, kb), lambda i, s: (0, at + (i ^ s[0]))),
            pl.BlockSpec(y.shape, lambda i, s: (0, 0), pipeline_mode=pl.Buffered(1)),
            pl.BlockSpec((kb, n), lambda i, s: (at + (i ^ s[0]), 0)),
        ],
        [pl.BlockSpec((kb, n), lambda i, s: (0, 0))] * 2, scalars=1,
    )


def laid_out(side, terms, shape, block, axis, place):
    count = len(terms)

    def kernel(side_ref, *refs):
        out = refs[-1]

        @pl.when(pl.program_id(0) == 0)
        def _():
            place(out, [refs[4 * q][...] + refs[4 * q + 1][...].astype(f32) for q in range(count)])

        @pl.when(pl.program_id(0) == 1)
        def _():
            place(
                out, [refs[4 * q + 2][...].astype(f32) + refs[4 * q + 3][...].astype(f32) for q in range(count)]
            )

    def index(w, side_ref):
        at = w ^ side_ref[0]
        return tuple(at if a == axis else 0 for a in range(len(shape)))

    arrays = [a for t in terms for a in t]
    return run(
        kernel, "laid_out", [(shape, f32)], [side, *arrays], (2,),
        [pl.BlockSpec(a.shape, lambda w, s: (0, 0)) for a in arrays], [pl.BlockSpec(block, index)], scalars=1,
    )[0]


class Wires:
    def __init__(self, dp, tp):
        self.dp, self.tp = dp, tp
        self.order = list(range(0, dp, 2)) + list(range(1, dp, 2))
        self.far = []
        bit = 2 * PAIR
        while bit < dp:
            self.far.append(bit)
            bit *= 2

    def over_dp(self, value, mask):
        pairs = []
        for d in range(self.dp):
            for t in range(self.tp):
                pairs.append((d * self.tp + t, (d ^ mask) * self.tp + t))
        return lax.ppermute(value, AXES, pairs)

    def over_tensor(self, value, mask):
        pairs = []
        for d in range(self.dp):
            for t in range(self.tp):
                pairs.append((d * self.tp + t, d * self.tp + (t ^ mask)))
        return lax.ppermute(value, AXES, pairs)

    def to_relative(self, value, d):
        width = value.shape[1] // self.dp
        return jnp.concatenate(
            [lax.dynamic_slice_in_dim(value, (d ^ m) * width, width, 1) for m in self.order], axis=1
        )

    def to_absolute(self, value, d):
        width = value.shape[1] // self.dp
        parts = []
        for j in range(self.dp):
            m = d ^ j
            place = (m >> 1) + (self.dp // 2) * (m & 1)
            parts.append(lax.dynamic_slice_in_dim(value, place * width, width, 1))
        return jnp.concatenate(parts, axis=1)

    def groups(self):
        found = []
        for d in range(self.dp):
            if not d & PAIR:
                found.append([e * self.tp + t for e in (d, d ^ PAIR) for t in range(self.tp)])
        return found


def halves(value, side, axis):
    width = value.shape[axis] // 2
    own = lax.dynamic_slice_in_dim(value, side * width, width, axis)
    other = lax.dynamic_slice_in_dim(value, (1 - side) * width, width, axis)
    return own, other


def joined(own, other, side, axis):
    low = jnp.where(side == 0, own, other)
    high = jnp.where(side == 0, other, own)
    return jnp.concatenate([low, high], axis=axis)


class Chain:
    def __init__(self):
        self.last = ()

    def pin(self, *values):
        return lax.optimization_barrier((values, self.last))[0]

    def wait(self, *values):
        self.last = self.pin(*values)
        return self.last if len(values) > 1 else self.last[0]

    def step(self, function, *values):
        out = function(*self.pin(*values))
        self.last = out
        return out


class Piece:
    def __init__(self, wires, chain, side, own, other):
        self.wires, self.chain, self.side, self.own, self.other = wires, chain, side, own, other

    def start1(self):
        own, other = self.chain.pin(self.own, self.other)
        far = self.wires.far[0]
        self.got = [
            self.wires.over_dp(own, far), self.wires.over_dp(other, far ^ PAIR), self.wires.over_dp(other, PAIR)
        ]

    def wait1(self):
        self.got = self.chain.wait(*self.got)

    def start2(self):
        blocks = self.chain.step(in_order, self.side, self.own, *self.got)
        for bit in self.wires.far[1:]:
            blocks = jnp.concatenate([blocks, self.chain.wait(self.wires.over_dp(blocks, bit))], axis=0)
        self.blocks = blocks
        self.got = self.wires.over_dp(*self.chain.pin(blocks), NEAR)

    def wait2(self):
        self.pair = (self.blocks, self.chain.wait(self.got))


class Grad:
    def __init__(self, wires, chain, side, x, y):
        self.wires, self.chain, self.side, self.x, self.y = wires, chain, side, x, y
        self.k = x.shape[1] // 2

    def odd(self):
        self.send = self.chain.step(lambda x, y: weight_part(x, y, self.k, self.k, bf16), self.x, self.y)

    def start1(self):
        self.got = self.wires.over_dp(*self.chain.pin(self.send), NEAR)

    def wait1(self):
        self.near = self.chain.wait(self.got)

    def start2(self):
        wires, chain = self.wires, self.chain
        kb = 2 * self.k // wires.dp
        if not wires.far[1:] and kb % 128 == 0:
            blocks = lambda s, x, y, g, at, types: weight_blocks(s, x, y, g, at, kb, types)
            far, far_pair = chain.step(
                lambda s, x, y, g: blocks(s, x, y, g, 2, (bf16, bf16)), self.side, self.x, self.y, self.near
            )
            self.keep, pair = chain.step(
                lambda s, x, y, g: blocks(s, x, y, g, 0, (f32, bf16)), self.side, self.x, self.y, self.near
            )
        else:
            total = chain.step(
                lambda x, y, g: weight_part(x, y, 0, self.k, f32, g, 0), self.x, self.y, self.near
            )
            for bit in reversed(wires.far[1:]):
                rows = total.shape[0] // 2
                got = chain.wait(wires.over_dp(total[rows:].astype(bf16), bit))
                total = total[:rows] + got.astype(f32)
            at = [p ^ self.side[0] for p in (0, 1)]
            cut = lambda p: lax.dynamic_slice_in_dim(total, p * kb, kb, 0)
            self.keep, pair = cut(at[0]), cut(at[1]).astype(bf16)
            far, far_pair = cut(2 + at[0]).astype(bf16), cut(2 + at[1]).astype(bf16)
        bit = wires.far[0]
        self.got = [
            wires.over_dp(*chain.pin(far), bit),
            wires.over_dp(*chain.pin(far_pair), bit ^ PAIR),
            wires.over_dp(*chain.pin(pair), PAIR),
        ]

    def wait2(self):
        self.terms = [self.keep, *self.chain.wait(*self.got)]


class RowGather:
    def __init__(self, wires, chain, value):
        self.chain = chain
        self.got = lax.all_gather(
            *chain.pin(value), AXES, axis=0, tiled=True, axis_index_groups=wires.groups()
        )

    def wait(self):
        return self.chain.wait(self.got)


class RowSum:
    def __init__(self, wires, chain, value):
        self.chain = chain
        self.got = lax.psum_scatter(
            *chain.pin(value), AXES, scatter_dimension=0, tiled=True, axis_index_groups=wires.groups()
        )

    def wait(self):
        return self.chain.wait(self.got)


def on_device(dp, tp, hidden_in, cotangent, lengths, gain_attn, w_qkv, w_out, gain_mlp, w_gate_up, w_down):
    wires = Wires(dp, tp)
    chain = Chain()
    d = lax.axis_index("dp").astype(jnp.int32)
    t = lax.axis_index("tensor").astype(jnp.int32)
    side = (d // PAIR) % 2
    local_rows, width = hidden_in.shape
    group_rows = local_rows * tp
    kb = width // dp
    cols = w_qkv.shape[2] // 2
    head_count = cols // HEAD_DIM
    rows = Rows(wires, jnp.stack([d - PAIR * side, t, lengths[0]]), local_rows, width)

    sides = jnp.reshape(side, (1,))
    n_down, n_gu = 2, 4
    ff = w_down.shape[0] // 2
    cut, cg = ff // n_down, ff // n_gu

    def piece(own, other):
        return Piece(wires, chain, sides, own, other)

    def cut_rest(w_out, w_down, w_gate_up):
        found = [[h.T for h in halves(w_out, side, 0)]]
        whole = [h.T for h in halves(w_down, side, 0)]
        for k in range(n_down):
            found.append([h[:, k * cut : (k + 1) * cut] for h in whole])
        whole = halves(w_gate_up, side, 2)
        for k in range(n_gu):
            found.append([h[:, :, k * cg : (k + 1) * cg].reshape(kb, 2 * cg) for h in whole])
        return found

    per = n_gu // n_down
    acts, grads_gu, grads = [], [], []

    def forward_gu(k):
        act, g = chain.step(lambda *a: gated(*a, k % per), normed_second, gus[k].pair, grad_acts[k // per])
        acts.append(act)
        grads_gu.append(g)
        grads.append(Grad(wires, chain, sides, normed_second, g))

    positions = jnp.arange(group_rows, dtype=jnp.int32)
    exponent = jnp.arange(HEAD_DIM // 2).astype(f32) * (2.0 / HEAD_DIM)
    frequency = ROPE_BASE ** (-exponent)
    angles = positions.astype(f32)[:, None] * frequency[None, :]
    cosine = jnp.tile(jnp.concatenate([jnp.cos(angles), jnp.cos(angles)], axis=1), (1, head_count))
    sine = jnp.tile(jnp.concatenate([-jnp.sin(angles), jnp.sin(angles)], axis=1), (1, head_count))

    gains = jnp.stack([gain_attn, gain_mlp])[:, None]
    pair_length = wires.over_dp(lengths, PAIR)

    def ordered(mine, theirs, axis):
        return jnp.concatenate(
            [jnp.where(side == 0, mine, theirs), jnp.where(side == 0, theirs, mine)], axis=axis
        )

    got = wires.over_dp(gains, PAIR)
    gains = ordered(gains, chain.wait(got), 1)
    for bit in wires.far:
        gains = jnp.concatenate([gains, chain.wait(wires.over_dp(*chain.pin(gains), bit))], axis=1)
    w_q, w_k, w_v = (piece(*halves(w_qkv[j], side, 1)) for j in range(3))
    w_q.start1()
    gains = jnp.concatenate([gains, chain.wait(wires.over_dp(*chain.pin(gains), NEAR))], axis=1)
    gains = gains.reshape(2, width)
    input_f, scale_first, v = chain.step(rows.open_first, hidden_in, gains)
    rows_a = RowGather(wires, chain, v)
    w_o, d0, d1, g0, g1, g2, g3 = (piece(*h) for h in chain.step(cut_rest, w_out, w_down, w_gate_up))
    gus = [g0, g1, g2, g3]
    grad_rows, gv = chain.step(rows.open_cotangent, cotangent)
    table = chain.step(
        lambda a, b, *c: (ordered(a, b, 0), *c), lengths, pair_length, positions, cosine, sine
    )
    w_q.wait1()
    w_k.start1()
    w_q.start2()
    rows_g = RowGather(wires, chain, gv)
    w_k.wait1()
    w_q.wait2()
    w_v.start1()
    w_k.start2()
    normed_first = rows_a.wait()
    query_raw = chain.step(product, normed_first, w_q.pair)
    w_v.wait1()
    w_k.wait2()
    w_o.start1()
    w_v.start2()
    key_raw = chain.step(product, normed_first, w_k.pair)
    w_o.wait1()
    w_v.wait2()
    d0.start1()
    w_o.start2()
    value_raw = chain.step(product, normed_first, w_v.pair)
    saved = chain.step(lambda *a: attend(*a), *table, query_raw, key_raw, value_raw)
    attn_flat = saved[0]
    w_o.wait2()
    mixed = chain.step(lambda y, p: back([y], [p], bf16), attn_flat, w_o.pair)
    d0.wait1()
    d1.start1()
    mixed_out = RowSum(wires, chain, mixed)
    d0.start2()
    grad_half = rows_g.wait()
    d1.wait1()
    d0.wait2()
    g0.start1()
    d1.start2()
    act_0 = chain.step(product, grad_half, d0.pair)
    g0.wait1()
    d1.wait2()
    g1.start1()
    g0.start2()
    act_1 = chain.step(product, grad_half, d1.pair)
    grad_acts = [act_0, act_1]
    middle, scale_second, v = chain.step(rows.open_second, input_f, mixed_out.wait(), gains)
    g1.wait1()
    g0.wait2()
    g2.start1()
    rows_n = RowGather(wires, chain, v)
    g1.start2()
    g2.wait1()
    g1.wait2()
    g3.start1()
    g2.start2()
    normed_second = rows_n.wait()
    forward_gu(0)
    grads[0].odd()
    g3.wait1()
    g2.wait2()
    g3.start2()
    forward_gu(1)
    grads[0].start1()
    forward_gu(2)
    second = chain.step(lambda y, p: back(y, p, f32), grads_gu, [g.pair for g in gus[:3]])
    g3.wait2()
    forward_gu(3)
    second = chain.step(lambda y, p, s: back([y], [p], bf16, s), grads_gu[3], g3.pair, second)
    grads[1].odd()
    grads[0].wait1()
    sum_second = RowSum(wires, chain, second)
    grads[1].start1()
    grads[0].start2()
    grads[2].odd()
    acts = [jnp.concatenate(acts[k * per : (k + 1) * per], axis=1) for k in range(n_down)]
    grads += [Grad(wires, chain, sides, grad_half, a) for a in acts]
    grads[3].odd()
    grads[1].wait1()
    grads[0].wait2()
    grads[2].start1()
    grads[1].start2()
    mlp_part = chain.step(lambda y, p: back(y, p, bf16), acts, [d0.pair, d1.pair])
    grads[4].odd()
    grads[2].wait1()
    grads[1].wait2()
    part_gain_mlp, grad_middle, v = chain.step(
        rows.close_second, sum_second.wait(), gains, middle, scale_second, grad_rows
    )
    rows_m = RowGather(wires, chain, v)
    grads[3].start1()
    grads[2].start2()
    grads[5].odd()
    grads[3].wait1()
    grads[2].wait2()
    grads[4].start1()
    grads[3].start2()
    grads[4].wait1()
    grads[3].wait2()
    grads[5].start1()
    mlp = RowSum(wires, chain, mlp_part)
    grads[4].start2()
    middle_half = rows_m.wait()
    grads.append(Grad(wires, chain, sides, middle_half, attn_flat))
    grads[6].odd()
    grad_mixed = chain.step(lambda x, p: product(x, p, bf16), middle_half, w_o.pair)
    grads[5].wait1()
    grads[4].wait2()
    grads[6].start1()
    grads[5].start2()
    grad_proj = chain.step(lambda *a: attend_back(*a), *table, saved, grad_mixed)
    grads += [Grad(wires, chain, sides, normed_first, g) for g in grad_proj]
    grads[7].odd()
    first = chain.step(
        lambda y, p: back(y, p, bf16), grad_proj, [w_q.pair, w_k.pair, w_v.pair]
    )
    grads[6].wait1()
    grads[5].wait2()
    grads[7].start1()
    sum_first = RowSum(wires, chain, first)
    grads[6].start2()
    grads[8].odd()
    grads[9].odd()

    def gain_open(part):
        total = jnp.concatenate([part, part_gain_mlp]).reshape(2, dp, kb)
        mine, theirs = total[:, 0::2], total[:, 1::2]
        low = jnp.where(side == 0, mine, theirs)
        high = jnp.where(side == 0, theirs, mine)
        return jnp.stack([low, high], axis=2).reshape(2, dp, kb)

    def gain_start(bit):
        nonlocal total, got
        rows = total.shape[1] // 2
        got = wires.over_dp(*chain.pin(total[:, rows:]), bit)
        total = total[:, :rows]

    def gain_wait():
        nonlocal total
        total = total + chain.wait(got)

    def place_gu(ref, parts):
        for k, p in enumerate(parts):
            ref[:, 0, k * cg : (k + 1) * cg] = p[:, :cg]
            ref[:, 1, k * cg : (k + 1) * cg] = p[:, cg:]

    def place_rows(ref, parts):
        n = parts[0].shape[1]
        for k, p in enumerate(parts):
            ref[k * n : (k + 1) * n] = p.T

    def place_stack(ref, parts):
        for k, p in enumerate(parts):
            ref[k] = p

    def lay(which, shape, axis, place):
        block = tuple(n // 2 if a == axis else n for a, n in enumerate(shape))
        return chain.step(
            lambda t: laid_out(sides, t, shape, block, axis, place), [grads[i].terms for i in which]
        )

    grads[7].wait1()
    grads[6].wait2()
    grads[8].start1()
    grads[7].start2()
    layer_out = chain.step(rows.close_layer, mlp.wait(), middle)
    grad_gate_up = lay((0, 1, 2, 3), (kb, 2, 2 * ff), 2, place_gu)
    grads[8].wait1()
    grads[7].wait2()
    grads[9].start1()
    grads[8].start2()
    grad_down = lay((4, 5), (2 * ff, kb), 0, place_rows)
    grad_out = lay((6,), (2 * cols, kb), 0, place_rows)
    grads[9].wait1()
    grads[8].wait2()
    grads[9].start2()
    part_gain_attn, grad_in = chain.step(
        rows.close_first, sum_first.wait(), gains, input_f, scale_first, grad_middle
    )
    total = gain_open(part_gain_attn)
    for bit in [NEAR] + wires.far[::-1] + [PAIR]:
        gain_start(bit)
        gain_wait()
    total = total[:, 0]
    total = total + chain.wait(wires.over_tensor(*chain.pin(total), 1))
    total = total + chain.wait(wires.over_tensor(*chain.pin(total), 2))
    grads[9].wait2()
    grad_qkv = lay((7, 8, 9), (3, kb, 2 * cols), 2, place_stack)
    return (layer_out, grad_in, total[0], grad_qkv, grad_out, total[1], grad_gate_up, grad_down)


def solution(mesh):
    placed = (
        P(("dp", "tensor"), None),
        P(("dp", "tensor"), None),
        P("dp"),
        P("dp"),
        P(None, "dp", "tensor"),
        P("tensor", "dp"),
        P("dp"),
        P("dp", None, "tensor"),
        P("tensor", "dp"),
    )
    dp, tp = mesh.shape["dp"], mesh.shape["tensor"]

    def body(*args):
        return on_device(dp, tp, *args)

    return jax.shard_map(
        body,
        mesh=mesh,
        in_specs=placed,
        out_specs=(
            P(("dp", "tensor"), None),
            P(("dp", "tensor"), None),
            P("dp"),
            P(None, "dp", "tensor"),
            P("tensor", "dp"),
            P("dp"),
            P("dp", None, "tensor"),
            P("tensor", "dp"),
        ),
        check_vma=False,
    )
```

time: 1400 us -> 929 us (0.66)
  waiting for transfers between devices: 790 us -> 366 us
  Pallas kernels: 0 us -> 324 us
  matrix products: 172 us -> 0 us
  local copies, waits for them, and re-layouts: 199 us -> 57.9 us
  other arithmetic: 67.5 us -> 2.04 us
    ppermute x93 -> x87, waiting for transfers between devices: 700 us -> 321 us  [over_dp(): return lax.ppermute(value, AXES, pairs)]
    pallas_call x0 -> x67, Pallas kernels: none -> 324 us  [run(): pl.pallas_call(kernel, out_shape=[jax.ShapeDtypeStruct(s, t) for s, t in...]
    dot_general x26 -> x0, matrix products: 172 us -> none  [the longest x18 123 us: mix(): return jnp.einsum(form, left, right, preferred_element_type=f32)]
    unnamed x376 -> x228, local copies, waits for them, and re-layouts: 130 us -> 31.6 us
    ppermute x50 -> x2, waiting for transfers between devices: 89.4 us -> 2.73 us  [over_tensor(): return lax.ppermute(value, AXES, pairs)]
    another operation x17 -> x4, local copies, waits for them, and re-layouts: 27.5 us -> 4.3 us  [the longest x1 1.96 us: on_device(): jnp.tile(jnp.concatenate([jnp.cos(angles), jnp.cos(angles)], axis=1), (1,...]
    reduce_scatter x0 -> x4, waiting for transfers between devices: none -> 23 us  [__init__(): lax.psum_scatter(*chain.pin(value), AXES, scatter_dimension=0, tiled=True...]
    convert_element_type x15 -> x1, other arithmetic: 20.2 us -> 0.01 us  [on_device(): angles = positions.astype(f32)[:, None] * frequency[None, :]]
  transfers between devices with their start and end apart: 143 -> 97, of which waited for: 60 -> 55; matrix products, arithmetic and copies ran while one was open for 20% -> 3% of each run, Pallas kernels for 0% -> 33%
where the time goes in v3:
time: 929 us; the launch traced here: 921 us
  waiting for transfers between devices  366 us (39%)
  Pallas kernels  324 us (35%)
  starting transfers between devices  154 us (17%)
  local copies, waits for them, and re-layouts  57.9 us (6%)
  between operations  17.1 us (2%)
    pallas_call x67, Pallas kernels, run(): pl.pallas_call(kernel, out_shape=[jax.ShapeDtypeStruct(s, t) for s, t in...  324 us
    ppermute x87, waiting for transfers between devices, over_dp(): return lax.ppermute(value, AXES, pairs)  321 us
    ppermute x87, starting transfers between devices, over_dp(): return lax.ppermute(value, AXES, pairs)  134 us
    unnamed x228, local copies, waits for them, and re-layouts  31.6 us
    reduce_scatter x4, waiting for transfers between devices, __init__(): lax.psum_scatter(*chain.pin(value), AXES, scatter_dimension=0, tiled=True...  23 us
    all_gather x4, waiting for transfers between devices, __init__(): lax.all_gather(*chain.pin(value), AXES, axis=0, tiled=True, axis_index_gr...  19.9 us
  transfers between devices with their start and end apart: 97, of which 55 were waited for; matrix products, arithmetic and copies ran while one was open for 3% of the time, Pallas kernels for 33%

profile of v3, /device:TPU:0, one launch (start us, length us, event | category | flops | bytes accessed | tf_op | source)
XLA Modules:
  0.0 921.1 jit_solution(6355108327318479829)
XLA Ops:
  75.8 8.7 collective-permute-done.7.refs_1_
  102.1 7.3 product.6.q_ref
  119.4 8.8 collective-permute-done.14.refs_3_
  145.8 12.0 %collective-permute-done.17.refs_2_ = bf16[384,384]{1,0:T(8,128)(2,1)S(1)} collective-permute-done((bf16[384,384]{1,0:T(8,128)(2,1)S(1)}, bf16[384,384]{1,0:T(8,128)(2,1)S(1)}, u32[]{:S(2)}, u32[]{:S(2)}) %collective-permute-start.17) | collective-permute-done | bytes 294944 | tf_op jit(solution)/shard_map/ppermute | solution.py:461
  165.4 7.2 product.8.v_ref
  176.2 14.9 %attend.1 = (bf16[1024,384]{1,0:T(8,128)(2,1)S(1)}, bf16[1024,384]{1,0:T(8,128)(2,1)}, bf16[1024,384]{1,0:T(8,128)(2,1)}, bf16[1024,384]{1,0:T(8,128)(2,1)}, f32[1024,4]{1,0:T(8,128)S(1)}) custom-call(s32[2]{0:T(128)S(1)} %copy-done.80, s32[512,1]{1,0:T(8,128)S(1)} %copy.25.rows_ref, s32[1,512]{1,0:T(1,128)S(1)} %bitcast.74, f32[512,384]{1,0:T(8,128)} %copy.26.cos_ref, ...), custom_call_target="tpu_custom_call" | custom-call | flops 1 | bytes 1 | tf_op jit(solution)/shard_map/attend/pallas_call | solution.py:152
  208.2 20.2 %collective-permute-done.23.refs_1_ = bf16[384,512]{1,0:T(8,128)(2,1)} collective-permute-done((bf16[384,512]{1,0:T(8,128)(2,1)S(1)}, bf16[384,512]{1,0:T(8,128)(2,1)}, u32[]{:S(2)}, u32[]{:S(2)}) %collective-permute-start.23) | collective-permute-done | bytes 393248 | tf_op jit(solution)/shard_map/ppermute | solution.py:461
  243.9 7.4 product.9.ga_ref
  251.3 16.8 %collective-permute-done.28.refs_1_ = bf16[384,512]{1,0:T(8,128)(2,1)S(1)} collective-permute-done((bf16[384,512]{1,0:T(8,128)(2,1)S(1)}, bf16[384,512]{1,0:T(8,128)(2,1)S(1)}, u32[]{:S(2)}, u32[]{:S(2)}) %collective-permute-start.28) | collective-permute-done | bytes 393248 | tf_op jit(solution)/shard_map/ppermute | solution.py:461
  284.0 7.4 product.10.ga_ref
  291.4 21.6 %reduce-scatter.5.cloned.1.call-done.got_ref = bf16[128,3072]{1,0:T(8,128)(2,1)} async-done(((bf16[1024,3072]{1,0:T(8,128)(2,1)}), bf16[128,3072]{1,0:T(8,128)(2,1)}) %reduce-scatter.5.cloned.1.call-update) | async-done | bytes 786448 | tf_op jit(solution)/shard_map/reduce_scatter | solution.py:610
  322.8 18.0 %collective-permute-done.35.refs_1_ = bf16[384,512]{1,0:T(8,128)(2,1)S(1)} collective-permute-done((bf16[384,512]{1,0:T(8,128)(2,1)S(1)}, bf16[384,512]{1,0:T(8,128)(2,1)S(1)}, u32[]{:S(2)}, u32[]{:S(2)}) %collective-permute-start.35) | collective-permute-done | bytes 393248 | tf_op jit(solution)/shard_map/ppermute | solution.py:461
  340.8 9.7 %collective-permute-done.36.refs_2_ = bf16[384,512]{1,0:T(8,128)(2,1)S(1)} collective-permute-done((bf16[384,512]{1,0:T(8,128)(2,1)S(1)}, bf16[384,512]{1,0:T(8,128)(2,1)S(1)}, u32[]{:S(2)}, u32[]{:S(2)}) %collective-permute-start.36) | collective-permute-done | bytes 393248 | tf_op jit(solution)/shard_map/ppermute | solution.py:461
  350.5 13.6 %collective-permute-done.37.refs_3_ = bf16[384,512]{1,0:T(8,128)(2,1)S(1)} collective-permute-done((bf16[384,512]{1,0:T(8,128)(2,1)S(1)}, bf16[384,512]{1,0:T(8,128)(2,1)S(1)}, u32[]{:S(2)}, u32[]{:S(2)}) %collective-permute-start.37) | collective-permute-done | bytes 393248 | tf_op jit(solution)/shard_map/ppermute | solution.py:461
  372.7 19.9 %all-gather.9.cloned.1.call-done.x_ref = bf16[1024,3072]{1,0:T(8,128)(2,1)} async-done(((bf16[128,3072]{1,0:T(8,128)(2,1)}), bf16[1024,3072]{1,0:T(8,128)(2,1)}) %all-gather.9.cloned.1.call-update) | async-done | bytes 6291472 | tf_op jit(solution)/shard_map/all_gather | solution.py:599
  424.8 16.3 %back.6.refs_3_ = f32[1024,3072]{1,0:T(8,128)} custom-call(bf16[1024,512]{1,0:T(8,128)(2,1)S(1)} %get-tuple-element.791.y_ref.refs_0_, bf16[1024,512]{1,0:T(8,128)(2,1)} %copy-done.10, bf16[1024,512]{1,0:T(8,128)(2,1)} %copy-done.7, bf16[1536,512]{1,0:T(8,128)(2,1)} %in_order.16.even.refs_3_, bf16[1536,512]{1,0:T(8,128)(2,1)} %collective-permute-done.31.odd.refs_4_, ...), custom_call_target="tpu_custom_call" | custom-call | flops 1 | bytes 1 | tf_op jit(solution)/shard_map/back/pallas_call | solution.py:152
  453.0 10.5 %back.7 = bf16[1024,3072]{1,0:T(8,128)(2,1)} custom-call(bf16[1024,512]{1,0:T(8,128)(2,1)S(1)} %get-tuple-element.874.refs_0_.y_ref, bf16[1536,512]{1,0:T(8,128)(2,1)} %in_order.19.even.refs_1_, bf16[1536,512]{1,0:T(8,128)(2,1)} %copy-done.90, f32[1024,3072]{1,0:T(8,128)} %back.6.refs_3_), custom_call_target="tpu_custom_call" | custom-call | flops 1 | bytes 1 | tf_op jit(solution)/shard_map/back/pallas_call | solution.py:152
  467.8 9.5 %collective-permute-done.44.g_ref = bf16[1536,512]{1,0:T(8,128)(2,1)} collective-permute-done((bf16[1536,512]{1,0:T(8,128)(2,1)}, bf16[1536,512]{1,0:T(8,128)(2,1)}, u32[]{:S(2)}, u32[]{:S(2)}) %collective-permute-start.44) | collective-permute-done | bytes 1572896 | tf_op jit(solution)/shard_map/ppermute | solution.py:461
  497.7 16.3 %collective-permute-done.45.g_ref = bf16[1536,512]{1,0:T(8,128)(2,1)S(1)} collective-permute-done((bf16[1536,512]{1,0:T(8,128)(2,1)}, bf16[1536,512]{1,0:T(8,128)(2,1)S(1)}, u32[]{:S(2)}, u32[]{:S(2)}) %collective-permute-start.45) | collective-permute-done | bytes 1572896 | tf_op jit(solution)/shard_map/ppermute | solution.py:461
  514.1 8.0 collective-permute-done.46.refs_1_
  536.0 11.5 %back.8 = bf16[1024,3072]{1,0:T(8,128)(2,1)} custom-call(bf16[1024,512]{1,0:T(8,128)(2,1)S(1)} %constant_dynamic-update-slice_fusion.refs_0_.y_ref, bf16[1024,512]{1,0:T(8,128)(2,1)} %copy-done, bf16[1536,512]{1,0:T(8,128)(2,1)} %in_order.14.even.refs_2_, bf16[1536,512]{1,0:T(8,128)(2,1)} %collective-permute-done.26.odd.refs_3_, ...), custom_call_target="tpu_custom_call" | custom-call | flops 1 | bytes 1 | tf_op jit(solution)/shard_map/back/pallas_call | solution.py:152
  557.6 9.0 collective-permute-done.49.refs_5_
  588.2 17.2 %collective-permute-done.53.g_ref = bf16[1536,512]{1,0:T(8,128)(2,1)S(1)} collective-permute-done((bf16[1536,512]{1,0:T(8,128)(2,1)}, bf16[1536,512]{1,0:T(8,128)(2,1)S(1)}, u32[]{:S(2)}, u32[]{:S(2)}) %collective-permute-start.53) | collective-permute-done | bytes 1572896 | tf_op jit(solution)/shard_map/ppermute | solution.py:461
  605.4 7.3 collective-permute-done.56.refs_11_
  618.8 7.2 collective-permute-done.54.refs_9_
  641.2 10.6 %collective-permute-done.60.g_ref = bf16[1536,512]{1,0:T(8,128)(2,1)S(1)} collective-permute-done((bf16[1536,512]{1,0:T(8,128)(2,1)S(1)}, bf16[1536,512]{1,0:T(8,128)(2,1)S(1)}, u32[]{:S(2)}, u32[]{:S(2)}) %collective-permute-start.60) | collective-permute-done | bytes 1572896 | tf_op jit(solution)/shard_map/ppermute | solution.py:461
  653.8 10.5 %collective-permute-done.57.refs_13_ = bf16[384,512]{1,0:T(8,128)(2,1)} collective-permute-done((bf16[384,512]{1,0:T(8,128)(2,1)S(1)}, bf16[384,512]{1,0:T(8,128)(2,1)}, u32[]{:S(2)}, u32[]{:S(2)}) %collective-permute-start.57) | collective-permute-done | bytes 393248 | tf_op jit(solution)/shard_map/ppermute | solution.py:461
  695.0 9.3 %collective-permute-done.62.refs_1_ = bf16[384,512]{1,0:T(8,128)(2,1)} collective-permute-done((bf16[384,512]{1,0:T(8,128)(2,1)}, bf16[384,512]{1,0:T(8,128)(2,1)}, u32[]{:S(2)}, u32[]{:S(2)}) %collective-permute-start.62) | collective-permute-done | bytes 393248 | tf_op jit(solution)/shard_map/ppermute | solution.py:461
  719.1 17.1 %attend_back.1 = (bf16[1024,384]{1,0:T(8,128)(2,1)S(1)}, bf16[1024,384]{1,0:T(8,128)(2,1)}, bf16[1024,384]{1,0:T(8,128)(2,1)}) custom-call(s32[2]{0:T(128)S(1)} %copy-done.81, s32[512,1]{1,0:T(8,128)S(1)} %copy.28.rows_ref, s32[1,512]{1,0:T(1,128)S(1)} %bitcast.76, f32[512,384]{1,0:T(8,128)} %copy.29.cos_ref, f32[512,384]{1,0:T(8,128)} %copy.30.sin_ref, ...), custom_call_target="tpu_custom_call" | custom-call | flops 1 | bytes 1 | tf_op jit(solution)/shard_map/attend_back/pallas_call | solution.py:152
  740.9 15.0 %back.9 = bf16[1024,3072]{1,0:T(8,128)(2,1)} custom-call(bf16[1024,384]{1,0:T(8,128)(2,1)S(1)} %get-tuple-element.990.y_ref.refs_0_, bf16[1024,384]{1,0:T(8,128)(2,1)S(1)} %copy-done.18, bf16[1024,384]{1,0:T(8,128)(2,1)} %get-tuple-element.1062.refs_2_.y_ref, bf16[1536,384]{1,0:T(8,128)(2,1)} %in_order.10.even.refs_3_, ...), custom_call_target="tpu_custom_call" | custom-call | flops 1 | bytes 1 | tf_op jit(solution)/shard_map/back/pallas_call | solution.py:152
  880.0 8.1 collective-permute-done.83
  889.3 18.4 %collective-permute-start.85 = (f32[2,384]{1,0:T(2,128)S(1)}, f32[2,384]{1,0:T(2,128)S(1)}, u32[]{:S(2)}, u32[]{:S(2)}) collective-permute-start(f32[2,384]{1,0:T(2,128)S(1)} %add.56), channel_id=1, source_target_pairs={{0,2},{1,3},{2,0},{3,1},{4,6},{5,7},{6,4},{7,5},{8,10},{9,11},{10,... | collective-permute-start | bytes 9224 | tf_op jit(solution)/shard_map/ppermute | solution.py:468
  (511 shorter events, 508.7 us)
Async XLA Ops:
  7.2 95.0 %all-gather.5.cloned.1.call-start = ((), (), s32[]{:S(2)}) async-start(), calls=%async_computation.4 | async-start | bytes 7077888 | tf_op jit(solution)/shard_map/all_gather | solution.py:599
  25.6 182.7 %all-gather.7.cloned.1.call-start = ((), (), s32[]{:S(2)}) async-start(), calls=%async_computation.6 | async-start | bytes 7077888 | tf_op jit(solution)/shard_map/all_gather | solution.py:599
  30.8 36.2 %collective-permute-start.5 = (bf16[384,384]{1,0:T(8,128)(2,1)}, bf16[384,384]{1,0:T(8,128)(2,1)S(1)}, u32[]{:S(2)}, u32[]{:S(2)}) collective-permute-start(bf16[384,384]{1,0:T(8,128)(2,1)} %get-tuple-element.577), channel_id=1, source_target_pairs={{0,24},{1,25},{2,26},{3,27},{4,28},{5,29},{6,30},{7,31},{8,16},{9,... | collective-permute-start | bytes 884744 | tf_op jit(solution)/shard_map/ppermute | solution.py:461
  33.2 33.7 %collective-permute-start.6 = (bf16[384,384]{1,0:T(8,128)(2,1)}, bf16[384,384]{1,0:T(8,128)(2,1)S(1)}, u32[]{:S(2)}, u32[]{:S(2)}) collective-permute-start(bf16[384,384]{1,0:T(8,128)(2,1)} %get-tuple-element.577), channel_id=1, source_target_pairs={{0,8},{1,9},{2,10},{3,11},{4,12},{5,13},{6,14},{7,15},{8,0},{9,1},... | collective-permute-start | bytes 884744 | tf_op jit(solution)/shard_map/ppermute | solution.py:461
  68.6 244.4 %reduce-scatter.5.cloned.1.call-start = ((), (), s32[]{:S(2)}) async-start(), calls=%async_computation.5 | async-start | bytes 7077888 | tf_op jit(solution)/shard_map/reduce_scatter | solution.py:610
  160.5 38.3 %collective-permute-start.20 = (bf16[384,512]{1,0:T(8,128)(2,1)S(1)}, bf16[384,512]{1,0:T(8,128)(2,1)S(1)}, u32[]{:S(2)}, u32[]{:S(2)}) collective-permute-start(bf16[384,512]{1,0:T(8,128)(2,1)S(1)} %get-tuple-element.657.refs_0_), channel_id=1, source_target_pairs={{0,16},{1,17},{2,18},{3,19},{4,20},{5,21},{6,22},{7,23},{8,24},{9,... | collective-permute-start | bytes 1179656 | tf_op jit(solution)/shard_map/ppermute | solution.py:461
  163.8 35.0 %collective-permute-start.21 = (bf16[384,512]{1,0:T(8,128)(2,1)}, bf16[384,512]{1,0:T(8,128)(2,1)S(1)}, u32[]{:S(2)}, u32[]{:S(2)}) collective-permute-start(bf16[384,512]{1,0:T(8,128)(2,1)} %get-tuple-element.650), channel_id=1, source_target_pairs={{0,24},{1,25},{2,26},{3,27},{4,28},{5,29},{6,30},{7,31},{8,16},{9,... | collective-permute-start | bytes 1179656 | tf_op jit(solution)/shard_map/ppermute | solution.py:461
  198.9 193.7 %all-gather.9.cloned.1.call-start = ((), (), s32[]{:S(2)}) async-start(), calls=%async_computation.7 | async-start | bytes 7077888 | tf_op jit(solution)/shard_map/all_gather | solution.py:599
  238.5 37.2 %collective-permute-start.27 = (bf16[1536,512]{1,0:T(8,128)(2,1)}, bf16[1536,512]{1,0:T(8,128)(2,1)S(1)}, u32[]{:S(2)}, u32[]{:S(2)}) collective-permute-start(bf16[1536,512]{1,0:T(8,128)(2,1)} %in_order.15.even.refs_4_), channel_id=1, source_target_pairs={{0,4},{1,5},{2,6},{3,7},{4,0},{5,1},{6,2},{7,3},{8,12},{9,13},{10,... | collective-permute-start | bytes 4718600 | tf_op jit(solution)/shard_map/ppermute | solution.py:461
  277.7 39.5 %collective-permute-start.31 = (bf16[1536,512]{1,0:T(8,128)(2,1)}, bf16[1536,512]{1,0:T(8,128)(2,1)}, u32[]{:S(2)}, u32[]{:S(2)}) collective-permute-start(bf16[1536,512]{1,0:T(8,128)(2,1)} %in_order.16.even.refs_3_), channel_id=1, source_target_pairs={{0,4},{1,5},{2,6},{3,7},{4,0},{5,1},{6,2},{7,3},{8,12},{9,13},{10,... | collective-permute-start | bytes 4718600 | tf_op jit(solution)/shard_map/ppermute | solution.py:461
  279.1 38.1 %collective-permute-start.32 = (bf16[384,512]{1,0:T(8,128)(2,1)S(1)}, bf16[384,512]{1,0:T(8,128)(2,1)S(1)}, u32[]{:S(2)}, u32[]{:S(2)}) collective-permute-start(bf16[384,512]{1,0:T(8,128)(2,1)S(1)} %bitcast.65), channel_id=1, source_target_pairs={{0,16},{1,17},{2,18},{3,19},{4,20},{5,21},{6,22},{7,23},{8,24},{9,... | collective-permute-start | bytes 1179656 | tf_op jit(solution)/shard_map/ppermute | solution.py:461
  282.2 35.0 %collective-permute-start.33 = (bf16[384,512]{1,0:T(8,128)(2,1)}, bf16[384,512]{1,0:T(8,128)(2,1)S(1)}, u32[]{:S(2)}, u32[]{:S(2)}) collective-permute-start(bf16[384,512]{1,0:T(8,128)(2,1)} %bitcast.36), channel_id=1, source_target_pairs={{0,24},{1,25},{2,26},{3,27},{4,28},{5,29},{6,30},{7,31},{8,16},{9,... | collective-permute-start | bytes 1179656 | tf_op jit(solution)/shard_map/ppermute | solution.py:461
  317.3 249.4 %reduce-scatter.7.cloned.1.call-start = ((), (), s32[]{:S(2)}) async-start(), calls=%async_computation.8 | async-start | bytes 7077888 | tf_op jit(solution)/shard_map/reduce_scatter | solution.py:610
  319.0 45.0 %collective-permute-start.38 = (bf16[1536,512]{1,0:T(8,128)(2,1)}, bf16[1536,512]{1,0:T(8,128)(2,1)S(1)}, u32[]{:S(2)}, u32[]{:S(2)}) collective-permute-start(bf16[1536,512]{1,0:T(8,128)(2,1)} %in_order.17.even.refs_5_), channel_id=1, source_target_pairs={{0,4},{1,5},{2,6},{3,7},{4,0},{5,1},{6,2},{7,3},{8,12},{9,13},{10,... | collective-permute-start | bytes 4718600 | tf_op jit(solution)/shard_map/ppermute | solution.py:461
  320.5 43.6 %collective-permute-start.37 = (bf16[384,512]{1,0:T(8,128)(2,1)S(1)}, bf16[384,512]{1,0:T(8,128)(2,1)S(1)}, u32[]{:S(2)}, u32[]{:S(2)}) collective-permute-start(bf16[384,512]{1,0:T(8,128)(2,1)S(1)} %bitcast.90), channel_id=1, source_target_pairs={{0,8},{1,9},{2,10},{3,11},{4,12},{5,13},{6,14},{7,15},{8,0},{9,1},... | collective-permute-start | bytes 1179656 | tf_op jit(solution)/shard_map/ppermute | solution.py:461
  365.9 38.9 %collective-permute-start.42 = (bf16[1536,512]{1,0:T(8,128)(2,1)}, bf16[1536,512]{1,0:T(8,128)(2,1)}, u32[]{:S(2)}, u32[]{:S(2)}) collective-permute-start(bf16[1536,512]{1,0:T(8,128)(2,1)} %in_order.18.even.refs_7_), channel_id=1, source_target_pairs={{0,4},{1,5},{2,6},{3,7},{4,0},{5,1},{6,2},{7,3},{8,12},{9,13},{10,... | collective-permute-start | bytes 4718600 | tf_op jit(solution)/shard_map/ppermute | solution.py:461
  367.6 37.1 %collective-permute-start.39 = (bf16[384,512]{1,0:T(8,128)(2,1)S(1)}, bf16[384,512]{1,0:T(8,128)(2,1)S(1)}, u32[]{:S(2)}, u32[]{:S(2)}) collective-permute-start(bf16[384,512]{1,0:T(8,128)(2,1)S(1)} %bitcast.61), channel_id=1, source_target_pairs={{0,16},{1,17},{2,18},{3,19},{4,20},{5,21},{6,22},{7,23},{8,24},{9,... | collective-permute-start | bytes 1179656 | tf_op jit(solution)/shard_map/ppermute | solution.py:461
  370.4 34.3 %collective-permute-start.40 = (bf16[384,512]{1,0:T(8,128)(2,1)}, bf16[384,512]{1,0:T(8,128)(2,1)S(1)}, u32[]{:S(2)}, u32[]{:S(2)}) collective-permute-start(bf16[384,512]{1,0:T(8,128)(2,1)} %bitcast.44), channel_id=1, source_target_pairs={{0,24},{1,25},{2,26},{3,27},{4,28},{5,29},{6,30},{7,31},{8,16},{9,... | collective-permute-start | bytes 1179656 | tf_op jit(solution)/shard_map/ppermute | solution.py:461
  406.5 37.4 %collective-permute-start.43 = (bf16[1536,512]{1,0:T(8,128)(2,1)}, bf16[1536,512]{1,0:T(8,128)(2,1)S(1)}, u32[]{:S(2)}, u32[]{:S(2)}) collective-permute-start(bf16[1536,512]{1,0:T(8,128)(2,1)} %in_order.19.even.refs_1_), channel_id=1, source_target_pairs={{0,4},{1,5},{2,6},{3,7},{4,0},{5,1},{6,2},{7,3},{8,12},{9,13},{10,... | collective-permute-start | bytes 4718600 | tf_op jit(solution)/shard_map/ppermute | solution.py:461
  416.7 60.7 %collective-permute-start.44 = (bf16[1536,512]{1,0:T(8,128)(2,1)}, bf16[1536,512]{1,0:T(8,128)(2,1)}, u32[]{:S(2)}, u32[]{:S(2)}) collective-permute-start(bf16[1536,512]{1,0:T(8,128)(2,1)} %weight_part.10), channel_id=1, source_target_pairs={{0,4},{1,5},{2,6},{3,7},{4,0},{5,1},{6,2},{7,3},{8,12},{9,13},{10,... | collective-permute-start | bytes 4718600 | tf_op jit(solution)/shard_map/ppermute | solution.py:461
  477.4 199.1 %all-gather.11.cloned.1.call-start = ((), (), s32[]{:S(2)}) async-start(), calls=%async_computation.10 | async-start | bytes 7077888 | tf_op jit(solution)/shard_map/all_gather | solution.py:599
  477.6 36.3 %collective-permute-start.45 = (bf16[1536,512]{1,0:T(8,128)(2,1)}, bf16[1536,512]{1,0:T(8,128)(2,1)S(1)}, u32[]{:S(2)}, u32[]{:S(2)}) collective-permute-start(bf16[1536,512]{1,0:T(8,128)(2,1)} %weight_part.11), channel_id=1, source_target_pairs={{0,4},{1,5},{2,6},{3,7},{4,0},{5,1},{6,2},{7,3},{8,12},{9,13},{10,... | collective-permute-start | bytes 4718600 | tf_op jit(solution)/shard_map/ppermute | solution.py:461
  487.2 34.9 %collective-permute-start.46 = (bf16[384,512]{1,0:T(8,128)(2,1)S(1)}, bf16[384,512]{1,0:T(8,128)(2,1)S(1)}, u32[]{:S(2)}, u32[]{:S(2)}) collective-permute-start(bf16[384,512]{1,0:T(8,128)(2,1)S(1)} %get-tuple-element.800), channel_id=1, source_target_pairs={{0,16},{1,17},{2,18},{3,19},{4,20},{5,21},{6,22},{7,23},{8,24},{9,... | collective-permute-start | bytes 1179656 | tf_op jit(solution)/shard_map/ppermute | solution.py:461
  572.8 225.2 %reduce-scatter.9.cloned.1.call-start = ((), (), s32[]{:S(2)}) async-start(), calls=%async_computation.9 | async-start | bytes 7077888 | tf_op jit(solution)/shard_map/reduce_scatter | solution.py:610
  580.4 37.6 %collective-permute-start.55 = (bf16[384,512]{1,0:T(8,128)(2,1)S(1)}, bf16[384,512]{1,0:T(8,128)(2,1)S(1)}, u32[]{:S(2)}, u32[]{:S(2)}) collective-permute-start(bf16[384,512]{1,0:T(8,128)(2,1)S(1)} %get-tuple-element.861), channel_id=1, source_target_pairs={{0,24},{1,25},{2,26},{3,27},{4,28},{5,29},{6,30},{7,31},{8,16},{9,... | collective-permute-start | bytes 1179656 | tf_op jit(solution)/shard_map/ppermute | solution.py:461
  583.0 42.9 %collective-permute-start.54 = (bf16[384,512]{1,0:T(8,128)(2,1)S(1)}, bf16[384,512]{1,0:T(8,128)(2,1)}, u32[]{:S(2)}, u32[]{:S(2)}) collective-permute-start(bf16[384,512]{1,0:T(8,128)(2,1)S(1)} %get-tuple-element.860), channel_id=1, source_target_pairs={{0,16},{1,17},{2,18},{3,19},{4,20},{5,21},{6,22},{7,23},{8,24},{9,... | collective-permute-start | bytes 1179656 | tf_op jit(solution)/shard_map/ppermute | solution.py:461
  664.3 191.4 %reduce-scatter.11.cloned.1.call-start = ((), (), s32[]{:S(2)}) async-start(), calls=%async_computation.11 | async-start | bytes 7077888 | tf_op jit(solution)/shard_map/reduce_scatter | solution.py:610
  704.3 51.6 %collective-permute-start.68 = (bf16[1536,384]{1,0:T(8,128)(2,1)}, bf16[1536,384]{1,0:T(8,128)(2,1)}, u32[]{:S(2)}, u32[]{:S(2)}) collective-permute-start(bf16[1536,384]{1,0:T(8,128)(2,1)} %weight_part.16), channel_id=1, source_target_pairs={{0,4},{1,5},{2,6},{3,7},{4,0},{5,1},{6,2},{7,3},{8,12},{9,13},{10,... | collective-permute-start | bytes 3538952 | tf_op jit(solution)/shard_map/ppermute | solution.py:461
  713.1 42.8 %collective-permute-start.67 = (bf16[384,512]{1,0:T(8,128)(2,1)}, bf16[384,512]{1,0:T(8,128)(2,1)}, u32[]{:S(2)}, u32[]{:S(2)}) collective-permute-start(bf16[384,512]{1,0:T(8,128)(2,1)} %get-tuple-element.943), channel_id=1, source_target_pairs={{0,8},{1,9},{2,10},{3,11},{4,12},{5,13},{6,14},{7,15},{8,0},{9,1},... | collective-permute-start | bytes 1179656 | tf_op jit(solution)/shard_map/ppermute | solution.py:461
  713.1 42.8 %collective-permute-start.66 = (bf16[384,512]{1,0:T(8,128)(2,1)}, bf16[384,512]{1,0:T(8,128)(2,1)S(1)}, u32[]{:S(2)}, u32[]{:S(2)}) collective-permute-start(bf16[384,512]{1,0:T(8,128)(2,1)} %get-tuple-element.942), channel_id=1, source_target_pairs={{0,24},{1,25},{2,26},{3,27},{4,28},{5,29},{6,30},{7,31},{8,16},{9,... | collective-permute-start | bytes 1179656 | tf_op jit(solution)/shard_map/ppermute | solution.py:461
  715.0 40.9 %collective-permute-start.65 = (bf16[384,512]{1,0:T(8,128)(2,1)}, bf16[384,512]{1,0:T(8,128)(2,1)S(1)}, u32[]{:S(2)}, u32[]{:S(2)}) collective-permute-start(bf16[384,512]{1,0:T(8,128)(2,1)} %get-tuple-element.941), channel_id=1, source_target_pairs={{0,16},{1,17},{2,18},{3,19},{4,20},{5,21},{6,22},{7,23},{8,24},{9,... | collective-permute-start | bytes 1179656 | tf_op jit(solution)/shard_map/ppermute | solution.py:461
  874.7 34.5 %collective-permute-start.88 = (bf16[384,384]{1,0:T(8,128)(2,1)S(1)}, bf16[384,384]{1,0:T(8,128)(2,1)S(1)}, u32[]{:S(2)}, u32[]{:S(2)}) collective-permute-start(bf16[384,384]{1,0:T(8,128)(2,1)S(1)} %get-tuple-element.1086), channel_id=1, source_target_pairs={{0,8},{1,9},{2,10},{3,11},{4,12},{5,13},{6,14},{7,15},{8,0},{9,1},... | collective-permute-start | bytes 884744 | tf_op jit(solution)/shard_map/ppermute | solution.py:461
  (174 other events, 3188.4 us)
Sparse Core Ops, SparseCore 0:
  25.7 70.3 all-gather.4
  97.8 64.6 all-gather.6
  199.0 113.9 reduce-scatter.4
  317.4 75.1 all-gather.8
  477.5 87.6 reduce-scatter.6
  572.9 59.5 all-gather.10
  664.4 109.3 reduce-scatter.8
  776.1 79.5 reduce-scatter.10

commit v4 on v3

--- a/solution.py
+++ b/solution.py
@@ -61,9 +61,9 @@
 def attend_kernel(len_ref, rows_ref, cols_ref, cos_ref, sin_ref, q_ref, k_ref, v_ref,
                   o_ref, qo_ref, ko_ref, vo_ref, lse_ref):
     allowed = allowed_pairs(rows_ref, cols_ref, len_ref[pl.program_id(0)])
-    cosine, sine = cos_ref[...], sin_ref[...]
+    q, k = group_block(q_ref), group_block(k_ref)
+    cosine, sine = (jnp.concatenate([r[...]] * (q.shape[1] // HEAD_DIM), axis=1) for r in (cos_ref, sin_ref))
     low = low_lanes(cosine.shape)
-    q, k = group_block(q_ref), group_block(k_ref)
     q = q * cosine + turned(q, low) * sine
     k = k * cosine + turned(k, low) * sine
     v = group_block(v_ref)
@@ -100,7 +100,7 @@
         dqs.append(jnp.dot(ds, kh, preferred_element_type=f32))
         dks.append(dot_first(ds, qh))
         dvs.append(dot_first(prob.astype(bf16), gh))
-    cosine, sine = cos_ref[...], sin_ref[...]
+    cosine, sine = (jnp.concatenate([r[...]] * (q.shape[1] // HEAD_DIM), axis=1) for r in (cos_ref, sin_ref))
     low = low_lanes(cosine.shape)
     for ref, parts in ((dq_ref, dqs), (dk_ref, dks)):
         u = jnp.concatenate(parts, axis=1)
@@ -110,11 +110,11 @@
 
 def attend_specs(group_rows, cols, lanes):
     tall = pl.BlockSpec((group_rows, cols), lambda g: (g, 0))
-    table = pl.BlockSpec((group_rows, cols), lambda g: (0, 0))
+    table = pl.BlockSpec((group_rows, HEAD_DIM), lambda g: (g, 0))
     head = [
         pl.BlockSpec(memory_space=pltpu.SMEM),
-        pl.BlockSpec((group_rows, 1), lambda g: (0, 0)),
-        pl.BlockSpec((1, group_rows), lambda g: (0, 0)),
+        pl.BlockSpec((group_rows, 1), lambda g: (g, 0)),
+        pl.BlockSpec((1, group_rows), lambda g: (0, g)),
         table,
         table,
     ]
@@ -212,48 +212,92 @@
     )
 
 
-def back(ys, pairs, dtype, part=None):
+def back(ys, pairs, dtype, part=None, turn=True, normed=None):
     rows = ys[0].shape[0]
     k = pairs[0][0].shape[0]
     count = len(ys)
     tile = rows // 4
+    extra = [a for a in (part, normed) if a is not None]
+    more = len(extra)
 
     def kernel(*refs):
-        y_refs, w_refs, out = refs[:count], refs[count : 3 * count], refs[-1]
+        y_refs, w_refs, out = refs[:count], refs[count : 3 * count], refs[3 * count + more]
         for s in range(2):
             c = slice(s * k, (s + 1) * k)
             total = refs[3 * count][:, c] if part is not None else None
             for y, w in zip(y_refs, w_refs[s::2]):
                 term = dot_last(y[...], w[...])
                 total = term if total is None else total + term
-            out[:, c] = total.astype(dtype)
+            if normed is not None:
+                sums = jnp.sum(total * refs[3 * count][:, c].astype(f32), axis=0, keepdims=True)
+
+                @pl.when(pl.program_id(0) == 0)
+                def _():
+                    refs[-1][:, c] = sums
+
+                @pl.when(pl.program_id(0) > 0)
+                def _():
+                    refs[-1][:, c] += sums
+
+            total = total.astype(dtype)
+            if not turn:
+                out[:, c] = total
+                continue
+
+            i = pl.program_id(0)
+            swapped = (i == 1) | (i == 2)
+
+            @pl.when(jnp.logical_not(swapped))
+            def _():
+                out[:, c] = total
+
+            @pl.when(swapped)
+            def _():
+                out[: tile // 2, c] = total[tile // 2 :]
+                out[tile // 2 :, c] = total[: tile // 2]
 
     flat = [w for p in pairs for w in p]
-    return run(
-        kernel, "back", [((rows, 2 * k), dtype)], [*ys, *flat] + ([] if part is None else [part]), (4,),
-        [tiles(tile, y.shape[1]) for y in ys]
-        + [still(w.shape) for w in flat]
-        + ([] if part is None else [tiles(tile, 2 * k)]),
-        [tiles(tile, 2 * k)],
+    outs = [((rows, 2 * k), dtype)] + ([] if normed is None else [((1, 2 * k), f32)])
+    got = run(
+        kernel, "back", outs, [*ys, *flat, *extra], (4,),
+        [tiles(tile, y.shape[1]) for y in ys] + [still(w.shape) for w in flat] + [tiles(tile, 2 * k)] * more,
+        [
+            pl.BlockSpec((tile, 2 * k), lambda i: (jnp.where(i < 2, i, 5 - i) if turn else i, 0)),
+            pl.BlockSpec((1, 2 * k), lambda i: (0, 0)),
+        ][: len(outs)],
+    )
+    return got[0] if normed is None else got
+
+
+def side_by_side(side, mine, theirs):
+    rows, n = mine.shape
+
+    def kernel(side_ref, a, b, out):
+        for q, ref in enumerate((a, b)):
+
+            @pl.when(pl.program_id(0) == q)
+            def _(ref=ref):
+                out[...] = ref[...].reshape(1, rows, n)
+
+    whole = pl.BlockSpec((rows, n), lambda i, s: (0, 0))
+    return run(
+        kernel, "side_by_side", [((2, rows, n), bf16)], [side, mine, theirs], (2,), [whole] * 2,
+        [pl.BlockSpec((1, rows, n), lambda i, s: (i ^ s[0], 0, 0))], scalars=1,
     )[0]
 
 
-def weight_part(x, y, first, count, dtype, got=None, got_first=0):
+def weight_part(x, y, first, count, dtype):
     rows = x.shape[0]
     n = y.shape[1]
     tile = count if count <= 768 else count // 2
-    base, got_base = first // tile, got_first // tile
-
-    def kernel(x_ref, y_ref, *rest):
-        total = dot_first(x_ref[...], y_ref[...])
-        if got is not None:
-            total += rest[0][...].astype(f32)
-        rest[-1][...] = total.astype(dtype)
-
-    extra = [] if got is None else [pl.BlockSpec((tile, n), lambda i: (i + got_base, 0))]
-    return run(
-        kernel, "weight_part", [((count, n), dtype)], [x, y] + ([] if got is None else [got]), (count // tile,),
-        [pl.BlockSpec((rows, tile), lambda i: (0, i + base)), still(y.shape)] + extra, [tiles(tile, n)],
+    base = first // tile
+
+    def kernel(x_ref, y_ref, out):
+        out[...] = dot_first(x_ref[...], y_ref[...]).astype(dtype)
+
+    return run(
+        kernel, "weight_part", [((count, n), dtype)], [x, y], (count // tile,),
+        [pl.BlockSpec((rows, tile), lambda i: (0, i + base)), still(y.shape)], [tiles(tile, n)],
     )[0]
 
 
@@ -332,11 +376,12 @@
             kernel, "open_second", self.outs(f32) + [((self.rows, 1), f32)] + self.outs(bf16), [x, got, gains]
         )
 
-    def norm_back(self, got_ref, gain, x_ref, scale_ref, rows_ref, part):
+    def norm_back(self, got_ref, gain, x_ref, scale_ref, rows_ref, part=None):
         grad = got_ref[...].astype(f32)
         scale = scale_ref[...]
         unit = x_ref[...] * scale
-        part[...] = jnp.sum(grad * unit, axis=0, keepdims=True)
+        if part is not None:
+            part[...] = jnp.sum(grad * unit, axis=0, keepdims=True)
         e = grad * gain
         return rows_ref[...] + scale * (e - unit * jnp.mean(e * unit, axis=1, keepdims=True))
 
@@ -352,16 +397,16 @@
         )
 
     def close_first(self, got, gains, x, scale, rows):
-        def kernel(info, got_ref, gain_ref, x_ref, scale_ref, rows_ref, part, out, scratch):
-            grad = self.norm_back(got_ref, gain_ref[0:1].astype(f32), x_ref, scale_ref, rows_ref, part)
+        def kernel(info, got_ref, gain_ref, x_ref, scale_ref, rows_ref, out, scratch):
+            grad = self.norm_back(got_ref, gain_ref[0:1].astype(f32), x_ref, scale_ref, rows_ref)
             self.store_absolute(out, grad, scratch, info)
 
-        part, out = run(
-            kernel, "close_first", [((1, self.width), f32)] + self.outs(f32),
+        out, = run(
+            kernel, "close_first", self.outs(f32),
             [self.info, got, gains, x, scale, rows], in_specs=[SMALL] + [VMEM] * 5,
             scratch=[pltpu.VMEM((self.rows, self.width), f32)],
         )
-        return part, self.absolute(out)
+        return self.absolute(out)
 
     def close_layer(self, got, middle):
         def kernel(info, got_ref, mid_ref, out, scratch):
@@ -393,26 +438,63 @@
     )[0]
 
 
-def weight_blocks(side, x, y, got, at, kb, dtypes):
-    rows = x.shape[0]
-    n = y.shape[1]
-
-    def kernel(side_ref, x_ref, y_ref, g_ref, *outs):
-        total = dot_first(x_ref[...], y_ref[...]) + g_ref[...].astype(f32)
-        for q, out in enumerate(outs):
-
-            @pl.when(pl.program_id(0) == q)
-            def _(out=out):
-                out[...] = total.astype(out.dtype)
-
-    return run(
-        kernel, "weight_blocks", [((kb, n), t) for t in dtypes], [side, x, y, got], (2,),
-        [
-            pl.BlockSpec((rows, kb), lambda i, s: (0, at + (i ^ s[0]))),
-            pl.BlockSpec(y.shape, lambda i, s: (0, 0), pipeline_mode=pl.Buffered(1)),
-            pl.BlockSpec((kb, n), lambda i, s: (at + (i ^ s[0]), 0)),
-        ],
-        [pl.BlockSpec((kb, n), lambda i, s: (0, 0))] * 2, scalars=1,
+def added(side, keep, got, at, kb, dtypes):
+    n = keep.shape[1]
+
+    def kernel(side_ref, k0, g0, k1, g1, first, second):
+        first[...] = (k0[...] + g0[...].astype(f32)).astype(first.dtype)
+        second[...] = (k1[...] + g1[...].astype(f32)).astype(second.dtype)
+
+    block = lambda q: pl.BlockSpec((kb, n), lambda i, s: (at + (q ^ s[0]), 0))
+    whole = pl.BlockSpec((kb, n), lambda i, s: (0, 0))
+    return run(
+        kernel, "added", [((kb, n), t) for t in dtypes], [side, keep, got, keep, got], (1,),
+        [block(0), block(0), block(1), block(1)], [whole, whole], scalars=1,
+    )
+
+
+def cut_gate_up(side, w, count):
+    kb, _, width = w.shape
+    c = width // 2 // count
+
+    def kernel(side_ref, w_ref, *outs):
+        for k, out in enumerate(outs):
+            out[:, :c] = w_ref[:, 0, k * c : (k + 1) * c]
+            out[:, c:] = w_ref[:, 1, k * c : (k + 1) * c]
+
+    return run(
+        kernel, "cut_gate_up", [((kb, 2 * c), bf16)] * count, [side, w], (1,),
+        [pl.BlockSpec((kb, 2, width // 2), lambda i, s: (0, 0, s[0]))],
+        [pl.BlockSpec((kb, 2 * c), lambda i, s: (0, 0))] * count, scalars=1,
+    )
+
+
+def cut_rows(side, w, count):
+    rows, kb = w.shape
+    c = rows // 2 // count
+
+    def kernel(side_ref, w_ref, *outs):
+        for k, out in enumerate(outs):
+            out[...] = w_ref[k * c : (k + 1) * c].T
+
+    return run(
+        kernel, "cut_rows", [((kb, c), bf16)] * count, [side, w], (1,),
+        [pl.BlockSpec((rows // 2, kb), lambda i, s: (s[0], 0))],
+        [pl.BlockSpec((kb, c), lambda i, s: (0, 0))] * count, scalars=1,
+    )
+
+
+def cut_columns(side, w):
+    count, kb, width = w.shape
+
+    def kernel(side_ref, w_ref, *outs):
+        for k, out in enumerate(outs):
+            out[...] = w_ref[k]
+
+    return run(
+        kernel, "cut_columns", [((kb, width // 2), bf16)] * count, [side, w], (1,),
+        [pl.BlockSpec((count, kb, width // 2), lambda i, s: (0, 0, s[0]))],
+        [pl.BlockSpec((kb, width // 2), lambda i, s: (0, 0))] * count, scalars=1,
     )
 
 
@@ -482,12 +564,20 @@
             parts.append(lax.dynamic_slice_in_dim(value, place * width, width, 1))
         return jnp.concatenate(parts, axis=1)
 
-    def groups(self):
-        found = []
-        for d in range(self.dp):
-            if not d & PAIR:
-                found.append([e * self.tp + t for e in (d, d ^ PAIR) for t in range(self.tp)])
-        return found
+    def walk(self):
+        return [t ^ (t >> 1) for t in range(self.tp)]
+
+    def pairs(self, walk):
+        there = self.walk() if walk else list(range(self.tp))
+        back = there[::-1] if walk else there
+        return [
+            [d * self.tp + t for t in there] + [(d ^ PAIR) * self.tp + t for t in back]
+            for d in range(self.dp)
+            if not d & PAIR
+        ]
+
+    def singles(self):
+        return [[d * self.tp + t for t in range(self.tp)] for d in range(self.dp)]
 
 
 def halves(value, side, axis):
@@ -559,35 +649,38 @@
     def wait1(self):
         self.near = self.chain.wait(self.got)
 
-    def start2(self):
+    def even(self):
+        self.ahead = self.chain.step(lambda x, y: weight_part(x, y, 0, self.k, f32), self.x, self.y)
+
+    def add(self):
         wires, chain = self.wires, self.chain
         kb = 2 * self.k // wires.dp
-        if not wires.far[1:] and kb % 128 == 0:
-            blocks = lambda s, x, y, g, at, types: weight_blocks(s, x, y, g, at, kb, types)
-            far, far_pair = chain.step(
-                lambda s, x, y, g: blocks(s, x, y, g, 2, (bf16, bf16)), self.side, self.x, self.y, self.near
+        if not wires.far[1:]:
+            self.sends = chain.step(
+                lambda s, e, g: added(s, e, g, 2, kb, (bf16, bf16)), self.side, self.ahead, self.near
             )
             self.keep, pair = chain.step(
-                lambda s, x, y, g: blocks(s, x, y, g, 0, (f32, bf16)), self.side, self.x, self.y, self.near
+                lambda s, e, g: added(s, e, g, 0, kb, (f32, bf16)), self.side, self.ahead, self.near
             )
-        else:
-            total = chain.step(
-                lambda x, y, g: weight_part(x, y, 0, self.k, f32, g, 0), self.x, self.y, self.near
-            )
-            for bit in reversed(wires.far[1:]):
-                rows = total.shape[0] // 2
-                got = chain.wait(wires.over_dp(total[rows:].astype(bf16), bit))
-                total = total[:rows] + got.astype(f32)
-            at = [p ^ self.side[0] for p in (0, 1)]
-            cut = lambda p: lax.dynamic_slice_in_dim(total, p * kb, kb, 0)
-            self.keep, pair = cut(at[0]), cut(at[1]).astype(bf16)
-            far, far_pair = cut(2 + at[0]).astype(bf16), cut(2 + at[1]).astype(bf16)
-        bit = wires.far[0]
-        self.got = [
-            wires.over_dp(*chain.pin(far), bit),
-            wires.over_dp(*chain.pin(far_pair), bit ^ PAIR),
-            wires.over_dp(*chain.pin(pair), PAIR),
-        ]
+            self.sends = [*self.sends, pair]
+            return
+        total = self.ahead + self.near.astype(f32)
+        for b in reversed(wires.far[1:]):
+            rows = total.shape[0] // 2
+            got = chain.wait(wires.over_dp(total[rows:].astype(bf16), b))
+            total = total[:rows] + got.astype(f32)
+        cut = lambda p: lax.dynamic_slice_in_dim(total, (p ^ self.side[0]) * kb, kb, 0)
+        far = lambda p: lax.dynamic_slice_in_dim(total, (2 + (p ^ self.side[0])) * kb, kb, 0)
+        self.keep = cut(0)
+        self.sends = [far(0).astype(bf16), far(1).astype(bf16), cut(1).astype(bf16)]
+
+    def start2(self):
+        bit = self.wires.far[0]
+        sends = self.chain.pin(*self.sends)
+        self.got = [self.wires.over_dp(v, m) for v, m in zip(sends, (bit, bit ^ PAIR, PAIR))]
+
+    def wait_pair(self):
+        self.got[2] = self.chain.wait(self.got[2])
 
     def wait2(self):
         self.terms = [self.keep, *self.chain.wait(*self.got)]
@@ -597,8 +690,26 @@
     def __init__(self, wires, chain, value):
         self.chain = chain
         self.got = lax.all_gather(
-            *chain.pin(value), AXES, axis=0, tiled=True, axis_index_groups=wires.groups()
-        )
+            *chain.pin(value), AXES, axis=0, tiled=True, axis_index_groups=wires.pairs(False)
+        )
+
+    def wait(self):
+        return self.chain.wait(self.got)
+
+
+class PairGather:
+    def __init__(self, wires, chain, side, value):
+        self.wires, self.chain, self.side, self.value = wires, chain, side, value
+        self.got = wires.over_dp(*chain.pin(value), PAIR)
+
+    def wait1(self):
+        self.both = self.chain.step(side_by_side, self.side, self.value, self.chain.wait(self.got))
+
+    def start2(self):
+        got = lax.all_gather(
+            *self.chain.pin(self.both), AXES, axis=1, tiled=True, axis_index_groups=self.wires.singles()
+        )
+        self.got = got.reshape(-1, got.shape[2])
 
     def wait(self):
         return self.chain.wait(self.got)
@@ -608,7 +719,7 @@
     def __init__(self, wires, chain, value):
         self.chain = chain
         self.got = lax.psum_scatter(
-            *chain.pin(value), AXES, scatter_dimension=0, tiled=True, axis_index_groups=wires.groups()
+            *chain.pin(value), AXES, scatter_dimension=0, tiled=True, axis_index_groups=wires.pairs(True)
         )
 
     def wait(self):
@@ -625,7 +736,6 @@
     group_rows = local_rows * tp
     kb = width // dp
     cols = w_qkv.shape[2] // 2
-    head_count = cols // HEAD_DIM
     rows = Rows(wires, jnp.stack([d - PAIR * side, t, lengths[0]]), local_rows, width)
 
     sides = jnp.reshape(side, (1,))
@@ -636,15 +746,8 @@
     def piece(own, other):
         return Piece(wires, chain, sides, own, other)
 
-    def cut_rest(w_out, w_down, w_gate_up):
-        found = [[h.T for h in halves(w_out, side, 0)]]
-        whole = [h.T for h in halves(w_down, side, 0)]
-        for k in range(n_down):
-            found.append([h[:, k * cut : (k + 1) * cut] for h in whole])
-        whole = halves(w_gate_up, side, 2)
-        for k in range(n_gu):
-            found.append([h[:, :, k * cg : (k + 1) * cg].reshape(kb, 2 * cg) for h in whole])
-        return found
+    def both(cut, w, *count):
+        return list(zip(*(cut(s, w, *count) for s in (sides, 1 - sides))))
 
     per = n_gu // n_down
     acts, grads_gu, grads = [], [], []
@@ -655,12 +758,12 @@
         grads_gu.append(g)
         grads.append(Grad(wires, chain, sides, normed_second, g))
 
-    positions = jnp.arange(group_rows, dtype=jnp.int32)
+    positions = jnp.tile(jnp.arange(group_rows, dtype=jnp.int32), 2)
     exponent = jnp.arange(HEAD_DIM // 2).astype(f32) * (2.0 / HEAD_DIM)
     frequency = ROPE_BASE ** (-exponent)
     angles = positions.astype(f32)[:, None] * frequency[None, :]
-    cosine = jnp.tile(jnp.concatenate([jnp.cos(angles), jnp.cos(angles)], axis=1), (1, head_count))
-    sine = jnp.tile(jnp.concatenate([-jnp.sin(angles), jnp.sin(angles)], axis=1), (1, head_count))
+    cosine = jnp.concatenate([jnp.cos(angles), jnp.cos(angles)], axis=1)
+    sine = jnp.concatenate([-jnp.sin(angles), jnp.sin(angles)], axis=1)
 
     gains = jnp.stack([gain_attn, gain_mlp])[:, None]
     pair_length = wires.over_dp(lengths, PAIR)
@@ -670,36 +773,42 @@
             [jnp.where(side == 0, mine, theirs), jnp.where(side == 0, theirs, mine)], axis=axis
         )
 
-    got = wires.over_dp(gains, PAIR)
-    gains = ordered(gains, chain.wait(got), 1)
-    for bit in wires.far:
+    masks = [PAIR, wires.far[0], wires.far[0] ^ PAIR]
+    got = [wires.over_dp(gains, m) for m in masks]
+    grad_rows, gv = chain.step(rows.open_cotangent, cotangent)
+    got = chain.wait(*got)
+    rows_g = PairGather(wires, chain, sides, gv)
+    w_q, w_k, w_v = (piece(*h) for h in both(cut_columns, w_qkv))
+    gains = jnp.concatenate([ordered(gains, got[0], 1), ordered(got[1], got[2], 1)], axis=1)
+    for bit in wires.far[1:]:
         gains = jnp.concatenate([gains, chain.wait(wires.over_dp(*chain.pin(gains), bit))], axis=1)
-    w_q, w_k, w_v = (piece(*halves(w_qkv[j], side, 1)) for j in range(3))
-    w_q.start1()
     gains = jnp.concatenate([gains, chain.wait(wires.over_dp(*chain.pin(gains), NEAR))], axis=1)
     gains = gains.reshape(2, width)
     input_f, scale_first, v = chain.step(rows.open_first, hidden_in, gains)
+    rows_g.wait1()
     rows_a = RowGather(wires, chain, v)
-    w_o, d0, d1, g0, g1, g2, g3 = (piece(*h) for h in chain.step(cut_rest, w_out, w_down, w_gate_up))
-    gus = [g0, g1, g2, g3]
-    grad_rows, gv = chain.step(rows.open_cotangent, cotangent)
+    w_q.start1()
     table = chain.step(
         lambda a, b, *c: (ordered(a, b, 0), *c), lengths, pair_length, positions, cosine, sine
     )
     w_q.wait1()
     w_k.start1()
+    rows_g.start2()
     w_q.start2()
-    rows_g = RowGather(wires, chain, gv)
+    cuts = chain.step(lambda o, w: both(cut_rows, o, 1) + both(cut_rows, w, n_down), w_out, w_down)
+    w_o, d0, d1 = (piece(*h) for h in cuts)
     w_k.wait1()
     w_q.wait2()
     w_v.start1()
     w_k.start2()
-    normed_first = rows_a.wait()
-    query_raw = chain.step(product, normed_first, w_q.pair)
+    cuts = chain.step(lambda g: both(cut_gate_up, g, n_gu), w_gate_up)
+    g0, g1, g2, g3 = gus = [piece(*h) for h in cuts]
     w_v.wait1()
     w_k.wait2()
     w_o.start1()
     w_v.start2()
+    normed_first = rows_a.wait()
+    query_raw = chain.step(product, normed_first, w_q.pair)
     key_raw = chain.step(product, normed_first, w_k.pair)
     w_o.wait1()
     w_v.wait2()
@@ -736,90 +845,120 @@
     g1.wait2()
     g3.start1()
     g2.start2()
+    g3.wait1()
+    g2.wait2()
+    g3.start2()
     normed_second = rows_n.wait()
     forward_gu(0)
     grads[0].odd()
-    g3.wait1()
-    g2.wait2()
-    g3.start2()
+    grads[0].start1()
     forward_gu(1)
-    grads[0].start1()
     forward_gu(2)
-    second = chain.step(lambda y, p: back(y, p, f32), grads_gu, [g.pair for g in gus[:3]])
+    second = chain.step(lambda y, p: back(y, p, f32, turn=False), grads_gu, [g.pair for g in gus[:3]])
     g3.wait2()
     forward_gu(3)
     second = chain.step(lambda y, p, s: back([y], [p], bf16, s), grads_gu[3], g3.pair, second)
-    grads[1].odd()
     grads[0].wait1()
     sum_second = RowSum(wires, chain, second)
+    grads[1].odd()
     grads[1].start1()
-    grads[0].start2()
+    grads[0].even()
+    grads[0].add()
+    grads[1].even()
     grads[2].odd()
     acts = [jnp.concatenate(acts[k * per : (k + 1) * per], axis=1) for k in range(n_down)]
     grads += [Grad(wires, chain, sides, grad_half, a) for a in acts]
+    grads[1].wait1()
+    grads[2].start1()
+    grads[0].start2()
+    grads[1].add()
+    grads[2].even()
     grads[3].odd()
-    grads[1].wait1()
-    grads[0].wait2()
-    grads[2].start1()
-    grads[1].start2()
     mlp_part = chain.step(lambda y, p: back(y, p, bf16), acts, [d0.pair, d1.pair])
-    grads[4].odd()
-    grads[2].wait1()
-    grads[1].wait2()
     part_gain_mlp, grad_middle, v = chain.step(
         rows.close_second, sum_second.wait(), gains, middle, scale_second, grad_rows
     )
-    rows_m = RowGather(wires, chain, v)
+    grads[2].wait1()
+    grads[0].wait2()
+    rows_m = PairGather(wires, chain, sides, v)
     grads[3].start1()
+    grads[1].start2()
+    grads[2].add()
+    grads[3].even()
+    grads[4].odd()
+    grads[3].wait1()
+    grads[1].wait2()
+    rows_m.wait1()
+    rows_m.start2()
+    grads[4].start1()
     grads[2].start2()
+    grads[3].add()
+    grads[4].even()
     grads[5].odd()
-    grads[3].wait1()
+    grads[4].wait1()
     grads[2].wait2()
-    grads[4].start1()
+    grads[5].start1()
     grads[3].start2()
-    grads[4].wait1()
-    grads[3].wait2()
-    grads[5].start1()
     mlp = RowSum(wires, chain, mlp_part)
-    grads[4].start2()
+    grads[4].add()
+    grads[5].even()
     middle_half = rows_m.wait()
     grads.append(Grad(wires, chain, sides, middle_half, attn_flat))
     grads[6].odd()
     grad_mixed = chain.step(lambda x, p: product(x, p, bf16), middle_half, w_o.pair)
-    grads[5].wait1()
-    grads[4].wait2()
-    grads[6].start1()
-    grads[5].start2()
     grad_proj = chain.step(lambda *a: attend_back(*a), *table, saved, grad_mixed)
     grads += [Grad(wires, chain, sides, normed_first, g) for g in grad_proj]
+    grads[5].wait1()
+    grads[3].wait2()
+    grads[6].start1()
+    grads[4].start2()
+    grads[5].add()
     grads[7].odd()
-    first = chain.step(
-        lambda y, p: back(y, p, bf16), grad_proj, [w_q.pair, w_k.pair, w_v.pair]
+    first, part_gain_attn = chain.step(
+        lambda y, p, x: back(y, p, bf16, normed=x), grad_proj, [w_q.pair, w_k.pair, w_v.pair], normed_first
     )
     grads[6].wait1()
-    grads[5].wait2()
+    grads[4].wait2()
+    sum_first = RowSum(wires, chain, first)
     grads[7].start1()
-    sum_first = RowSum(wires, chain, first)
-    grads[6].start2()
+    grads[5].start2()
+    grads[6].even()
+    grads[6].add()
     grads[8].odd()
-    grads[9].odd()
-
-    def gain_open(part):
-        total = jnp.concatenate([part, part_gain_mlp]).reshape(2, dp, kb)
-        mine, theirs = total[:, 0::2], total[:, 1::2]
-        low = jnp.where(side == 0, mine, theirs)
-        high = jnp.where(side == 0, theirs, mine)
-        return jnp.stack([low, high], axis=2).reshape(2, dp, kb)
-
-    def gain_start(bit):
-        nonlocal total, got
-        rows = total.shape[1] // 2
-        got = wires.over_dp(*chain.pin(total[:, rows:]), bit)
-        total = total[:, :rows]
-
-    def gain_wait():
-        nonlocal total
-        total = total + chain.wait(got)
+    grads[7].even()
+
+    def open_gains(attn, mlp, gains):
+        parts = jnp.concatenate([attn / gains[0:1].astype(f32), mlp]).reshape(2, dp, kb)
+        return parts
+
+    class GainSum:
+        def __init__(self, total):
+            self.total = total
+
+        def start(self, bit):
+            rows = self.total.shape[1] // 2
+            if bit == PAIR:
+                mine = jnp.where(side == 0, self.total[:, :1], self.total[:, 1:])
+                send = jnp.where(side == 0, self.total[:, 1:], self.total[:, :1])
+            else:
+                mine, send = self.total[:, :rows], self.total[:, rows:]
+            self.total = mine
+            self.got = wires.over_dp(*chain.pin(send), bit)
+
+        def start_tensor(self, mask):
+            self.got = wires.over_tensor(*chain.pin(self.total), mask)
+
+        def wait(self):
+            self.total = self.total + chain.wait(self.got)
+
+    gain_sum = GainSum(chain.step(open_gains, part_gain_attn, part_gain_mlp, gains))
+    gain_sum.start(NEAR)
+
+    def lay(which, shape, axis, place):
+        block = tuple(n // 2 if a == axis else n for a, n in enumerate(shape))
+        return chain.step(
+            lambda t: laid_out(sides, t, shape, block, axis, place), [grads[i].terms for i in which]
+        )
 
     def place_gu(ref, parts):
         for k, p in enumerate(parts):
@@ -835,37 +974,44 @@
         for k, p in enumerate(parts):
             ref[k] = p
 
-    def lay(which, shape, axis, place):
-        block = tuple(n // 2 if a == axis else n for a, n in enumerate(shape))
-        return chain.step(
-            lambda t: laid_out(sides, t, shape, block, axis, place), [grads[i].terms for i in which]
-        )
-
     grads[7].wait1()
+    grads[5].wait2()
+    grads[8].start1()
+    grads[6].start2()
+    grads[7].add()
+    grads[8].even()
+    grads[9].odd()
+    grads[9].even()
+    layer_out = chain.step(rows.close_layer, mlp.wait(), middle)
+    gain_sum.wait()
+    for bit in wires.far[:0:-1]:
+        gain_sum.start(bit)
+        gain_sum.wait()
+    gain_sum.start(wires.far[0])
+    grads[8].wait1()
     grads[6].wait2()
-    grads[8].start1()
+    grads[9].start1()
     grads[7].start2()
-    layer_out = chain.step(rows.close_layer, mlp.wait(), middle)
+    grads[8].add()
     grad_gate_up = lay((0, 1, 2, 3), (kb, 2, 2 * ff), 2, place_gu)
-    grads[8].wait1()
+    gain_sum.wait()
+    gain_sum.start(PAIR)
+    grad_down = lay((4, 5), (2 * ff, kb), 0, place_rows)
     grads[7].wait2()
-    grads[9].start1()
     grads[8].start2()
-    grad_down = lay((4, 5), (2 * ff, kb), 0, place_rows)
+    grads[9].wait1()
+    grads[9].add()
+    grads[8].wait_pair()
+    grads[9].start2()
     grad_out = lay((6,), (2 * cols, kb), 0, place_rows)
-    grads[9].wait1()
+    gain_sum.wait()
+    gain_sum.start_tensor(1)
+    grad_in = chain.step(rows.close_first, sum_first.wait(), gains, input_f, scale_first, grad_middle)
+    gain_sum.wait()
+    gain_sum.start_tensor(2)
     grads[8].wait2()
-    grads[9].start2()
-    part_gain_attn, grad_in = chain.step(
-        rows.close_first, sum_first.wait(), gains, input_f, scale_first, grad_middle
-    )
-    total = gain_open(part_gain_attn)
-    for bit in [NEAR] + wires.far[::-1] + [PAIR]:
-        gain_start(bit)
-        gain_wait()
-    total = total[:, 0]
-    total = total + chain.wait(wires.over_tensor(*chain.pin(total), 1))
-    total = total + chain.wait(wires.over_tensor(*chain.pin(total), 2))
+    gain_sum.wait()
+    total = gain_sum.total[:, 0]
     grads[9].wait2()
     grad_qkv = lay((7, 8, 9), (3, kb, 2 * cols), 2, place_stack)
     return (layer_out, grad_in, total[0], grad_qkv, grad_out, total[1], grad_gate_up, grad_down)

time: 929 us -> 867 us (0.933)
  waiting for transfers between devices: 366 us -> 299 us
  Pallas kernels: 324 us -> 379 us
  starting transfers between devices: 154 us -> 127 us
  local copies, waits for them, and re-layouts: 57.9 us -> 33 us
    pallas_call x67 -> x87, Pallas kernels: 324 us -> 379 us  [run(): pl.pallas_call(kernel, out_shape=[jax.ShapeDtypeStruct(s, t) for s, t in...]
    ppermute x87 -> x90, waiting for transfers between devices: 321 us -> 273 us  [over_dp(): return lax.ppermute(value, AXES, pairs)]
    all_gather x4 -> x2, waiting for transfers between devices: 19.9 us -> 0.01 us  [__init__(): lax.all_gather(*chain.pin(value), AXES, axis=0, tiled=True, axis_index_gr...]
    ppermute x2, starting transfers between devices: 18.4 us -> 0.14 us  [over_tensor(): return lax.ppermute(value, AXES, pairs)]
    optimization_barrier x6 -> x0, local copies, waits for them, and re-layouts: 10.5 us -> none  [pin(): return lax.optimization_barrier((values, self.last))[0]]
    ppermute x87 -> x90, starting transfers between devices: 134 us -> 127 us  [over_dp(): return lax.ppermute(value, AXES, pairs)]
    unnamed x228 -> x244, local copies, waits for them, and re-layouts: 31.6 us -> 30.4 us
  transfers between devices with their start and end apart: 97 -> 100, of which waited for: 55 -> 37; matrix products, arithmetic and copies ran while one was open for 3% -> 0% of each run, Pallas kernels for 33% -> 43%
where the time goes in v4:
time: 867 us; the launch traced here: 859 us
  Pallas kernels  379 us (44%)
  waiting for transfers between devices  299 us (34%)
  starting transfers between devices  127 us (15%)
  local copies, waits for them, and re-layouts  33 us (4%)
  between operations  17.4 us (2%)
    pallas_call x87, Pallas kernels, run(): pl.pallas_call(kernel, out_shape=[jax.ShapeDtypeStruct(s, t) for s, t in...  379 us
    ppermute x90, waiting for transfers between devices, over_dp(): return lax.ppermute(value, AXES, pairs)  273 us
    ppermute x90, starting transfers between devices, over_dp(): return lax.ppermute(value, AXES, pairs)  127 us
    unnamed x244, local copies, waits for them, and re-layouts  30.4 us
    reduce_scatter x4, waiting for transfers between devices, __init__(): lax.psum_scatter(*chain.pin(value), AXES, scatter_dimension=0, tiled=True...  23.7 us
  transfers between devices with their start and end apart: 100, of which 37 were waited for; matrix products, arithmetic and copies ran while one was open for 0% of the time, Pallas kernels for 43%

profile of v4, /device:TPU:0, one launch (start us, length us, event | category | flops | bytes accessed | tf_op | source)
XLA Modules:
  0.0 858.6 jit_solution(187372495165779133)
XLA Ops:
  26.3 11.0 %collective-permute-done.5.b = bf16[128,3072]{1,0:T(8,128)(2,1)S(1)} collective-permute-done((bf16[128,3072]{1,0:T(8,128)(2,1)S(1)}, bf16[128,3072]{1,0:T(8,128)(2,1)S(1)}, u32[]{:S(2)}, u32[]{:S(2)}) %collective-permute-start.5) | collective-permute-done | bytes 786464 | tf_op jit(solution)/shard_map/ppermute | solution.py:543
  50.3 28.3 %collective-permute-done.6.refs_1_ = bf16[384,384]{1,0:T(8,128)(2,1)S(1)} collective-permute-done((bf16[384,384]{1,0:T(8,128)(2,1)S(1)}, bf16[384,384]{1,0:T(8,128)(2,1)S(1)}, u32[]{:S(2)}, u32[]{:S(2)}) %collective-permute-start.6) | collective-permute-done | bytes 294944 | tf_op jit(solution)/shard_map/ppermute | solution.py:543
  96.5 7.0 collective-permute-done.11.refs_2_
  140.2 7.1 product.6.q_ref
  147.3 7.1 product.7.k_ref
  169.4 7.4 product.8.v_ref
  177.0 15.5 %attend.1 = (bf16[1024,384]{1,0:T(8,128)(2,1)}, bf16[1024,384]{1,0:T(8,128)(2,1)}, bf16[1024,384]{1,0:T(8,128)(2,1)}, bf16[1024,384]{1,0:T(8,128)(2,1)}, f32[1024,4]{1,0:T(8,128)S(1)}) custom-call(s32[2]{0:T(128)S(1)} %pad_add_fusion.1.len_ref, s32[1024,1]{1,0:T(8,128)S(1)} %copy.17.rows_ref, s32[1,1024]{1,0:T(1,128)S(1)} %bitcast.32, ...), custom_call_target="tpu_custom_call" | custom-call | flops 1 | bytes 1 | tf_op jit(solution)/shard_map/attend/pallas_call | solution.py:152
  193.9 7.9 back.5
  210.3 22.5 %collective-permute-done.25.refs_1_ = bf16[384,512]{1,0:T(8,128)(2,1)S(1)} collective-permute-done((bf16[384,512]{1,0:T(8,128)(2,1)S(1)}, bf16[384,512]{1,0:T(8,128)(2,1)S(1)}, u32[]{:S(2)}, u32[]{:S(2)}) %collective-permute-start.25) | collective-permute-done | bytes 393248 | tf_op jit(solution)/shard_map/ppermute | solution.py:543
  246.5 7.4 product.9.ga_ref
  254.0 17.4 %collective-permute-done.30.refs_1_ = bf16[384,512]{1,0:T(8,128)(2,1)S(1)} collective-permute-done((bf16[384,512]{1,0:T(8,128)(2,1)S(1)}, bf16[384,512]{1,0:T(8,128)(2,1)S(1)}, u32[]{:S(2)}, u32[]{:S(2)}) %collective-permute-start.30) | collective-permute-done | bytes 393248 | tf_op jit(solution)/shard_map/ppermute | solution.py:543
  284.4 7.3 product.10.ga_ref
  291.7 23.7 %reduce-scatter.5.cloned.1.call-done.got_ref = bf16[128,3072]{1,0:T(8,128)(2,1)} async-done(((bf16[1024,3072]{1,0:T(8,128)(2,1)}), bf16[128,3072]{1,0:T(8,128)(2,1)}) %reduce-scatter.5.cloned.1.call-update) | async-done | bytes 786448 | tf_op jit(solution)/shard_map/reduce_scatter | solution.py:721
  325.8 15.0 %collective-permute-done.38.refs_1_ = bf16[384,512]{1,0:T(8,128)(2,1)S(1)} collective-permute-done((bf16[384,512]{1,0:T(8,128)(2,1)S(1)}, bf16[384,512]{1,0:T(8,128)(2,1)S(1)}, u32[]{:S(2)}, u32[]{:S(2)}) %collective-permute-start.38) | collective-permute-done | bytes 393248 | tf_op jit(solution)/shard_map/ppermute | solution.py:543
  340.7 10.9 %collective-permute-done.39.refs_2_ = bf16[384,512]{1,0:T(8,128)(2,1)S(1)} collective-permute-done((bf16[384,512]{1,0:T(8,128)(2,1)S(1)}, bf16[384,512]{1,0:T(8,128)(2,1)S(1)}, u32[]{:S(2)}, u32[]{:S(2)}) %collective-permute-start.39) | collective-permute-done | bytes 393248 | tf_op jit(solution)/shard_map/ppermute | solution.py:543
  351.7 13.7 %collective-permute-done.40.refs_3_ = bf16[384,512]{1,0:T(8,128)(2,1)S(1)} collective-permute-done((bf16[384,512]{1,0:T(8,128)(2,1)S(1)}, bf16[384,512]{1,0:T(8,128)(2,1)S(1)}, u32[]{:S(2)}, u32[]{:S(2)}) %collective-permute-start.40) | collective-permute-done | bytes 393248 | tf_op jit(solution)/shard_map/ppermute | solution.py:543
  372.4 14.0 %collective-permute-done.41.refs_1_ = bf16[384,512]{1,0:T(8,128)(2,1)S(1)} collective-permute-done((bf16[384,512]{1,0:T(8,128)(2,1)S(1)}, bf16[384,512]{1,0:T(8,128)(2,1)S(1)}, u32[]{:S(2)}, u32[]{:S(2)}) %collective-permute-start.41) | collective-permute-done | bytes 393248 | tf_op jit(solution)/shard_map/ppermute | solution.py:543
  397.6 7.1 gated.4
  411.3 7.1 gated.5
  420.2 7.1 gated.6
  428.3 16.3 %back.6.refs_3_ = f32[1024,3072]{1,0:T(8,128)} custom-call(bf16[1024,512]{1,0:T(8,128)(2,1)S(1)} %get-tuple-element.839.y_ref.refs_0_, bf16[1024,512]{1,0:T(8,128)(2,1)} %copy-done.17, bf16[1024,512]{1,0:T(8,128)(2,1)} %copy-done.15, bf16[1536,512]{1,0:T(8,128)(2,1)} %in_order.16.even.refs_3_, bf16[1536,512]{1,0:T(8,128)(2,1)} %collective-permute-done.33.odd.refs_4_, ...), custom_call_target="tpu_custom_call" | custom-call | flops 1 | bytes 1 | tf_op jit(solution)/shard_map/back/pallas_call | solution.py:152
  444.6 7.1 gated.7
  451.8 11.1 %back.7 = bf16[1024,3072]{1,0:T(8,128)(2,1)} custom-call(bf16[1024,512]{1,0:T(8,128)(2,1)S(1)} %get-tuple-element.910.refs_0_.y_ref, bf16[1536,512]{1,0:T(8,128)(2,1)} %in_order.19.even.refs_1_, bf16[1536,512]{1,0:T(8,128)(2,1)} %collective-permute-done.45.odd.refs_2_, f32[1024,3072]{1,0:T(8,128)} %back.6.refs_3_), custom_call_target="tpu_custom_call" | custom-call | flops 1 | bytes 1 | tf_op jit(solution)/shard_map/back/pallas_call | solution.py:152
  488.2 13.6 %collective-permute-done.47.g0.g1 = bf16[1536,512]{1,0:T(8,128)(2,1)S(1)} collective-permute-done((bf16[1536,512]{1,0:T(8,128)(2,1)}, bf16[1536,512]{1,0:T(8,128)(2,1)S(1)}, u32[]{:S(2)}, u32[]{:S(2)}) %collective-permute-start.47) | collective-permute-done | bytes 1572896 | tf_op jit(solution)/shard_map/ppermute | solution.py:543
  521.4 12.8 %back.8 = bf16[1024,3072]{1,0:T(8,128)(2,1)} custom-call(bf16[1024,512]{1,0:T(8,128)(2,1)S(1)} %constant_dynamic-update-slice_fusion.5.refs_0_.y_ref, bf16[1024,512]{1,0:T(8,128)(2,1)} %copy-done.6, bf16[1536,512]{1,0:T(8,128)(2,1)} %in_order.14.even.refs_2_, bf16[1536,512]{1,0:T(8,128)(2,1)} %collective-permute-done.28.odd.refs_3_, ...), custom_call_target="tpu_custom_call" | custom-call | flops 1 | bytes 1 | tf_op jit(solution)/shard_map/back/pallas_call | solution.py:152
  558.9 12.8 %collective-permute-done.56.g0.g1 = bf16[1536,512]{1,0:T(8,128)(2,1)S(1)} collective-permute-done((bf16[1536,512]{1,0:T(8,128)(2,1)S(1)}, bf16[1536,512]{1,0:T(8,128)(2,1)S(1)}, u32[]{:S(2)}, u32[]{:S(2)}) %collective-permute-start.56) | collective-permute-done | bytes 1572896 | tf_op jit(solution)/shard_map/ppermute | solution.py:543
  603.2 14.4 %collective-permute-done.60.g0.g1 = bf16[1536,512]{1,0:T(8,128)(2,1)} collective-permute-done((bf16[1536,512]{1,0:T(8,128)(2,1)}, bf16[1536,512]{1,0:T(8,128)(2,1)}, u32[]{:S(2)}, u32[]{:S(2)}) %collective-permute-start.60) | collective-permute-done | bytes 1572896 | tf_op jit(solution)/shard_map/ppermute | solution.py:543
  645.1 17.7 %attend_back.1 = (bf16[1024,384]{1,0:T(8,128)(2,1)}, bf16[1024,384]{1,0:T(8,128)(2,1)}, bf16[1024,384]{1,0:T(8,128)(2,1)}) custom-call(s32[2]{0:T(128)S(1)} %pad_add_fusion.1.len_ref, s32[1024,1]{1,0:T(8,128)S(1)} %copy.18.rows_ref, s32[1,1024]{1,0:T(1,128)S(1)} %bitcast.34, f32[1024,96]{1,0:T(8,128)S(1)} %copy-done.25, f32[1024,96]{1,0:T(8,128)S(1)} %copy-done.26, ...), custom_call_target="tpu_custom_call" | custom-call | flops 1 | bytes 1 | tf_op jit(solution)/shard_map/attend_back/pallas_call | solution.py:152
  678.2 17.4 %back.9 = (bf16[1024,3072]{1,0:T(8,128)(2,1)}, f32[1,3072]{1,0:T(1,128)S(1)}) custom-call(bf16[1024,384]{1,0:T(8,128)(2,1)S(1)} %copy-done.23, bf16[1024,384]{1,0:T(8,128)(2,1)S(1)} %copy-done.22, bf16[1024,384]{1,0:T(8,128)(2,1)} %get-tuple-element.1058.refs_2_.y_ref, bf16[1536,384]{1,0:T(8,128)(2,1)} %in_order.10.even.refs_3_, ...), custom_call_target="tpu_custom_call" | custom-call | flops 1 | bytes 1 | tf_op jit(solution)/shard_map/back/pallas_call | solution.py:152
  775.9 7.0 laid_out.4
  782.9 9.9 %collective-permute-done.74 = f32[2,2,384]{2,0,1:T(2,128)S(1)} collective-permute-done((f32[2,2,384]{2,0,1:T(2,128)S(1)}, f32[2,2,384]{2,0,1:T(2,128)S(1)}, u32[]{:S(2)}, u32[]{:S(2)}) %collective-permute-start.74) | collective-permute-done | bytes 6176 | tf_op jit(solution)/shard_map/ppermute | solution.py:543
  826.9 20.2 %collective-permute-done.89.refs_9_ = bf16[384,384]{1,0:T(8,128)(2,1)S(1)} collective-permute-done((bf16[384,384]{1,0:T(8,128)(2,1)S(1)}, bf16[384,384]{1,0:T(8,128)(2,1)S(1)}, u32[]{:S(2)}, u32[]{:S(2)}) %collective-permute-start.89) | collective-permute-done | bytes 294944 | tf_op jit(solution)/shard_map/ppermute | solution.py:543
  (537 shorter events, 436.3 us)
Async XLA Ops:
  7.2 133.0 %all-gather.5.cloned.1.call-start = ((), (), s32[]{:S(2)}) async-start(), calls=%async_computation.4 | async-start | bytes 7077888 | tf_op jit(solution)/shard_map/all_gather | solution.py:692
  38.5 171.7 %all-gather.7.cloned.1.call-start = ((), (), s32[]{:S(2)}) async-start(), calls=%async_computation.6 | async-start | bytes 7864320 | tf_op jit(solution)/shard_map/all_gather | solution.py:709
  41.5 37.1 %collective-permute-start.7 = (bf16[384,384]{1,0:T(8,128)(2,1)S(1)}, bf16[384,384]{1,0:T(8,128)(2,1)S(1)}, u32[]{:S(2)}, u32[]{:S(2)}) collective-permute-start(bf16[384,384]{1,0:T(8,128)(2,1)S(1)} %get-tuple-element.616), channel_id=1, source_target_pairs={{0,24},{1,25},{2,26},{3,27},{4,28},{5,29},{6,30},{7,31},{8,16},{9,... | collective-permute-start | bytes 884744 | tf_op jit(solution)/shard_map/ppermute | solution.py:543
  78.6 236.8 %reduce-scatter.5.cloned.1.call-start = ((), (), s32[]{:S(2)}) async-start(), calls=%async_computation.5 | async-start | bytes 7077888 | tf_op jit(solution)/shard_map/reduce_scatter | solution.py:721
  162.0 39.7 %collective-permute-start.22 = (bf16[384,512]{1,0:T(8,128)(2,1)}, bf16[384,512]{1,0:T(8,128)(2,1)S(1)}, u32[]{:S(2)}, u32[]{:S(2)}) collective-permute-start(bf16[384,512]{1,0:T(8,128)(2,1)} %get-tuple-element.713.refs_0_), channel_id=1, source_target_pairs={{0,16},{1,17},{2,18},{3,19},{4,20},{5,21},{6,22},{7,23},{8,24},{9,... | collective-permute-start | bytes 1179656 | tf_op jit(solution)/shard_map/ppermute | solution.py:543
  201.8 195.8 %all-gather.9.cloned.1.call-start = ((), (), s32[]{:S(2)}) async-start(), calls=%async_computation.7 | async-start | bytes 7077888 | tf_op jit(solution)/shard_map/all_gather | solution.py:692
  204.9 35.1 %collective-permute-start.28 = (bf16[1536,512]{1,0:T(8,128)(2,1)}, bf16[1536,512]{1,0:T(8,128)(2,1)}, u32[]{:S(2)}, u32[]{:S(2)}) collective-permute-start(bf16[1536,512]{1,0:T(8,128)(2,1)} %in_order.14.even.refs_2_), channel_id=1, source_target_pairs={{0,4},{1,5},{2,6},{3,7},{4,0},{5,1},{6,2},{7,3},{8,12},{9,13},{10,... | collective-permute-start | bytes 4718600 | tf_op jit(solution)/shard_map/ppermute | solution.py:543
  241.7 35.4 %collective-permute-start.29 = (bf16[1536,512]{1,0:T(8,128)(2,1)}, bf16[1536,512]{1,0:T(8,128)(2,1)S(1)}, u32[]{:S(2)}, u32[]{:S(2)}) collective-permute-start(bf16[1536,512]{1,0:T(8,128)(2,1)} %in_order.15.even.refs_4_), channel_id=1, source_target_pairs={{0,4},{1,5},{2,6},{3,7},{4,0},{5,1},{6,2},{7,3},{8,12},{9,13},{10,... | collective-permute-start | bytes 4718600 | tf_op jit(solution)/shard_map/ppermute | solution.py:543
  278.8 40.8 %collective-permute-start.33 = (bf16[1536,512]{1,0:T(8,128)(2,1)}, bf16[1536,512]{1,0:T(8,128)(2,1)}, u32[]{:S(2)}, u32[]{:S(2)}) collective-permute-start(bf16[1536,512]{1,0:T(8,128)(2,1)} %in_order.16.even.refs_3_), channel_id=1, source_target_pairs={{0,4},{1,5},{2,6},{3,7},{4,0},{5,1},{6,2},{7,3},{8,12},{9,13},{10,... | collective-permute-start | bytes 4718600 | tf_op jit(solution)/shard_map/ppermute | solution.py:543
  279.2 40.3 %collective-permute-start.34 = (bf16[384,512]{1,0:T(8,128)(2,1)S(1)}, bf16[384,512]{1,0:T(8,128)(2,1)S(1)}, u32[]{:S(2)}, u32[]{:S(2)}) collective-permute-start(bf16[384,512]{1,0:T(8,128)(2,1)S(1)} %copy-done.68), channel_id=1, source_target_pairs={{0,16},{1,17},{2,18},{3,19},{4,20},{5,21},{6,22},{7,23},{8,24},{9,... | collective-permute-start | bytes 1179656 | tf_op jit(solution)/shard_map/ppermute | solution.py:543
  282.9 36.7 %collective-permute-start.35 = (bf16[384,512]{1,0:T(8,128)(2,1)S(1)}, bf16[384,512]{1,0:T(8,128)(2,1)S(1)}, u32[]{:S(2)}, u32[]{:S(2)}) collective-permute-start(bf16[384,512]{1,0:T(8,128)(2,1)S(1)} %copy-done.90), channel_id=1, source_target_pairs={{0,24},{1,25},{2,26},{3,27},{4,28},{5,29},{6,30},{7,31},{8,16},{9,... | collective-permute-start | bytes 1179656 | tf_op jit(solution)/shard_map/ppermute | solution.py:543
  284.4 35.2 %collective-permute-start.36 = (bf16[384,512]{1,0:T(8,128)(2,1)S(1)}, bf16[384,512]{1,0:T(8,128)(2,1)S(1)}, u32[]{:S(2)}, u32[]{:S(2)}) collective-permute-start(bf16[384,512]{1,0:T(8,128)(2,1)S(1)} %copy-done.90), channel_id=1, source_target_pairs={{0,8},{1,9},{2,10},{3,11},{4,12},{5,13},{6,14},{7,15},{8,0},{9,1},... | collective-permute-start | bytes 1179656 | tf_op jit(solution)/shard_map/ppermute | solution.py:543
  319.6 214.6 %reduce-scatter.7.cloned.1.call-start = ((), (), s32[]{:S(2)}) async-start(), calls=%async_computation.8 | async-start | bytes 7077888 | tf_op jit(solution)/shard_map/reduce_scatter | solution.py:721
  321.8 43.6 %collective-permute-start.37 = (bf16[1536,512]{1,0:T(8,128)(2,1)}, bf16[1536,512]{1,0:T(8,128)(2,1)S(1)}, u32[]{:S(2)}, u32[]{:S(2)}) collective-permute-start(bf16[1536,512]{1,0:T(8,128)(2,1)} %in_order.17.even.refs_5_), channel_id=1, source_target_pairs={{0,4},{1,5},{2,6},{3,7},{4,0},{5,1},{6,2},{7,3},{8,12},{9,13},{10,... | collective-permute-start | bytes 4718600 | tf_op jit(solution)/shard_map/ppermute | solution.py:543
  324.6 40.8 %collective-permute-start.40 = (bf16[384,512]{1,0:T(8,128)(2,1)S(1)}, bf16[384,512]{1,0:T(8,128)(2,1)S(1)}, u32[]{:S(2)}, u32[]{:S(2)}) collective-permute-start(bf16[384,512]{1,0:T(8,128)(2,1)S(1)} %copy-done.88), channel_id=1, source_target_pairs={{0,8},{1,9},{2,10},{3,11},{4,12},{5,13},{6,14},{7,15},{8,0},{9,1},... | collective-permute-start | bytes 1179656 | tf_op jit(solution)/shard_map/ppermute | solution.py:543
  397.2 47.4 %collective-permute-start.45 = (bf16[1536,512]{1,0:T(8,128)(2,1)}, bf16[1536,512]{1,0:T(8,128)(2,1)}, u32[]{:S(2)}, u32[]{:S(2)}) collective-permute-start(bf16[1536,512]{1,0:T(8,128)(2,1)} %in_order.19.even.refs_1_), channel_id=1, source_target_pairs={{0,4},{1,5},{2,6},{3,7},{4,0},{5,1},{6,2},{7,3},{8,12},{9,13},{10,... | collective-permute-start | bytes 4718600 | tf_op jit(solution)/shard_map/ppermute | solution.py:543
  409.7 53.2 %collective-permute-start.46 = (bf16[1536,512]{1,0:T(8,128)(2,1)}, bf16[1536,512]{1,0:T(8,128)(2,1)}, u32[]{:S(2)}, u32[]{:S(2)}) collective-permute-start(bf16[1536,512]{1,0:T(8,128)(2,1)} %weight_part.20), channel_id=1, source_target_pairs={{0,4},{1,5},{2,6},{3,7},{4,0},{5,1},{6,2},{7,3},{8,12},{9,13},{10,... | collective-permute-start | bytes 4718600 | tf_op jit(solution)/shard_map/ppermute | solution.py:543
  462.9 170.5 %all-gather.11.cloned.1.call-start = ((), (), s32[]{:S(2)}) async-start(), calls=%async_computation.10 | async-start | bytes 7864320 | tf_op jit(solution)/shard_map/all_gather | solution.py:709
  501.8 37.7 %collective-permute-start.48 = (bf16[1536,512]{1,0:T(8,128)(2,1)}, bf16[1536,512]{1,0:T(8,128)(2,1)}, u32[]{:S(2)}, u32[]{:S(2)}) collective-permute-start(bf16[1536,512]{1,0:T(8,128)(2,1)} %weight_part.24), channel_id=1, source_target_pairs={{0,4},{1,5},{2,6},{3,7},{4,0},{5,1},{6,2},{7,3},{8,12},{9,13},{10,... | collective-permute-start | bytes 4718600 | tf_op jit(solution)/shard_map/ppermute | solution.py:543
  503.5 36.0 %collective-permute-start.49 = (bf16[384,512]{1,0:T(8,128)(2,1)}, bf16[384,512]{1,0:T(8,128)(2,1)}, u32[]{:S(2)}, u32[]{:S(2)}) collective-permute-start(bf16[384,512]{1,0:T(8,128)(2,1)} %get-tuple-element.888), channel_id=1, source_target_pairs={{0,16},{1,17},{2,18},{3,19},{4,20},{5,21},{6,22},{7,23},{8,24},{9,... | collective-permute-start | bytes 1179656 | tf_op jit(solution)/shard_map/ppermute | solution.py:543
  504.3 35.3 %collective-permute-start.50 = (bf16[384,512]{1,0:T(8,128)(2,1)}, bf16[384,512]{1,0:T(8,128)(2,1)}, u32[]{:S(2)}, u32[]{:S(2)}) collective-permute-start(bf16[384,512]{1,0:T(8,128)(2,1)} %get-tuple-element.889), channel_id=1, source_target_pairs={{0,24},{1,25},{2,26},{3,27},{4,28},{5,29},{6,30},{7,31},{8,16},{9,... | collective-permute-start | bytes 1179656 | tf_op jit(solution)/shard_map/ppermute | solution.py:543
  540.0 41.2 %collective-permute-start.52 = (bf16[128,3072]{1,0:T(8,128)(2,1)S(1)}, bf16[128,3072]{1,0:T(8,128)(2,1)S(1)}, u32[]{:S(2)}, u32[]{:S(2)}) collective-permute-start(bf16[128,3072]{1,0:T(8,128)(2,1)S(1)} %get-tuple-element.919.a), channel_id=1, source_target_pairs={{0,8},{1,9},{2,10},{3,11},{4,12},{5,13},{6,14},{7,15},{8,0},{9,1},... | collective-permute-start | bytes 2359304 | tf_op jit(solution)/shard_map/ppermute | solution.py:543
  543.0 35.2 %collective-permute-start.54 = (bf16[384,512]{1,0:T(8,128)(2,1)S(1)}, bf16[384,512]{1,0:T(8,128)(2,1)S(1)}, u32[]{:S(2)}, u32[]{:S(2)}) collective-permute-start(bf16[384,512]{1,0:T(8,128)(2,1)S(1)} %copy-done.97), channel_id=1, source_target_pairs={{0,24},{1,25},{2,26},{3,27},{4,28},{5,29},{6,30},{7,31},{8,16},{9,... | collective-permute-start | bytes 1179656 | tf_op jit(solution)/shard_map/ppermute | solution.py:543
  544.4 36.8 %collective-permute-start.55 = (bf16[384,512]{1,0:T(8,128)(2,1)S(1)}, bf16[384,512]{1,0:T(8,128)(2,1)S(1)}, u32[]{:S(2)}, u32[]{:S(2)}) collective-permute-start(bf16[384,512]{1,0:T(8,128)(2,1)S(1)} %copy-done.94), channel_id=1, source_target_pairs={{0,8},{1,9},{2,10},{3,11},{4,12},{5,13},{6,14},{7,15},{8,0},{9,1},... | collective-permute-start | bytes 1179656 | tf_op jit(solution)/shard_map/ppermute | solution.py:543
  583.1 174.0 %reduce-scatter.9.cloned.1.call-start = ((), (), s32[]{:S(2)}) async-start(), calls=%async_computation.9 | async-start | bytes 7077888 | tf_op jit(solution)/shard_map/reduce_scatter | solution.py:721
  583.2 34.5 %collective-permute-start.60 = (bf16[1536,512]{1,0:T(8,128)(2,1)}, bf16[1536,512]{1,0:T(8,128)(2,1)}, u32[]{:S(2)}, u32[]{:S(2)}) collective-permute-start(bf16[1536,512]{1,0:T(8,128)(2,1)} %weight_part.28), channel_id=1, source_target_pairs={{0,4},{1,5},{2,6},{3,7},{4,0},{5,1},{6,2},{7,3},{8,12},{9,13},{10,... | collective-permute-start | bytes 4718600 | tf_op jit(solution)/shard_map/ppermute | solution.py:543
  617.7 200.5 %reduce-scatter.11.cloned.1.call-start = ((), (), s32[]{:S(2)}) async-start(), calls=%async_computation.11 | async-start | bytes 7077888 | tf_op jit(solution)/shard_map/reduce_scatter | solution.py:721
  617.7 45.1 %collective-permute-start.64 = (bf16[1536,512]{1,0:T(8,128)(2,1)}, bf16[1536,512]{1,0:T(8,128)(2,1)}, u32[]{:S(2)}, u32[]{:S(2)}) collective-permute-start(bf16[1536,512]{1,0:T(8,128)(2,1)} %weight_part.30), channel_id=1, source_target_pairs={{0,4},{1,5},{2,6},{3,7},{4,0},{5,1},{6,2},{7,3},{8,12},{9,13},{10,... | collective-permute-start | bytes 4718600 | tf_op jit(solution)/shard_map/ppermute | solution.py:543
  618.8 44.1 %collective-permute-start.61 = (bf16[384,512]{1,0:T(8,128)(2,1)}, bf16[384,512]{1,0:T(8,128)(2,1)}, u32[]{:S(2)}, u32[]{:S(2)}) collective-permute-start(bf16[384,512]{1,0:T(8,128)(2,1)} %get-tuple-element.976), channel_id=1, source_target_pairs={{0,16},{1,17},{2,18},{3,19},{4,20},{5,21},{6,22},{7,23},{8,24},{9,... | collective-permute-start | bytes 1179656 | tf_op jit(solution)/shard_map/ppermute | solution.py:543
  620.5 42.4 %collective-permute-start.62 = (bf16[384,512]{1,0:T(8,128)(2,1)}, bf16[384,512]{1,0:T(8,128)(2,1)}, u32[]{:S(2)}, u32[]{:S(2)}) collective-permute-start(bf16[384,512]{1,0:T(8,128)(2,1)} %get-tuple-element.977), channel_id=1, source_target_pairs={{0,24},{1,25},{2,26},{3,27},{4,28},{5,29},{6,30},{7,31},{8,16},{9,... | collective-permute-start | bytes 1179656 | tf_op jit(solution)/shard_map/ppermute | solution.py:543
  622.8 40.1 %collective-permute-start.63 = (bf16[384,512]{1,0:T(8,128)(2,1)}, bf16[384,512]{1,0:T(8,128)(2,1)}, u32[]{:S(2)}, u32[]{:S(2)}) collective-permute-start(bf16[384,512]{1,0:T(8,128)(2,1)} %get-tuple-element.978), channel_id=1, source_target_pairs={{0,8},{1,9},{2,10},{3,11},{4,12},{5,13},{6,14},{7,15},{8,0},{9,1},... | collective-permute-start | bytes 1179656 | tf_op jit(solution)/shard_map/ppermute | solution.py:543
  763.4 39.2 %collective-permute-start.84 = (bf16[1536,384]{1,0:T(8,128)(2,1)S(1)}, bf16[1536,384]{1,0:T(8,128)(2,1)S(1)}, u32[]{:S(2)}, u32[]{:S(2)}) collective-permute-start(bf16[1536,384]{1,0:T(8,128)(2,1)S(1)} %weight_part.38), channel_id=1, source_target_pairs={{0,4},{1,5},{2,6},{3,7},{4,0},{5,1},{6,2},{7,3},{8,12},{9,13},{10,... | collective-permute-start | bytes 3538952 | tf_op jit(solution)/shard_map/ppermute | solution.py:543
  (188 other events, 2699.8 us)
Sparse Core Ops, SparseCore 0:
  38.6 69.7 all-gather.4
  110.5 45.7 all-gather.6
  201.9 113.4 reduce-scatter.4
  319.7 75.6 all-gather.8
  463.0 37.8 reduce-scatter.6
  583.2 44.6 all-gather.10
  630.9 75.0 reduce-scatter.8
  708.2 89.5 reduce-scatter.10

commit v5 on v4

--- a/solution.py
+++ b/solution.py
@@ -874,7 +874,6 @@
     grads[1].add()
     grads[2].even()
     grads[3].odd()
-    mlp_part = chain.step(lambda y, p: back(y, p, bf16), acts, [d0.pair, d1.pair])
     part_gain_mlp, grad_middle, v = chain.step(
         rows.close_second, sum_second.wait(), gains, middle, scale_second, grad_rows
     )
@@ -886,6 +885,7 @@
     grads[2].add()
     grads[3].even()
     grads[4].odd()
+    mlp_part = chain.step(lambda y, p: back(y, p, bf16), acts, [d0.pair, d1.pair])
     grads[3].wait1()
     grads[1].wait2()
     rows_m.wait1()
@@ -895,13 +895,13 @@
     grads[3].add()
     grads[4].even()
     grads[5].odd()
+    grads[5].even()
     grads[4].wait1()
     grads[2].wait2()
     grads[5].start1()
     grads[3].start2()
     mlp = RowSum(wires, chain, mlp_part)
     grads[4].add()
-    grads[5].even()
     middle_half = rows_m.wait()
     grads.append(Grad(wires, chain, sides, middle_half, attn_flat))
     grads[6].odd()

time: 867 us -> 869 us (level)
    unnamed x244 -> x224, local copies, waits for them, and re-layouts: 30.4 us -> 29.5 us
  transfers between devices with their start and end apart: 100 -> 100, of which waited for: 37 -> 35; matrix products, arithmetic and copies ran while one was open for 0% -> 0% of each run, Pallas kernels for 43% -> 43%
where the time goes in v5:
time: 869 us; the launch traced here: 861 us
  Pallas kernels  380 us (44%)
  waiting for transfers between devices  294 us (34%)
  starting transfers between devices  134 us (15%)
  local copies, waits for them, and re-layouts  32.1 us (4%)
  between operations  17.2 us (2%)
    pallas_call x87, Pallas kernels, run(): pl.pallas_call(kernel, out_shape=[jax.ShapeDtypeStruct(s, t) for s, t in...  380 us
    ppermute x90, waiting for transfers between devices, over_dp(): return lax.ppermute(value, AXES, pairs)  269 us
    ppermute x90, starting transfers between devices, over_dp(): return lax.ppermute(value, AXES, pairs)  132 us
    unnamed x224, local copies, waits for them, and re-layouts  29.5 us
    reduce_scatter x4, waiting for transfers between devices, __init__(): lax.psum_scatter(*chain.pin(value), AXES, scatter_dimension=0, tiled=True...  22.7 us
  transfers between devices with their start and end apart: 100, of which 35 were waited for; matrix products, arithmetic and copies ran while one was open for 0% of the time, Pallas kernels for 43%

profile of v5, /device:TPU:0, one launch (start us, length us, event | category | flops | bytes accessed | tf_op | source)
XLA Modules:
  0.0 861.5 jit_solution(1950205564983797238)
XLA Ops:
  26.3 11.0 %collective-permute-done.5.b = bf16[128,3072]{1,0:T(8,128)(2,1)S(1)} collective-permute-done((bf16[128,3072]{1,0:T(8,128)(2,1)S(1)}, bf16[128,3072]{1,0:T(8,128)(2,1)S(1)}, u32[]{:S(2)}, u32[]{:S(2)}) %collective-permute-start.5) | collective-permute-done | bytes 786464 | tf_op jit(solution)/shard_map/ppermute | solution.py:543
  50.9 28.9 %collective-permute-done.6.refs_1_ = bf16[384,384]{1,0:T(8,128)(2,1)S(1)} collective-permute-done((bf16[384,384]{1,0:T(8,128)(2,1)S(1)}, bf16[384,384]{1,0:T(8,128)(2,1)S(1)}, u32[]{:S(2)}, u32[]{:S(2)}) %collective-permute-start.6) | collective-permute-done | bytes 294944 | tf_op jit(solution)/shard_map/ppermute | solution.py:543
  140.8 7.1 product.6.q_ref
  148.0 7.1 product.7.k_ref
  169.9 7.3 product.8.v_ref
  177.5 15.5 %attend.1 = (bf16[1024,384]{1,0:T(8,128)(2,1)}, bf16[1024,384]{1,0:T(8,128)(2,1)}, bf16[1024,384]{1,0:T(8,128)(2,1)}, bf16[1024,384]{1,0:T(8,128)(2,1)}, f32[1024,4]{1,0:T(8,128)S(1)}) custom-call(s32[2]{0:T(128)S(1)} %pad_add_fusion.1.len_ref, s32[1024,1]{1,0:T(8,128)S(1)} %copy.17.rows_ref, s32[1,1024]{1,0:T(1,128)S(1)} %bitcast.32, ...), custom_call_target="tpu_custom_call" | custom-call | flops 1 | bytes 1 | tf_op jit(solution)/shard_map/attend/pallas_call | solution.py:152
  195.0 7.9 back.5
  211.9 23.0 %collective-permute-done.25.refs_1_ = bf16[384,512]{1,0:T(8,128)(2,1)S(1)} collective-permute-done((bf16[384,512]{1,0:T(8,128)(2,1)S(1)}, bf16[384,512]{1,0:T(8,128)(2,1)S(1)}, u32[]{:S(2)}, u32[]{:S(2)}) %collective-permute-start.25) | collective-permute-done | bytes 393248 | tf_op jit(solution)/shard_map/ppermute | solution.py:543
  248.6 7.4 product.9.ga_ref
  256.0 17.3 %collective-permute-done.30.refs_1_ = bf16[384,512]{1,0:T(8,128)(2,1)S(1)} collective-permute-done((bf16[384,512]{1,0:T(8,128)(2,1)S(1)}, bf16[384,512]{1,0:T(8,128)(2,1)S(1)}, u32[]{:S(2)}, u32[]{:S(2)}) %collective-permute-start.30) | collective-permute-done | bytes 393248 | tf_op jit(solution)/shard_map/ppermute | solution.py:543
  286.9 7.3 product.10.ga_ref
  294.3 22.7 %reduce-scatter.5.cloned.1.call-done.got_ref = bf16[128,3072]{1,0:T(8,128)(2,1)} async-done(((bf16[1024,3072]{1,0:T(8,128)(2,1)}), bf16[128,3072]{1,0:T(8,128)(2,1)}) %reduce-scatter.5.cloned.1.call-update) | async-done | bytes 786448 | tf_op jit(solution)/shard_map/reduce_scatter | solution.py:721
  327.4 15.5 %collective-permute-done.38.refs_1_ = bf16[384,512]{1,0:T(8,128)(2,1)S(1)} collective-permute-done((bf16[384,512]{1,0:T(8,128)(2,1)S(1)}, bf16[384,512]{1,0:T(8,128)(2,1)S(1)}, u32[]{:S(2)}, u32[]{:S(2)}) %collective-permute-start.38) | collective-permute-done | bytes 393248 | tf_op jit(solution)/shard_map/ppermute | solution.py:543
  342.9 10.6 %collective-permute-done.39.refs_2_ = bf16[384,512]{1,0:T(8,128)(2,1)S(1)} collective-permute-done((bf16[384,512]{1,0:T(8,128)(2,1)S(1)}, bf16[384,512]{1,0:T(8,128)(2,1)S(1)}, u32[]{:S(2)}, u32[]{:S(2)}) %collective-permute-start.39) | collective-permute-done | bytes 393248 | tf_op jit(solution)/shard_map/ppermute | solution.py:543
  353.5 13.0 %collective-permute-done.40.refs_3_ = bf16[384,512]{1,0:T(8,128)(2,1)S(1)} collective-permute-done((bf16[384,512]{1,0:T(8,128)(2,1)S(1)}, bf16[384,512]{1,0:T(8,128)(2,1)S(1)}, u32[]{:S(2)}, u32[]{:S(2)}) %collective-permute-start.40) | collective-permute-done | bytes 393248 | tf_op jit(solution)/shard_map/ppermute | solution.py:543
  374.3 13.8 %collective-permute-done.41.refs_1_ = bf16[384,512]{1,0:T(8,128)(2,1)S(1)} collective-permute-done((bf16[384,512]{1,0:T(8,128)(2,1)S(1)}, bf16[384,512]{1,0:T(8,128)(2,1)S(1)}, u32[]{:S(2)}, u32[]{:S(2)}) %collective-permute-start.41) | collective-permute-done | bytes 393248 | tf_op jit(solution)/shard_map/ppermute | solution.py:543
  399.9 7.1 gated.4
  413.0 7.1 gated.5
  421.9 7.1 gated.6
  430.0 16.4 %back.6.refs_3_ = f32[1024,3072]{1,0:T(8,128)} custom-call(bf16[1024,512]{1,0:T(8,128)(2,1)S(1)} %get-tuple-element.839.y_ref.refs_0_, bf16[1024,512]{1,0:T(8,128)(2,1)} %copy-done.17, bf16[1024,512]{1,0:T(8,128)(2,1)} %copy-done.15, bf16[1536,512]{1,0:T(8,128)(2,1)} %in_order.16.even.refs_3_, bf16[1536,512]{1,0:T(8,128)(2,1)} %collective-permute-done.33.odd.refs_4_, ...), custom_call_target="tpu_custom_call" | custom-call | flops 1 | bytes 1 | tf_op jit(solution)/shard_map/back/pallas_call | solution.py:152
  446.4 7.1 gated.7
  453.5 11.1 %back.7 = bf16[1024,3072]{1,0:T(8,128)(2,1)} custom-call(bf16[1024,512]{1,0:T(8,128)(2,1)S(1)} %get-tuple-element.899.refs_0_.y_ref, bf16[1536,512]{1,0:T(8,128)(2,1)} %in_order.19.even.refs_1_, bf16[1536,512]{1,0:T(8,128)(2,1)} %collective-permute-done.45.odd.refs_2_, f32[1024,3072]{1,0:T(8,128)} %back.6.refs_3_), custom_call_target="tpu_custom_call" | custom-call | flops 1 | bytes 1 | tf_op jit(solution)/shard_map/back/pallas_call | solution.py:152
  490.6 14.3 %collective-permute-done.47.g0.g1 = bf16[1536,512]{1,0:T(8,128)(2,1)S(1)} collective-permute-done((bf16[1536,512]{1,0:T(8,128)(2,1)}, bf16[1536,512]{1,0:T(8,128)(2,1)S(1)}, u32[]{:S(2)}, u32[]{:S(2)}) %collective-permute-start.47) | collective-permute-done | bytes 1572896 | tf_op jit(solution)/shard_map/ppermute | solution.py:543
  529.3 10.0 %collective-permute-done.48.g0.g1 = bf16[1536,512]{1,0:T(8,128)(2,1)} collective-permute-done((bf16[1536,512]{1,0:T(8,128)(2,1)}, bf16[1536,512]{1,0:T(8,128)(2,1)}, u32[]{:S(2)}, u32[]{:S(2)}) %collective-permute-start.48) | collective-permute-done | bytes 1572896 | tf_op jit(solution)/shard_map/ppermute | solution.py:543
  559.7 12.8 %back.8 = bf16[1024,3072]{1,0:T(8,128)(2,1)} custom-call(bf16[1024,512]{1,0:T(8,128)(2,1)S(1)} %constant_dynamic-update-slice_fusion.5.y_ref.refs_0_, bf16[1024,512]{1,0:T(8,128)(2,1)} %copy-done.6, bf16[1536,512]{1,0:T(8,128)(2,1)} %in_order.14.even.refs_2_, bf16[1536,512]{1,0:T(8,128)(2,1)} %collective-permute-done.28.odd.refs_3_, ...), custom_call_target="tpu_custom_call" | custom-call | flops 1 | bytes 1 | tf_op jit(solution)/shard_map/back/pallas_call | solution.py:152
  609.6 11.4 %collective-permute-done.60.g0.g1 = bf16[1536,512]{1,0:T(8,128)(2,1)} collective-permute-done((bf16[1536,512]{1,0:T(8,128)(2,1)}, bf16[1536,512]{1,0:T(8,128)(2,1)}, u32[]{:S(2)}, u32[]{:S(2)}) %collective-permute-start.60) | collective-permute-done | bytes 1572896 | tf_op jit(solution)/shard_map/ppermute | solution.py:543
  644.8 17.7 %attend_back.1 = (bf16[1024,384]{1,0:T(8,128)(2,1)}, bf16[1024,384]{1,0:T(8,128)(2,1)}, bf16[1024,384]{1,0:T(8,128)(2,1)}) custom-call(s32[2]{0:T(128)S(1)} %pad_add_fusion.1.len_ref, s32[1024,1]{1,0:T(8,128)S(1)} %copy.18.rows_ref, s32[1,1024]{1,0:T(1,128)S(1)} %bitcast.34, f32[1024,96]{1,0:T(8,128)S(1)} %copy-done.26, f32[1024,96]{1,0:T(8,128)S(1)} %copy-done.27, ...), custom_call_target="tpu_custom_call" | custom-call | flops 1 | bytes 1 | tf_op jit(solution)/shard_map/attend_back/pallas_call | solution.py:152
  678.3 17.4 %back.9 = (bf16[1024,3072]{1,0:T(8,128)(2,1)}, f32[1,3072]{1,0:T(1,128)S(1)}) custom-call(bf16[1024,384]{1,0:T(8,128)(2,1)S(1)} %copy-done.24, bf16[1024,384]{1,0:T(8,128)(2,1)S(1)} %copy-done.23, bf16[1024,384]{1,0:T(8,128)(2,1)} %get-tuple-element.1058.refs_2_.y_ref, bf16[1536,384]{1,0:T(8,128)(2,1)} %in_order.10.even.refs_3_, ...), custom_call_target="tpu_custom_call" | custom-call | flops 1 | bytes 1 | tf_op jit(solution)/shard_map/back/pallas_call | solution.py:152
  731.3 7.0 collective-permute-start.76
  778.1 7.2 laid_out.4
  785.3 7.6 collective-permute-done.74
  830.4 19.6 %collective-permute-done.89.refs_9_ = bf16[384,384]{1,0:T(8,128)(2,1)S(1)} collective-permute-done((bf16[384,384]{1,0:T(8,128)(2,1)S(1)}, bf16[384,384]{1,0:T(8,128)(2,1)S(1)}, u32[]{:S(2)}, u32[]{:S(2)}) %collective-permute-start.89) | collective-permute-done | bytes 294944 | tf_op jit(solution)/shard_map/ppermute | solution.py:543
  (517 shorter events, 447.6 us)
Async XLA Ops:
  7.2 133.6 %all-gather.5.cloned.1.call-start = ((), (), s32[]{:S(2)}) async-start(), calls=%async_computation.4 | async-start | bytes 7077888 | tf_op jit(solution)/shard_map/all_gather | solution.py:692
  38.5 173.4 %all-gather.7.cloned.1.call-start = ((), (), s32[]{:S(2)}) async-start(), calls=%async_computation.6 | async-start | bytes 7864320 | tf_op jit(solution)/shard_map/all_gather | solution.py:709
  42.1 37.7 %collective-permute-start.7 = (bf16[384,384]{1,0:T(8,128)(2,1)S(1)}, bf16[384,384]{1,0:T(8,128)(2,1)S(1)}, u32[]{:S(2)}, u32[]{:S(2)}) collective-permute-start(bf16[384,384]{1,0:T(8,128)(2,1)S(1)} %get-tuple-element.616), channel_id=1, source_target_pairs={{0,24},{1,25},{2,26},{3,27},{4,28},{5,29},{6,30},{7,31},{8,16},{9,... | collective-permute-start | bytes 884744 | tf_op jit(solution)/shard_map/ppermute | solution.py:543
  45.0 34.8 %collective-permute-start.8 = (bf16[384,384]{1,0:T(8,128)(2,1)S(1)}, bf16[384,384]{1,0:T(8,128)(2,1)S(1)}, u32[]{:S(2)}, u32[]{:S(2)}) collective-permute-start(bf16[384,384]{1,0:T(8,128)(2,1)S(1)} %get-tuple-element.616), channel_id=1, source_target_pairs={{0,8},{1,9},{2,10},{3,11},{4,12},{5,13},{6,14},{7,15},{8,0},{9,1},... | collective-permute-start | bytes 884744 | tf_op jit(solution)/shard_map/ppermute | solution.py:543
  79.9 237.1 %reduce-scatter.5.cloned.1.call-start = ((), (), s32[]{:S(2)}) async-start(), calls=%async_computation.5 | async-start | bytes 7077888 | tf_op jit(solution)/shard_map/reduce_scatter | solution.py:721
  162.7 40.1 %collective-permute-start.22 = (bf16[384,512]{1,0:T(8,128)(2,1)}, bf16[384,512]{1,0:T(8,128)(2,1)}, u32[]{:S(2)}, u32[]{:S(2)}) collective-permute-start(bf16[384,512]{1,0:T(8,128)(2,1)} %get-tuple-element.713.refs_0_), channel_id=1, source_target_pairs={{0,16},{1,17},{2,18},{3,19},{4,20},{5,21},{6,22},{7,23},{8,24},{9,... | collective-permute-start | bytes 1179656 | tf_op jit(solution)/shard_map/ppermute | solution.py:543
  202.9 197.0 %all-gather.9.cloned.1.call-start = ((), (), s32[]{:S(2)}) async-start(), calls=%async_computation.7 | async-start | bytes 7077888 | tf_op jit(solution)/shard_map/all_gather | solution.py:692
  206.1 35.4 %collective-permute-start.28 = (bf16[1536,512]{1,0:T(8,128)(2,1)}, bf16[1536,512]{1,0:T(8,128)(2,1)}, u32[]{:S(2)}, u32[]{:S(2)}) collective-permute-start(bf16[1536,512]{1,0:T(8,128)(2,1)} %in_order.14.even.refs_2_), channel_id=1, source_target_pairs={{0,4},{1,5},{2,6},{3,7},{4,0},{5,1},{6,2},{7,3},{8,12},{9,13},{10,... | collective-permute-start | bytes 4718600 | tf_op jit(solution)/shard_map/ppermute | solution.py:543
  243.3 35.8 %collective-permute-start.29 = (bf16[1536,512]{1,0:T(8,128)(2,1)}, bf16[1536,512]{1,0:T(8,128)(2,1)S(1)}, u32[]{:S(2)}, u32[]{:S(2)}) collective-permute-start(bf16[1536,512]{1,0:T(8,128)(2,1)} %in_order.15.even.refs_4_), channel_id=1, source_target_pairs={{0,4},{1,5},{2,6},{3,7},{4,0},{5,1},{6,2},{7,3},{8,12},{9,13},{10,... | collective-permute-start | bytes 4718600 | tf_op jit(solution)/shard_map/ppermute | solution.py:543
  280.8 40.4 %collective-permute-start.33 = (bf16[1536,512]{1,0:T(8,128)(2,1)}, bf16[1536,512]{1,0:T(8,128)(2,1)}, u32[]{:S(2)}, u32[]{:S(2)}) collective-permute-start(bf16[1536,512]{1,0:T(8,128)(2,1)} %in_order.16.even.refs_3_), channel_id=1, source_target_pairs={{0,4},{1,5},{2,6},{3,7},{4,0},{5,1},{6,2},{7,3},{8,12},{9,13},{10,... | collective-permute-start | bytes 4718600 | tf_op jit(solution)/shard_map/ppermute | solution.py:543
  281.8 39.4 %collective-permute-start.34 = (bf16[384,512]{1,0:T(8,128)(2,1)S(1)}, bf16[384,512]{1,0:T(8,128)(2,1)S(1)}, u32[]{:S(2)}, u32[]{:S(2)}) collective-permute-start(bf16[384,512]{1,0:T(8,128)(2,1)S(1)} %copy-done.65), channel_id=1, source_target_pairs={{0,16},{1,17},{2,18},{3,19},{4,20},{5,21},{6,22},{7,23},{8,24},{9,... | collective-permute-start | bytes 1179656 | tf_op jit(solution)/shard_map/ppermute | solution.py:543
  284.7 36.5 %collective-permute-start.35 = (bf16[384,512]{1,0:T(8,128)(2,1)S(1)}, bf16[384,512]{1,0:T(8,128)(2,1)S(1)}, u32[]{:S(2)}, u32[]{:S(2)}) collective-permute-start(bf16[384,512]{1,0:T(8,128)(2,1)S(1)} %copy-done.87), channel_id=1, source_target_pairs={{0,24},{1,25},{2,26},{3,27},{4,28},{5,29},{6,30},{7,31},{8,16},{9,... | collective-permute-start | bytes 1179656 | tf_op jit(solution)/shard_map/ppermute | solution.py:543
  321.3 202.5 %reduce-scatter.7.cloned.1.call-start = ((), (), s32[]{:S(2)}) async-start(), calls=%async_computation.8 | async-start | bytes 7077888 | tf_op jit(solution)/shard_map/reduce_scatter | solution.py:721
  323.4 43.0 %collective-permute-start.37 = (bf16[1536,512]{1,0:T(8,128)(2,1)}, bf16[1536,512]{1,0:T(8,128)(2,1)S(1)}, u32[]{:S(2)}, u32[]{:S(2)}) collective-permute-start(bf16[1536,512]{1,0:T(8,128)(2,1)} %in_order.17.even.refs_5_), channel_id=1, source_target_pairs={{0,4},{1,5},{2,6},{3,7},{4,0},{5,1},{6,2},{7,3},{8,12},{9,13},{10,... | collective-permute-start | bytes 4718600 | tf_op jit(solution)/shard_map/ppermute | solution.py:543
  326.1 40.3 %collective-permute-start.40 = (bf16[384,512]{1,0:T(8,128)(2,1)S(1)}, bf16[384,512]{1,0:T(8,128)(2,1)S(1)}, u32[]{:S(2)}, u32[]{:S(2)}) collective-permute-start(bf16[384,512]{1,0:T(8,128)(2,1)S(1)} %copy-done.85), channel_id=1, source_target_pairs={{0,8},{1,9},{2,10},{3,11},{4,12},{5,13},{6,14},{7,15},{8,0},{9,1},... | collective-permute-start | bytes 1179656 | tf_op jit(solution)/shard_map/ppermute | solution.py:543
  398.8 47.6 %collective-permute-start.45 = (bf16[1536,512]{1,0:T(8,128)(2,1)}, bf16[1536,512]{1,0:T(8,128)(2,1)}, u32[]{:S(2)}, u32[]{:S(2)}) collective-permute-start(bf16[1536,512]{1,0:T(8,128)(2,1)} %in_order.19.even.refs_1_), channel_id=1, source_target_pairs={{0,4},{1,5},{2,6},{3,7},{4,0},{5,1},{6,2},{7,3},{8,12},{9,13},{10,... | collective-permute-start | bytes 4718600 | tf_op jit(solution)/shard_map/ppermute | solution.py:543
  412.0 52.6 %collective-permute-start.46 = (bf16[1536,512]{1,0:T(8,128)(2,1)}, bf16[1536,512]{1,0:T(8,128)(2,1)}, u32[]{:S(2)}, u32[]{:S(2)}) collective-permute-start(bf16[1536,512]{1,0:T(8,128)(2,1)} %weight_part.20), channel_id=1, source_target_pairs={{0,4},{1,5},{2,6},{3,7},{4,0},{5,1},{6,2},{7,3},{8,12},{9,13},{10,... | collective-permute-start | bytes 4718600 | tf_op jit(solution)/shard_map/ppermute | solution.py:543
  464.7 168.4 %all-gather.11.cloned.1.call-start = ((), (), s32[]{:S(2)}) async-start(), calls=%async_computation.10 | async-start | bytes 7864320 | tf_op jit(solution)/shard_map/all_gather | solution.py:709
  470.4 34.5 %collective-permute-start.47 = (bf16[1536,512]{1,0:T(8,128)(2,1)}, bf16[1536,512]{1,0:T(8,128)(2,1)S(1)}, u32[]{:S(2)}, u32[]{:S(2)}) collective-permute-start(bf16[1536,512]{1,0:T(8,128)(2,1)} %weight_part.21), channel_id=1, source_target_pairs={{0,4},{1,5},{2,6},{3,7},{4,0},{5,1},{6,2},{7,3},{8,12},{9,13},{10,... | collective-permute-start | bytes 4718600 | tf_op jit(solution)/shard_map/ppermute | solution.py:543
  504.9 34.5 %collective-permute-start.48 = (bf16[1536,512]{1,0:T(8,128)(2,1)}, bf16[1536,512]{1,0:T(8,128)(2,1)}, u32[]{:S(2)}, u32[]{:S(2)}) collective-permute-start(bf16[1536,512]{1,0:T(8,128)(2,1)} %weight_part.24), channel_id=1, source_target_pairs={{0,4},{1,5},{2,6},{3,7},{4,0},{5,1},{6,2},{7,3},{8,12},{9,13},{10,... | collective-permute-start | bytes 4718600 | tf_op jit(solution)/shard_map/ppermute | solution.py:543
  540.5 43.0 %collective-permute-start.52 = (bf16[128,3072]{1,0:T(8,128)(2,1)}, bf16[128,3072]{1,0:T(8,128)(2,1)}, u32[]{:S(2)}, u32[]{:S(2)}) collective-permute-start(bf16[128,3072]{1,0:T(8,128)(2,1)} %get-tuple-element.919.a), channel_id=1, source_target_pairs={{0,8},{1,9},{2,10},{3,11},{4,12},{5,13},{6,14},{7,15},{8,0},{9,1},... | collective-permute-start | bytes 2359304 | tf_op jit(solution)/shard_map/ppermute | solution.py:543
  542.3 35.7 %collective-permute-start.54 = (bf16[384,512]{1,0:T(8,128)(2,1)}, bf16[384,512]{1,0:T(8,128)(2,1)}, u32[]{:S(2)}, u32[]{:S(2)}) collective-permute-start(bf16[384,512]{1,0:T(8,128)(2,1)} %get-tuple-element.910), channel_id=1, source_target_pairs={{0,24},{1,25},{2,26},{3,27},{4,28},{5,29},{6,30},{7,31},{8,16},{9,... | collective-permute-start | bytes 1179656 | tf_op jit(solution)/shard_map/ppermute | solution.py:543
  544.9 38.6 %collective-permute-start.55 = (bf16[384,512]{1,0:T(8,128)(2,1)}, bf16[384,512]{1,0:T(8,128)(2,1)}, u32[]{:S(2)}, u32[]{:S(2)}) collective-permute-start(bf16[384,512]{1,0:T(8,128)(2,1)} %get-tuple-element.911), channel_id=1, source_target_pairs={{0,8},{1,9},{2,10},{3,11},{4,12},{5,13},{6,14},{7,15},{8,0},{9,1},... | collective-permute-start | bytes 1179656 | tf_op jit(solution)/shard_map/ppermute | solution.py:543
  586.1 171.6 %reduce-scatter.9.cloned.1.call-start = ((), (), s32[]{:S(2)}) async-start(), calls=%async_computation.9 | async-start | bytes 7077888 | tf_op jit(solution)/shard_map/reduce_scatter | solution.py:721
  586.2 34.8 %collective-permute-start.60 = (bf16[1536,512]{1,0:T(8,128)(2,1)}, bf16[1536,512]{1,0:T(8,128)(2,1)}, u32[]{:S(2)}, u32[]{:S(2)}) collective-permute-start(bf16[1536,512]{1,0:T(8,128)(2,1)} %weight_part.28), channel_id=1, source_target_pairs={{0,4},{1,5},{2,6},{3,7},{4,0},{5,1},{6,2},{7,3},{8,12},{9,13},{10,... | collective-permute-start | bytes 4718600 | tf_op jit(solution)/shard_map/ppermute | solution.py:543
  586.5 34.5 %collective-permute-start.57 = (bf16[384,512]{1,0:T(8,128)(2,1)}, bf16[384,512]{1,0:T(8,128)(2,1)}, u32[]{:S(2)}, u32[]{:S(2)}) collective-permute-start(bf16[384,512]{1,0:T(8,128)(2,1)} %get-tuple-element.921), channel_id=1, source_target_pairs={{0,16},{1,17},{2,18},{3,19},{4,20},{5,21},{6,22},{7,23},{8,24},{9,... | collective-permute-start | bytes 1179656 | tf_op jit(solution)/shard_map/ppermute | solution.py:543
  621.0 200.7 %reduce-scatter.11.cloned.1.call-start = ((), (), s32[]{:S(2)}) async-start(), calls=%async_computation.11 | async-start | bytes 7077888 | tf_op jit(solution)/shard_map/reduce_scatter | solution.py:721
  621.1 41.4 %collective-permute-start.64 = (bf16[1536,512]{1,0:T(8,128)(2,1)}, bf16[1536,512]{1,0:T(8,128)(2,1)}, u32[]{:S(2)}, u32[]{:S(2)}) collective-permute-start(bf16[1536,512]{1,0:T(8,128)(2,1)} %weight_part.30), channel_id=1, source_target_pairs={{0,4},{1,5},{2,6},{3,7},{4,0},{5,1},{6,2},{7,3},{8,12},{9,13},{10,... | collective-permute-start | bytes 4718600 | tf_op jit(solution)/shard_map/ppermute | solution.py:543
  621.4 41.0 %collective-permute-start.61 = (bf16[384,512]{1,0:T(8,128)(2,1)S(1)}, bf16[384,512]{1,0:T(8,128)(2,1)}, u32[]{:S(2)}, u32[]{:S(2)}) collective-permute-start(bf16[384,512]{1,0:T(8,128)(2,1)S(1)} %get-tuple-element.976), channel_id=1, source_target_pairs={{0,16},{1,17},{2,18},{3,19},{4,20},{5,21},{6,22},{7,23},{8,24},{9,... | collective-permute-start | bytes 1179656 | tf_op jit(solution)/shard_map/ppermute | solution.py:543
  625.1 37.3 %collective-permute-start.62 = (bf16[384,512]{1,0:T(8,128)(2,1)S(1)}, bf16[384,512]{1,0:T(8,128)(2,1)}, u32[]{:S(2)}, u32[]{:S(2)}) collective-permute-start(bf16[384,512]{1,0:T(8,128)(2,1)S(1)} %get-tuple-element.977), channel_id=1, source_target_pairs={{0,24},{1,25},{2,26},{3,27},{4,28},{5,29},{6,30},{7,31},{8,16},{9,... | collective-permute-start | bytes 1179656 | tf_op jit(solution)/shard_map/ppermute | solution.py:543
  627.1 35.4 %collective-permute-start.63 = (bf16[384,512]{1,0:T(8,128)(2,1)S(1)}, bf16[384,512]{1,0:T(8,128)(2,1)}, u32[]{:S(2)}, u32[]{:S(2)}) collective-permute-start(bf16[384,512]{1,0:T(8,128)(2,1)S(1)} %get-tuple-element.978), channel_id=1, source_target_pairs={{0,8},{1,9},{2,10},{3,11},{4,12},{5,13},{6,14},{7,15},{8,0},{9,1},... | collective-permute-start | bytes 1179656 | tf_op jit(solution)/shard_map/ppermute | solution.py:543
  763.5 39.2 %collective-permute-start.84 = (bf16[1536,384]{1,0:T(8,128)(2,1)S(1)}, bf16[1536,384]{1,0:T(8,128)(2,1)S(1)}, u32[]{:S(2)}, u32[]{:S(2)}) collective-permute-start(bf16[1536,384]{1,0:T(8,128)(2,1)S(1)} %weight_part.38), channel_id=1, source_target_pairs={{0,4},{1,5},{2,6},{3,7},{4,0},{5,1},{6,2},{7,3},{8,12},{9,13},{10,... | collective-permute-start | bytes 3538952 | tf_op jit(solution)/shard_map/ppermute | solution.py:543
  (178 other events, 2657.4 us)
Sparse Core Ops, SparseCore 0:
  38.6 70.2 all-gather.4
  111.0 45.7 all-gather.6
  203.0 113.9 reduce-scatter.4
  321.4 75.9 all-gather.8
  464.8 38.4 reduce-scatter.6
  586.2 44.5 all-gather.10
  633.7 78.7 reduce-scatter.8
  714.8 92.4 reduce-scatter.10
